TPU v7x, 256 devices: a whole 4x4x8 slice. The times are simulated.
256 devices in a mesh: freq: 4 (over z_lo), space: 64 (over x, z_hi, y, core).
Axes of the slice: x: 4, y: 4, z: 8 (z_hi: 2, z_lo: 4; z = z_hi * 4 + z_lo), core: 2. Of those that a mesh axis runs over, the one named last changes fastest.
Arguments:
- wavefields: float32 [2, 4, 2, 2048, 2048], P(None, 'freq', None, 'space'), may hold values from -6 to 6
- frequencies: float32 [4], P('freq'), may hold values from 1.5 to 4
- velocity: float32 [16, 2048, 2048], P('freq', 'space'), may hold values from 1 to 2
- slab_owner: int32 [1], replicated, may hold values from 0 to 15
- ref_velocity: float32 [1, 2], replicated, may hold values from 1 to 2
- ref_index: int32 [1, 128], replicated, may hold values from 0 to 1
Outputs:
- extrapolated: float32 [2, 4, 2, 2048, 2048], P(None, 'freq', None, 'space')
- image: float32 [1, 2048, 2048], P(None, 'space')
All inputs are finite; a program needn't handle non-finite values.
Results may differ from a plain program's by a relative error of at most 0.0003.
Values sent between devices are 32-bit elements; how exact they have to be, the bound alone decides.
No kernel may reach another device: no remote copies, remote signals or barrier semaphores. Data moves between devices by JAX's collectives and lax.ppermute only.
A program may use at most 64 MiB of HBM per device.

v0:
```python
import functools
import math

import jax
import jax.numpy as jnp
import numpy as np
from jax import lax
from jax.experimental import pallas as pl
from jax.experimental.pallas import tpu as pltpu
from jax.sharding import PartitionSpec as P

DZ = 4
INTERPRET = False
VMEM_BYTES = 20 * 2**20
BF16 = jnp.bfloat16

NY_A, NY_B = 16, 128
NX_S, NX_R = 64, 32
NY, NX = NY_A * NY_B, NX_S * NX_R


def split_bf16(matrix):
    high = np.asarray(matrix, np.float32).astype(BF16)
    low = (np.asarray(matrix, np.float64) - high.astype(np.float64)).astype(np.float32).astype(BF16)
    return high, low


@functools.cache
def constants():
    k2 = np.arange(NY_B)
    b = np.arange(NY_B)
    angle = 2.0 * np.pi * (np.outer(k2, b) % NY_B) / NY_B
    cosine, sine = np.cos(angle), np.sin(angle)
    forward = np.stack(
        [np.concatenate([cosine, sine], 1), np.concatenate([-sine, cosine], 1)], 0
    )
    forward = forward.reshape(2, 8, 16, 256).transpose(1, 0, 2, 3).reshape(256, 256)
    inverse = forward.copy() / NY
    fh, fl = split_bf16(forward)
    y_forward = np.concatenate([fh, fl, fh], 1)
    ih, il = split_bf16(inverse)
    y_inverse = np.concatenate([ih, il, ih], 0)
    r = np.arange(NX_R)
    angle = 2.0 * np.pi * (np.outer(r, r) % NX_R) / NX_R
    cosine = np.kron(np.eye(4), np.cos(angle))
    sine = np.kron(np.eye(4), np.sin(angle))
    x_forward = np.block([[cosine, -sine], [sine, cosine]])
    x_inverse = np.block([[cosine, sine], [-sine, cosine]]) / NX
    xh, xl = split_bf16(x_forward)
    x_forward = np.concatenate([xh, xl, xh], 0)
    xh, xl = split_bf16(x_inverse)
    x_inverse = np.concatenate([xh, xl, xh], 0)
    angle = 2.0 * np.pi * np.outer(np.arange(NY_A), b) / NY
    y_twiddle = np.stack([np.cos(angle), -np.sin(angle)]).astype(np.float32)
    angle = 2.0 * np.pi * np.outer(np.arange(NX_S), np.tile(r, 4)) / NX
    x_twiddle = np.stack([np.cos(angle), -np.sin(angle)]).astype(np.float32)
    return dict(
        y_forward=y_forward,
        y_inverse=y_inverse,
        x_forward=x_forward,
        x_inverse=x_inverse,
        y_twiddle=y_twiddle,
        x_twiddle=x_twiddle,
    )


def times(value, numerator, length, sign):
    real, imag = value
    turn = (sign * numerator) % length
    eighth = turn * 8
    if turn == 0:
        return real, imag
    if eighth % length == 0:
        step = eighth // length
        half = math.sqrt(0.5)
        if step == 2:
            return -imag, real
        if step == 4:
            return -real, -imag
        if step == 6:
            return imag, -real
        if step == 1:
            return (real - imag) * half, (real + imag) * half
        if step == 3:
            return (real + imag) * -half, (real - imag) * half
        if step == 5:
            return (imag - real) * half, (real + imag) * -half
        return (real + imag) * half, (imag - real) * half
    cosine = math.cos(2.0 * math.pi * turn / length)
    sine = math.sin(2.0 * math.pi * turn / length)
    return real * cosine - imag * sine, real * sine + imag * cosine


def plus(left, right):
    return left[0] + right[0], left[1] + right[1]


def minus(left, right):
    return left[0] - right[0], left[1] - right[1]


def transform(values, sign):
    length = len(values)
    if length == 1:
        return values
    if length == 2:
        return [plus(values[0], values[1]), minus(values[0], values[1])]
    if length == 4:
        even_sum, even_diff = plus(values[0], values[2]), minus(values[0], values[2])
        odd_sum, odd_diff = plus(values[1], values[3]), minus(values[1], values[3])
        if sign > 0:
            first = (even_diff[0] - odd_diff[1], even_diff[1] + odd_diff[0])
            third = (even_diff[0] + odd_diff[1], even_diff[1] - odd_diff[0])
        else:
            first = (even_diff[0] + odd_diff[1], even_diff[1] - odd_diff[0])
            third = (even_diff[0] - odd_diff[1], even_diff[1] + odd_diff[0])
        return [plus(even_sum, odd_sum), first, minus(even_sum, odd_sum), third]
    radix = 4 if length % 4 == 0 and length > 8 else 2
    rest = length // radix
    columns = [transform(values[i::radix], sign) for i in range(radix)]
    result = [None] * length
    for k in range(rest):
        picked = [times(columns[i][k], i * k, length, sign) for i in range(radix)]
        for q, value in enumerate(transform(picked, sign)):
            result[k + rest * q] = value
    return result


def spread(value):
    high = value.astype(BF16)
    low = (value - high.astype(jnp.float32)).astype(BF16)
    return jnp.concatenate([high, high, low], axis=1)


def matmul(left, right, contract):
    return lax.dot_general(left, right, (contract, ((), ())), preferred_element_type=jnp.float32)


def forward_y_kernel(wave_ref, matrix_ref, twiddle_ref, out_ref, mid_ref):
    for field in range(2):
        for tile in range(4):
            rows = slice(8 * tile, 8 * tile + 8)
            values = [
                tuple(wave_ref[field, 0, c, rows, 128 * a : 128 * a + 128] for c in range(2))
                for a in range(NY_A)
            ]
            for k1, (real, imag) in enumerate(transform(values, -1)):
                if k1:
                    tr, ti = twiddle_ref[0, k1 : k1 + 1, :], twiddle_ref[1, k1 : k1 + 1, :]
                    real, imag = real * tr - imag * ti, real * ti + imag * tr
                at = k1 * 64 + field * 32 + tile * 8
                mid_ref[at : at + 8, 0:128] = real
                mid_ref[at : at + 8, 128:256] = imag
    matrix = matrix_ref[...]
    for pair in range(4):
        packed = spread(mid_ref[256 * pair : 256 * pair + 256, :])
        product = matmul(matrix, packed, ((1,), (1,)))
        for half in range(2):
            at = 16 * pair + 8 * half
            out_ref[at : at + 8] = product[:, 128 * half : 128 * half + 128].reshape(8, 32, 128)


def column_transform(load, store, sign, hold_ref):
    for n0 in range(8):
        piece = transform([load(8 * n1 + n0) for n1 in range(8)], sign)
        for ka in range(8):
            real, imag = times(piece[ka], n0 * ka, 64, sign)
            hold_ref[0, ka * 8 + n0] = real
            hold_ref[1, ka * 8 + n0] = imag
    for ka in range(8):
        values = [(hold_ref[0, ka * 8 + n0], hold_ref[1, ka * 8 + n0]) for n0 in range(8)]
        for kb, value in enumerate(transform(values, sign)):
            store(ka + 8 * kb, value)


def middle_kernel(
    in_ref, shift_ref, mask_ref, forward_ref, inverse_ref, twiddle_ref, out_ref, mid_ref, back_ref, hold_ref
):
    for tile in range(2):
        sub = 8 * tile

        def load(s, sub=sub):
            return in_ref[s, sub : sub + 8, :], in_ref[s, 16 + sub : 24 + sub, :]

        def store(m1, value, sub=sub):
            real, imag = value
            tr, ti = twiddle_ref[0, m1 : m1 + 1, :], twiddle_ref[1, m1 : m1 + 1, :]
            at = m1 * 16 + sub
            mid_ref[at : at + 8, 0:128] = real * tr - imag * ti
            mid_ref[at : at + 8, 128:256] = real * ti + imag * tr

        column_transform(load, store, -1, hold_ref.at[0])
    forward, inverse = forward_ref[...], inverse_ref[...]
    for part in range(4):
        rows = slice(256 * part, 256 * part + 256)
        spectrum = matmul(spread(mid_ref[rows, :]), forward, ((1,), (0,)))
        real, imag = spectrum[:, :128], spectrum[:, 128:]
        for ref in range(2):
            cosine, sine = shift_ref[2 * ref, rows, :], shift_ref[2 * ref + 1, rows, :]
            turned = jnp.concatenate([real * cosine - imag * sine, real * sine + imag * cosine], axis=1)
            back_ref[ref, rows, :] = matmul(spread(turned), inverse, ((1,), (0,)))
    for tile in range(2):
        sub = 8 * tile
        for ref in range(2):

            def load(m1, ref=ref, sub=sub):
                at = m1 * 16 + sub
                real, imag = back_ref[ref, at : at + 8, 0:128], back_ref[ref, at : at + 8, 128:256]
                tr, ti = twiddle_ref[0, m1 : m1 + 1, :], twiddle_ref[1, m1 : m1 + 1, :]
                return real * tr + imag * ti, imag * tr - real * ti

            if ref == 0:

                def store(s, value, sub=sub):
                    out_ref[s, sub : sub + 8, :] = value[0]
                    out_ref[s, 16 + sub : 24 + sub, :] = value[1]

            else:

                def store(s, value, sub=sub):
                    chosen = mask_ref[s : s + 1, :] > 0.5
                    out_ref[s, sub : sub + 8, :] = jnp.where(chosen, value[0], out_ref[s, sub : sub + 8, :])
                    out_ref[s, 16 + sub : 24 + sub, :] = jnp.where(
                        chosen, value[1], out_ref[s, 16 + sub : 24 + sub, :]
                    )

            column_transform(load, store, 1, hold_ref.at[ref])


def inverse_y_kernel(in_ref, phase_ref, matrix_ref, twiddle_ref, out_ref, edge_ref, mid_ref):
    matrix = matrix_ref[...]
    for p in range(8):
        block = in_ref[8 * p : 8 * p + 8].reshape(256, 128)
        mid_ref[128 * p : 128 * p + 128, :] = matmul(spread(block.T), matrix, ((1,), (0,)))
    for field in range(2):
        for tile in range(4):
            rows = slice(8 * tile, 8 * tile + 8)
            values = []
            for k1 in range(NY_A):
                at = k1 * 64 + field * 32 + tile * 8
                real, imag = mid_ref[at : at + 8, 0:128], mid_ref[at : at + 8, 128:256]
                if k1:
                    tr, ti = twiddle_ref[0, k1 : k1 + 1, :], twiddle_ref[1, k1 : k1 + 1, :]
                    real, imag = real * tr + imag * ti, imag * tr - real * ti
                values.append((real, imag))
            for a, (real, imag) in enumerate(transform(values, 1)):
                lanes = slice(128 * a, 128 * a + 128)
                cosine, sine = phase_ref[0, rows, lanes], phase_ref[1, rows, lanes]
                if field == 0:
                    real, imag = real * cosine + imag * sine, imag * cosine - real * sine
                else:
                    real, imag = real * cosine - imag * sine, imag * cosine + real * sine
                for c, value in enumerate((real, imag)):
                    out_ref[field, c, rows, lanes] = value
                    row = 2 * field + c
                    if tile == 0:
                        edge_ref[0, row : row + 1, lanes] = value[0:1]
                    if tile == 3:
                        edge_ref[1, row : row + 1, lanes] = value[7:8]


def laplace_kernel(place_ref, wave_ref, above_ref, below_ref, coupling_ref, out_ref, *rest):
    image_refs, image_hold = rest[:4], rest[4]
    row = lax.broadcasted_iota(jnp.int32, (8, 2048), 0)
    lane = lax.broadcasted_iota(jnp.int32, (8, 2048), 1)
    for tile in range(4):
        rows = slice(8 * tile, 8 * tile + 8)
        coupling = coupling_ref[rows, :]
        results = []
        for field in range(2):
            laplace = []
            for c in range(2):
                value = wave_ref[field, c, rows, :]
                index = 2 * field + c
                if tile == 0:
                    before = above_ref[index : index + 1, :]
                else:
                    before = wave_ref[field, c, 8 * tile - 1 : 8 * tile, :]
                if tile == 3:
                    after = below_ref[index : index + 1, :]
                else:
                    after = wave_ref[field, c, 8 * tile + 8 : 8 * tile + 9, :]
                up = jnp.where(row == 0, before, pltpu.roll(value, 1, 0))
                down = jnp.where(row == 7, after, pltpu.roll(value, 7, 0))
                left = jnp.where(lane == 0, 0.0, pltpu.roll(value, 1, 1))
                right = jnp.where(lane == 2047, 0.0, pltpu.roll(value, 2047, 1))
                laplace.append(up + down + left + right - 4.0 * value)
            sign = -1.0 if field == 0 else 1.0
            scaled = coupling * sign
            real = wave_ref[field, 0, rows, :] - scaled * laplace[1]
            imag = wave_ref[field, 1, rows, :] + scaled * laplace[0]
            out_ref[field, 0, 0, rows, :] = real
            out_ref[field, 0, 1, rows, :] = imag
            results.append((real, imag))
        image_hold[rows, :] = results[0][0] * results[1][0] + results[0][1] * results[1][1]
    place = place_ref[0]
    for k in range(4):
        at = pl.multiple_of(((place + k) % 4) * 8, 8)
        image_refs[k][...] = image_hold[pl.ds(at, 8), :]


def assemble_kernel(place_ref, own_ref, *rest):
    others, out_ref = rest[:3], rest[3]
    place = place_ref[0]
    for k, ref in enumerate((own_ref,) + tuple(others)):
        at = pl.multiple_of(((place + 4 - k) % 4) * 8, 8)
        out_ref[0, pl.ds(at, 8), :] = ref[...]


def whole(memory=pltpu.VMEM):
    return pl.BlockSpec(memory_space=memory)


def f32(*shape):
    return jax.ShapeDtypeStruct(shape, jnp.float32)


def call(kernel, out_shape, operands, scratch=(), smem=0, near=(), near_out=False):
    many = isinstance(out_shape, (tuple, list))
    if not INTERPRET:
        operands = tuple(
            pltpu.with_memory_space_constraint(x, pltpu.VMEM) if i in near else x
            for i, x in enumerate(operands)
        )
        if near_out:
            shapes = out_shape if many else (out_shape,)
            shapes = tuple(pltpu.VMEM(x.shape, x.dtype) for x in shapes)
            out_shape = shapes if many else shapes[0]
    return pl.pallas_call(
        kernel,
        out_shape=out_shape,
        in_specs=[whole(pltpu.SMEM)] * smem + [whole()] * (len(operands) - smem),
        out_specs=[whole()] * len(out_shape) if many else whole(),
        scratch_shapes=list(scratch),
        interpret=INTERPRET,
        compiler_params=pltpu.CompilerParams(vmem_limit_bytes=VMEM_BYTES),
    )(*operands)


def forward_y(wavefields):
    const = constants()
    return call(
        forward_y_kernel,
        f32(64, 32, 128),
        (wavefields, jnp.asarray(const["y_forward"]), jnp.asarray(const["y_twiddle"])),
        (pltpu.VMEM((1024, 256), jnp.float32),),
        near_out=True,
    )


def middle(blocks, shift, mask):
    const = constants()
    return call(
        middle_kernel,
        f32(64, 32, 128),
        (
            blocks,
            shift,
            mask,
            jnp.asarray(const["x_forward"]),
            jnp.asarray(const["x_inverse"]),
            jnp.asarray(const["x_twiddle"]),
        ),
        (
            pltpu.VMEM((1024, 256), jnp.float32),
            pltpu.VMEM((2, 1024, 256), jnp.float32),
            pltpu.VMEM((2, 2, 64, 8, 128), jnp.float32),
        ),
        near=(0, 1, 2),
        near_out=True,
    )


def inverse_y(blocks, phase):
    const = constants()
    return call(
        inverse_y_kernel,
        (f32(2, 2, 32, 2048), f32(2, 4, 2048)),
        (blocks, phase, jnp.asarray(const["y_inverse"]), jnp.asarray(const["y_twiddle"])),
        (pltpu.VMEM((1024, 256), jnp.float32),),
        near=(0, 1),
        near_out=True,
    )


def laplace(place, wave, above, below, coupling):
    return call(
        laplace_kernel,
        (f32(2, 1, 2, 32, 2048),) + (f32(8, 2048),) * 4,
        (place, wave, above, below, coupling),
        (pltpu.VMEM((32, 2048), jnp.float32),),
        smem=1,
    )


def assemble(place, pieces):
    return call(assemble_kernel, f32(1, 32, 2048), (place,) + tuple(pieces), smem=1)


def wave_values(number, length):
    signed = jnp.where(number < length // 2, number, number - length)
    return 2.0 * math.pi / length * signed.astype(jnp.float32)


def shift_tables(space_index, omega, ref_velocity):
    row = lax.broadcasted_iota(jnp.int32, (1024, 128), 0)
    lane = lax.broadcasted_iota(jnp.int32, (1024, 128), 1)
    kx = wave_values(row // 16 + 64 * (lane % 32), NX)
    k1 = 2 * (space_index // 8) + lane // 64
    k2 = 16 * (space_index % 8) + row % 16
    ky = wave_values(k1 + 16 * k2, NY)
    sign = jnp.where((lane // 32) % 2 == 0, -1.0, 1.0).astype(jnp.float32)
    squared = kx**2 + ky**2
    tables = []
    for ref in range(2):
        vertical = (omega / ref_velocity[ref]) ** 2 - squared
        root = DZ * jnp.sqrt(jnp.abs(vertical))
        travels = vertical >= 0.0
        tables.append(jnp.where(travels, jnp.cos(root), jnp.exp(-root)))
        tables.append(jnp.where(travels, sign * jnp.sin(root), 0.0))
    return jnp.stack(tables)


def mask_table(ref_index):
    return jnp.tile(jnp.repeat(ref_index.reshape(64, 2), 16, axis=1), (1, 4)).astype(jnp.float32)


def phase_tables(speed, ref_rows, omega):
    time_shift = omega * DZ * (1.0 / speed - 1.0 / ref_rows)
    return jnp.stack([jnp.cos(time_shift), jnp.sin(time_shift)])


def coupling_table(speed, ref_rows, omega):
    return DZ * (speed - ref_rows) * ref_rows / (16.0 * omega)


def shifted_pairs(step, count=4):
    return [(i, (i + step) % count) for i in range(count)]


def slab_speed(velocity, owner, freq_index):
    stored = lax.dynamic_index_in_dim(velocity, owner % 4, 0, keepdims=False).reshape(4, 8, 2048)
    source = owner // 4
    mine = lax.dynamic_index_in_dim(stored, freq_index, 0, keepdims=False)
    for step in (1, 2, 3):
        piece = lax.dynamic_index_in_dim(stored, (freq_index + step) % 4, 0, keepdims=False)
        arrived = lax.ppermute(piece, "freq", shifted_pairs(step))
        mine = jnp.where((freq_index + 4 - step) % 4 == source, arrived, mine)
    return gathered(mine)


def gathered(mine):
    return [mine] + [lax.ppermute(mine, "freq", shifted_pairs(step)) for step in (1, 2, 3)]


def per_device(wavefields, frequencies, velocity, slab_owner, ref_velocity, ref_index):
    space_index = lax.axis_index("space")
    freq_index = lax.axis_index("freq")
    place = freq_index.reshape(1).astype(jnp.int32)
    omega = frequencies[0]
    blocks = forward_y(wavefields)
    blocks = lax.all_to_all(blocks, "space", split_axis=0, concat_axis=0, tiled=True)
    shift = shift_tables(space_index, omega, ref_velocity[0])
    speed = assemble(place, slab_speed(velocity, slab_owner[0], freq_index))[0]
    local_refs = lax.dynamic_slice_in_dim(ref_index[0], 2 * space_index, 2)
    ref_rows = jnp.repeat(ref_velocity[0][local_refs], 16)[:, None]
    phase = phase_tables(speed, ref_rows, omega)
    coupling = coupling_table(speed, ref_rows, omega)
    mask = mask_table(ref_index[0])
    blocks, shift, mask, phase, coupling = lax.optimization_barrier((blocks, shift, mask, phase, coupling))
    blocks = middle(blocks, shift, mask)
    blocks = lax.all_to_all(blocks, "space", split_axis=0, concat_axis=0, tiled=True)
    wave, edges = inverse_y(blocks, phase)
    count = 64
    above = lax.ppermute(edges[1], "space", [(i, i + 1) for i in range(count - 1)])
    below = lax.ppermute(edges[0], "space", [(i + 1, i) for i in range(count - 1)])
    fields, *quarters = laplace(place, wave, above, below, coupling)
    total = quarters[0]
    for step in (1, 2, 3):
        total = total + lax.ppermute(quarters[step], "freq", shifted_pairs(step))
    image = assemble(place, gathered(total))
    return fields, image


def solution(mesh):
    in_specs = (
        P(None, "freq", None, "space", None),
        P("freq"),
        P("freq", "space", None),
        P(),
        P(),
        P(),
    )
    out_specs = (P(None, "freq", None, "space", None), P(None, "space", None))
    return jax.shard_map(
        per_device, mesh=mesh, in_specs=in_specs, out_specs=out_specs, check_vma=False
    )
```

profile of v0, /device:TPU:2, one launch (start us, length us, event | category | flops | bytes accessed | tf_op | source)
XLA Modules:
  0.0 144.3 jit_solution(14599966935681217486)
XLA Ops:
  0.6 0.0 copy-start
  1.4 0.4 copy-done
  1.9 0.7 dynamic-slice_bitcast_fusion.1
  2.6 4.6 %collective-permute-start = (f32[8,2048]{1,0:T(8,128)}, f32[8,2048]{1,0:T(8,128)S(1)}, u32[]{:S(2)}, u32[]{:S(2)}) collective-permute-start(f32[8,2048]{1,0:T(8,128)} %get-tuple-element.30), channel_id=1, source_target_pairs={{0,192},{64,0},{128,64},{192,128},{1,193},{65,1},{129,65},{193,129... | collective-permute-start | bytes 196616 | tf_op jit(solution)/shard_map/ppermute | solution.py:447
  7.2 0.0 collective-permute-start.1
  7.2 0.7 collective-permute-start.2
  7.9 1.2 copy-done.2
  9.1 1.0 copy-done.5
  10.1 0.7 copy-done.8
  10.8 1.8 %shard_map.131 = f32[64,32,128]{2,1,0:T(8,128)} custom-call(f32[2,1,2,32,2048]{4,3,2,1,0:T(8,128)S(1)} %copy-done.2, bf16[256,768]{1,0:T(8,128)(2,1)S(1)} %copy-done.5, f32[2,16,128]{2,1,0:T(8,128)S(1)} %copy-done.8), custom_call_target="tpu_custom_call" | custom-call | tf_op jit(solution)/shard_map/pallas_call | solution.py:329
  12.6 13.0 %all-to-all-start = ((f32[64,32,128]{2,1,0:T(8,128)}), f32[64,32,128]{2,1,0:T(8,128)}, u32[]{:S(2)}, u32[]{:S(2)}) async-start(f32[64,32,128]{2,1,0:T(8,128)} %shard_map.131), calls=%async_computation | async-start | bytes 2097152 | tf_op jit(solution)/shard_map/all_to_all | solution.py:462
  25.8 0.1 fusion.24
  25.9 0.6 fusion.25
  26.4 0.6 gather_fusion
  27.1 0.1 broadcast_in_dim.21
  27.1 0.1 broadcast_in_dim_reshape.3
  29.2 4.7 %exponential_select_fusion.1 = (f32[1,1024,128]{2,1,0:T(8,128)S(1)}, f32[1,1024,128]{2,1,0:T(8,128)S(1)}, f32[1,1024,128]{2,1,0:T(8,128)S(1)}, f32[1,1024,128]{2,1,0:T(8,128)S(1)}) fusion(f32[]{:T(128)S(6)} %integer_pow.50, s32[1024]{0:T(1024)S(1)} %get-tuple-element.46, s32[1024]{0:T(1024)S(1)} %get-tuple-element.47, ...), kind=kLoop, calls=%fused_computation.25 | loop fusion | flops 6946816 | bytes 2119056 | tf_op jit(solution)/shard_map/jit(_where)/select_n | solution.py:419
  33.9 0.1 pad_maximum_fusion.shift_ref
  34.1 0.0 copy-start.7
  34.1 0.0 collective-permute-done.1
  34.2 0.6 copy-done.11
  34.8 0.0 collective-permute-done.2
  34.8 0.9 fusion.14.own_ref
  35.6 2.0 %collective-permute-start.3 = (f32[8,2048]{1,0:T(8,128)S(1)}, f32[8,2048]{1,0:T(8,128)S(1)}, u32[]{:S(2)}, u32[]{:S(2)}) collective-permute-start(f32[8,2048]{1,0:T(8,128)S(1)} %fusion.14.own_ref), channel_id=1, source_target_pairs={{0,64},{64,128},{128,192},{192,0},{1,65},{65,129},{129,193},{193,1... | collective-permute-start | bytes 196616 | tf_op jit(solution)/shard_map/ppermute | solution.py:453
  37.6 0.6 collective-permute-start.4
  38.2 1.9 %collective-permute-start.5 = (f32[8,2048]{1,0:T(8,128)S(1)}, f32[8,2048]{1,0:T(8,128)S(1)}, u32[]{:S(2)}, u32[]{:S(2)}) collective-permute-start(f32[8,2048]{1,0:T(8,128)S(1)} %fusion.14.own_ref), channel_id=1, source_target_pairs={{0,192},{64,0},{128,64},{192,128},{1,193},{65,1},{129,65},{193,129... | collective-permute-start | bytes 196616 | tf_op jit(solution)/shard_map/ppermute | solution.py:453
  40.1 0.7 convert_reduce_fusion
  40.8 0.1 convert_element_type.61
  40.9 0.1 copy.14
  41.0 5.0 %collective-permute-done.3.rest_0_ = f32[8,2048]{1,0:T(8,128)S(1)} collective-permute-done((f32[8,2048]{1,0:T(8,128)S(1)}, f32[8,2048]{1,0:T(8,128)S(1)}, u32[]{:S(2)}, u32[]{:S(2)}) %collective-permute-start.3) | collective-permute-done | bytes 65568 | tf_op jit(solution)/shard_map/ppermute | solution.py:453
  45.9 2.2 %collective-permute-done.4.rest_1_ = f32[8,2048]{1,0:T(8,128)S(1)} collective-permute-done((f32[8,2048]{1,0:T(8,128)S(1)}, f32[8,2048]{1,0:T(8,128)S(1)}, u32[]{:S(2)}, u32[]{:S(2)}) %collective-permute-start.4) | collective-permute-done | bytes 65568 | tf_op jit(solution)/shard_map/ppermute | solution.py:453
  48.2 6.7 %collective-permute-done.5.rest_2_ = f32[8,2048]{1,0:T(8,128)S(1)} collective-permute-done((f32[8,2048]{1,0:T(8,128)S(1)}, f32[8,2048]{1,0:T(8,128)S(1)}, u32[]{:S(2)}, u32[]{:S(2)}) %collective-permute-start.5) | collective-permute-done | bytes 65568 | tf_op jit(solution)/shard_map/ppermute | solution.py:453
  54.9 1.1 fusion.16
  56.0 0.8 pad_maximum_fusion.1.phase_ref
  56.9 0.1 fusion.12.coupling_ref
  57.0 0.0 all-to-all-done.in_ref
  57.0 0.6 tile.2
  57.6 0.9 copy.15.mask_ref
  58.5 0.0 copy-done.7
  58.5 0.0 copy-start.3
  58.6 1.0 copy-done.3
  59.5 1.0 copy-done.4
  60.5 4.4 %shard_map.133 = f32[64,32,128]{2,1,0:T(8,128)S(1)} custom-call(f32[64,32,128]{2,1,0:T(8,128)} %all-to-all-done.in_ref, f32[4,1024,128]{2,1,0:T(8,128)S(1)} %pad_maximum_fusion.shift_ref, f32[64,128]{1,0:T(8,128)S(1)} %copy.15.mask_ref, bf16[768,256]{1,0:T(8,128)(2,1)S(1)} %copy-done.3, bf16[768,256]{1,0:T(8,128)(2,1)S(1)} %copy-done.4, ...), custom_call_target="tpu_custom_call" | custom-call | tf_op jit(solution)/shard_map/pallas_call | solution.py:329
  65.0 0.0 copy-start.6
  65.0 0.0 copy-start.9
  65.0 37.4 %all_to_all.10.in_ref = f32[64,32,128]{2,1,0:T(8,128)S(1)} all-to-all(f32[64,32,128]{2,1,0:T(8,128)S(1)} %shard_map.133), channel_id=1, replica_groups=mesh['freq'=4,'space'=64] {'space'}, dimensions={0} | all-to-all | bytes 2097152 | tf_op jit(solution)/shard_map/all_to_all | solution.py:472
  102.4 1.0 shard_map.134
  103.4 4.1 %collective-permute-start.6 = (f32[4,2048]{1,0:T(4,128)S(1)}, f32[4,2048]{1,0:T(4,128)S(1)}, u32[]{:S(2)}, u32[]{:S(2)}) collective-permute-start(f32[4,2048]{1,0:T(4,128)S(1)} %get-tuple-element.32), channel_id=1, source_target_pairs={{0,1},{1,2},{2,3},{3,4},{4,5},{5,6},{6,7},{7,8},{8,9},{9,10},{10,1... | collective-permute-start | bytes 98312 | tf_op jit(solution)/shard_map/ppermute | solution.py:475
  107.5 8.4 %collective-permute-start.7 = (f32[4,2048]{1,0:T(4,128)S(1)}, f32[4,2048]{1,0:T(4,128)S(1)}, u32[]{:S(2)}, u32[]{:S(2)}) collective-permute-start(f32[4,2048]{1,0:T(4,128)S(1)} %get-tuple-element.31), channel_id=1, source_target_pairs={{1,0},{2,1},{3,2},{4,3},{5,4},{6,5},{7,6},{8,7},{9,8},{10,9},{11,1... | collective-permute-start | bytes 98312 | tf_op jit(solution)/shard_map/ppermute | solution.py:476
  115.9 0.0 collective-permute-done.6.above_ref
  115.9 1.6 %collective-permute-done.7.below_ref = f32[4,2048]{1,0:T(4,128)S(1)} collective-permute-done((f32[4,2048]{1,0:T(4,128)S(1)}, f32[4,2048]{1,0:T(4,128)S(1)}, u32[]{:S(2)}, u32[]{:S(2)}) %collective-permute-start.7) | collective-permute-done | bytes 32800 | tf_op jit(solution)/shard_map/ppermute | solution.py:476
  117.5 1.6 %shard_map.135 = (f32[2,1,2,32,2048]{4,3,2,1,0:T(8,128)}, f32[8,2048]{1,0:T(8,128)S(1)}, f32[8,2048]{1,0:T(8,128)S(1)}, f32[8,2048]{1,0:T(8,128)S(1)}, f32[8,2048]{1,0:T(8,128)S(1)}) custom-call(s32[1]{0:T(128)} %bitcast.place_ref, f32[2,2,32,2048]{3,2,1,0:T(8,128)S(1)} %get-tuple-element.18.wave_ref, f32[4,2048]{1,0:T(4,128)S(1)} %collective-permute-done.6.above_ref, ...), custom_call_target="tpu_custom_call" | custom-call | tf_op jit(solution)/shard_map/pallas_call | solution.py:329
  119.1 0.0 collective-permute-start.10
  119.1 9.3 %collective-permute-start.8 = (f32[8,2048]{1,0:T(8,128)S(1)}, f32[8,2048]{1,0:T(8,128)S(1)}, u32[]{:S(2)}, u32[]{:S(2)}) collective-permute-start(f32[8,2048]{1,0:T(8,128)S(1)} %get-tuple-element.23), channel_id=1, source_target_pairs={{0,64},{64,128},{128,192},{192,0},{1,65},{65,129},{129,193},{193,1... | collective-permute-start | bytes 196616 | tf_op jit(solution)/shard_map/ppermute | solution.py:480
  128.4 1.5 %collective-permute-start.9 = (f32[8,2048]{1,0:T(8,128)S(1)}, f32[8,2048]{1,0:T(8,128)S(1)}, u32[]{:S(2)}, u32[]{:S(2)}) collective-permute-start(f32[8,2048]{1,0:T(8,128)S(1)} %get-tuple-element.24), channel_id=1, source_target_pairs={{0,128},{64,192},{128,0},{192,64},{1,129},{65,193},{129,1},{193,65... | collective-permute-start | bytes 196616 | tf_op jit(solution)/shard_map/ppermute | solution.py:480
  129.9 0.8 collective-permute-done.10
  130.7 2.0 %collective-permute-done.8 = f32[8,2048]{1,0:T(8,128)S(1)} collective-permute-done((f32[8,2048]{1,0:T(8,128)S(1)}, f32[8,2048]{1,0:T(8,128)S(1)}, u32[]{:S(2)}, u32[]{:S(2)}) %collective-permute-start.8) | collective-permute-done | bytes 65568 | tf_op jit(solution)/shard_map/ppermute | solution.py:480
  132.7 4.0 %collective-permute-done.9 = f32[8,2048]{1,0:T(8,128)S(1)} collective-permute-done((f32[8,2048]{1,0:T(8,128)S(1)}, f32[8,2048]{1,0:T(8,128)S(1)}, u32[]{:S(2)}, u32[]{:S(2)}) %collective-permute-start.9) | collective-permute-done | bytes 65568 | tf_op jit(solution)/shard_map/ppermute | solution.py:480
  136.7 0.1 collective-permute-start.11
  136.8 1.7 %collective-permute-start.12 = (f32[8,2048]{1,0:T(8,128)S(1)}, f32[8,2048]{1,0:T(8,128)S(1)}, u32[]{:S(2)}, u32[]{:S(2)}) collective-permute-start(f32[8,2048]{1,0:T(8,128)S(1)} %add_add_fusion.own_ref), channel_id=1, source_target_pairs={{0,128},{64,192},{128,0},{192,64},{1,129},{65,193},{129,1},{193,65... | collective-permute-start | bytes 196616 | tf_op jit(solution)/shard_map/ppermute | solution.py:453
  138.5 2.1 %collective-permute-start.13 = (f32[8,2048]{1,0:T(8,128)S(1)}, f32[8,2048]{1,0:T(8,128)S(1)}, u32[]{:S(2)}, u32[]{:S(2)}) collective-permute-start(f32[8,2048]{1,0:T(8,128)S(1)} %add_add_fusion.own_ref), channel_id=1, source_target_pairs={{0,192},{64,0},{128,64},{192,128},{1,193},{65,1},{129,65},{193,129... | collective-permute-start | bytes 196616 | tf_op jit(solution)/shard_map/ppermute | solution.py:453
  140.6 2.2 %collective-permute-done.11.rest_0_ = f32[8,2048]{1,0:T(8,128)S(1)} collective-permute-done((f32[8,2048]{1,0:T(8,128)S(1)}, f32[8,2048]{1,0:T(8,128)S(1)}, u32[]{:S(2)}, u32[]{:S(2)}) %collective-permute-start.11) | collective-permute-done | bytes 65568 | tf_op jit(solution)/shard_map/ppermute | solution.py:453
  142.9 0.7 collective-permute-done.13.rest_2_
  143.6 0.7 shard_map.136
  (30 shorter events, 0.2 us)
Async XLA Ops:
  0.6 1.2 copy-start
  2.6 31.5 %collective-permute-start = (f32[8,2048]{1,0:T(8,128)}, f32[8,2048]{1,0:T(8,128)S(1)}, u32[]{:S(2)}, u32[]{:S(2)}) collective-permute-start(f32[8,2048]{1,0:T(8,128)} %get-tuple-element.30), channel_id=1, source_target_pairs={{0,192},{64,0},{128,64},{192,128},{1,193},{65,1},{129,65},{193,129... | collective-permute-start | bytes 196616 | tf_op jit(solution)/shard_map/ppermute | solution.py:447
  7.2 26.9 %collective-permute-start.1 = (f32[8,2048]{1,0:T(8,128)}, f32[8,2048]{1,0:T(8,128)}, u32[]{:S(2)}, u32[]{:S(2)}) collective-permute-start(f32[8,2048]{1,0:T(8,128)} %get-tuple-element.29), channel_id=1, source_target_pairs={{0,128},{64,192},{128,0},{192,64},{1,129},{65,193},{129,1},{193,65... | collective-permute-start | bytes 196616 | tf_op jit(solution)/shard_map/ppermute | solution.py:447
  7.2 27.5 %collective-permute-start.2 = (f32[8,2048]{1,0:T(8,128)}, f32[8,2048]{1,0:T(8,128)}, u32[]{:S(2)}, u32[]{:S(2)}) collective-permute-start(f32[8,2048]{1,0:T(8,128)} %get-tuple-element.28), channel_id=1, source_target_pairs={{0,64},{64,128},{128,192},{192,0},{1,65},{65,129},{129,193},{193,1... | collective-permute-start | bytes 196616 | tf_op jit(solution)/shard_map/ppermute | solution.py:447
  7.9 1.2 copy-start.2
  9.1 1.0 copy-start.5
  10.1 0.7 copy-start.8
  10.8 14.9 %copy-start.12 = (s32[1,128]{1,0:T(1,128)S(1)}, s32[1,128]{1,0:T(1,128)}, u32[]{:S(2)}) copy-start(s32[1,128]{1,0:T(1,128)} %param.17) | copy-start | bytes 1540
  10.8 15.0 %copy-start.10 = (f32[1,2]{1,0:T(1,128)S(1)}, f32[1,2]{1,0:T(1,128)}, u32[]{:S(2)}) copy-start(f32[1,2]{1,0:T(1,128)} %param.16) | copy-start | bytes 28
  12.6 44.4 %all-to-all-start = ((f32[64,32,128]{2,1,0:T(8,128)}), f32[64,32,128]{2,1,0:T(8,128)}, u32[]{:S(2)}, u32[]{:S(2)}) async-start(f32[64,32,128]{2,1,0:T(8,128)} %shard_map.131), calls=%async_computation | async-start | bytes 2097152 | tf_op jit(solution)/shard_map/all_to_all | solution.py:462
  34.1 24.5 %copy-start.7 = (f32[2,64,128]{2,1,0:T(8,128)S(1)}, f32[2,64,128]{2,1,0:T(8,128)}, u32[]{:S(2)}) copy-start(f32[2,64,128]{2,1,0:T(8,128)} %constant.222.clone.twiddle_ref) | copy-start | bytes 196612
  34.1 0.6 copy-start.11
  35.6 10.3 %collective-permute-start.3 = (f32[8,2048]{1,0:T(8,128)S(1)}, f32[8,2048]{1,0:T(8,128)S(1)}, u32[]{:S(2)}, u32[]{:S(2)}) collective-permute-start(f32[8,2048]{1,0:T(8,128)S(1)} %fusion.14.own_ref), channel_id=1, source_target_pairs={{0,64},{64,128},{128,192},{192,0},{1,65},{65,129},{129,193},{193,1... | collective-permute-start | bytes 196616 | tf_op jit(solution)/shard_map/ppermute | solution.py:453
  37.6 10.6 %collective-permute-start.4 = (f32[8,2048]{1,0:T(8,128)S(1)}, f32[8,2048]{1,0:T(8,128)S(1)}, u32[]{:S(2)}, u32[]{:S(2)}) collective-permute-start(f32[8,2048]{1,0:T(8,128)S(1)} %fusion.14.own_ref), channel_id=1, source_target_pairs={{0,128},{64,192},{128,0},{192,64},{1,129},{65,193},{129,1},{193,65... | collective-permute-start | bytes 196616 | tf_op jit(solution)/shard_map/ppermute | solution.py:453
  38.2 16.6 %collective-permute-start.5 = (f32[8,2048]{1,0:T(8,128)S(1)}, f32[8,2048]{1,0:T(8,128)S(1)}, u32[]{:S(2)}, u32[]{:S(2)}) collective-permute-start(f32[8,2048]{1,0:T(8,128)S(1)} %fusion.14.own_ref), channel_id=1, source_target_pairs={{0,192},{64,0},{128,64},{192,128},{1,193},{65,1},{129,65},{193,129... | collective-permute-start | bytes 196616 | tf_op jit(solution)/shard_map/ppermute | solution.py:453
  58.5 1.0 copy-start.3
  59.5 1.0 copy-start.4
  65.0 37.4 %copy-start.1 = (f32[2,32,2048]{2,1,0:T(8,128)S(1)}, f32[2,32,2048]{2,1,0:T(8,128)}, u32[]{:S(2)}) copy-start(f32[2,32,2048]{2,1,0:T(8,128)} %pad_maximum_fusion.1.phase_ref) | copy-start | bytes 1572868
  65.0 37.4 %copy-start.6 = (bf16[768,256]{1,0:T(8,128)(2,1)S(1)}, bf16[768,256]{1,0:T(8,128)(2,1)}, u32[]{:S(2)}) copy-start(bf16[768,256]{1,0:T(8,128)(2,1)} %constant.223.clone.matrix_ref) | copy-start | bytes 1179652
  65.0 37.4 %copy-start.9 = (f32[2,16,128]{2,1,0:T(8,128)S(1)}, f32[2,16,128]{2,1,0:T(8,128)}, u32[]{:S(2)}) copy-start(f32[2,16,128]{2,1,0:T(8,128)} %constant.219.clone.twiddle_ref) | copy-start | bytes 49156
  103.4 12.5 %collective-permute-start.6 = (f32[4,2048]{1,0:T(4,128)S(1)}, f32[4,2048]{1,0:T(4,128)S(1)}, u32[]{:S(2)}, u32[]{:S(2)}) collective-permute-start(f32[4,2048]{1,0:T(4,128)S(1)} %get-tuple-element.32), channel_id=1, source_target_pairs={{0,1},{1,2},{2,3},{3,4},{4,5},{5,6},{6,7},{7,8},{8,9},{9,10},{10,1... | collective-permute-start | bytes 98312 | tf_op jit(solution)/shard_map/ppermute | solution.py:475
  107.5 10.0 %collective-permute-start.7 = (f32[4,2048]{1,0:T(4,128)S(1)}, f32[4,2048]{1,0:T(4,128)S(1)}, u32[]{:S(2)}, u32[]{:S(2)}) collective-permute-start(f32[4,2048]{1,0:T(4,128)S(1)} %get-tuple-element.31), channel_id=1, source_target_pairs={{1,0},{2,1},{3,2},{4,3},{5,4},{6,5},{7,6},{8,7},{9,8},{10,9},{11,1... | collective-permute-start | bytes 98312 | tf_op jit(solution)/shard_map/ppermute | solution.py:476
  119.1 11.5 %collective-permute-start.10 = (f32[8,2048]{1,0:T(8,128)S(1)}, f32[8,2048]{1,0:T(8,128)S(1)}, u32[]{:S(2)}, u32[]{:S(2)}) collective-permute-start(f32[8,2048]{1,0:T(8,128)S(1)} %get-tuple-element.25), channel_id=1, source_target_pairs={{0,192},{64,0},{128,64},{192,128},{1,193},{65,1},{129,65},{193,129... | collective-permute-start | bytes 196616 | tf_op jit(solution)/shard_map/ppermute | solution.py:480
  119.1 13.5 %collective-permute-start.8 = (f32[8,2048]{1,0:T(8,128)S(1)}, f32[8,2048]{1,0:T(8,128)S(1)}, u32[]{:S(2)}, u32[]{:S(2)}) collective-permute-start(f32[8,2048]{1,0:T(8,128)S(1)} %get-tuple-element.23), channel_id=1, source_target_pairs={{0,64},{64,128},{128,192},{192,0},{1,65},{65,129},{129,193},{193,1... | collective-permute-start | bytes 196616 | tf_op jit(solution)/shard_map/ppermute | solution.py:480
  128.4 8.3 %collective-permute-start.9 = (f32[8,2048]{1,0:T(8,128)S(1)}, f32[8,2048]{1,0:T(8,128)S(1)}, u32[]{:S(2)}, u32[]{:S(2)}) collective-permute-start(f32[8,2048]{1,0:T(8,128)S(1)} %get-tuple-element.24), channel_id=1, source_target_pairs={{0,128},{64,192},{128,0},{192,64},{1,129},{65,193},{129,1},{193,65... | collective-permute-start | bytes 196616 | tf_op jit(solution)/shard_map/ppermute | solution.py:480
  136.7 6.2 %collective-permute-start.11 = (f32[8,2048]{1,0:T(8,128)S(1)}, f32[8,2048]{1,0:T(8,128)S(1)}, u32[]{:S(2)}, u32[]{:S(2)}) collective-permute-start(f32[8,2048]{1,0:T(8,128)S(1)} %add_add_fusion.own_ref), channel_id=1, source_target_pairs={{0,64},{64,128},{128,192},{192,0},{1,65},{65,129},{129,193},{193,1... | collective-permute-start | bytes 196616 | tf_op jit(solution)/shard_map/ppermute | solution.py:453
  136.8 6.1 %collective-permute-start.12 = (f32[8,2048]{1,0:T(8,128)S(1)}, f32[8,2048]{1,0:T(8,128)S(1)}, u32[]{:S(2)}, u32[]{:S(2)}) collective-permute-start(f32[8,2048]{1,0:T(8,128)S(1)} %add_add_fusion.own_ref), channel_id=1, source_target_pairs={{0,128},{64,192},{128,0},{192,64},{1,129},{65,193},{129,1},{193,65... | collective-permute-start | bytes 196616 | tf_op jit(solution)/shard_map/ppermute | solution.py:453
  138.5 5.0 %collective-permute-start.13 = (f32[8,2048]{1,0:T(8,128)S(1)}, f32[8,2048]{1,0:T(8,128)S(1)}, u32[]{:S(2)}, u32[]{:S(2)}) collective-permute-start(f32[8,2048]{1,0:T(8,128)S(1)} %add_add_fusion.own_ref), channel_id=1, source_target_pairs={{0,192},{64,0},{128,64},{192,128},{1,193},{65,1},{129,65},{193,129... | collective-permute-start | bytes 196616 | tf_op jit(solution)/shard_map/ppermute | solution.py:453
where the time goes:
time: 145 us; the launch traced here: 144 us
  starting transfers between devices  49.9 us (34%)
  blocking collectives  37.4 us (26%)
  waiting for transfers between devices  25.2 us (17%)
  local copies, waits for them, and re-layouts  9.81 us (7%)
  Pallas kernels  9.57 us (7%)
  other arithmetic  8.59 us (6%)
  between operations  3.77 us (3%)
    all_to_all x1, blocking collectives, per_device(): lax.all_to_all(blocks, 'space', split_axis=0, concat_axis=0, tiled=True)  37.4 us
    ppermute x6, waiting for transfers between devices, gathered(): lax.ppermute(mine, 'freq', shifted_pairs(step))  16.8 us
    all_to_all x1, starting transfers between devices, per_device(): lax.all_to_all(blocks, 'space', split_axis=0, concat_axis=0, tiled=True)  13 us
    ppermute x3, starting transfers between devices, per_device(): total = total + lax.ppermute(quarters[step], 'freq', shifted_pairs(step))  10.8 us
    pallas_call x6, Pallas kernels, call(): pl.pallas_call(kernel, out_shape=out_shape, in_specs=[whole(pltpu.SMEM)]...  9.57 us
    ppermute x1, starting transfers between devices, per_device(): lax.ppermute(edges[0], 'space', [(i + 1, i) for i in range(count - 1)])  8.4 us
    ppermute x6, starting transfers between devices, gathered(): lax.ppermute(mine, 'freq', shifted_pairs(step))  8.36 us
    ppermute x3, waiting for transfers between devices, per_device(): total = total + lax.ppermute(quarters[step], 'freq', shifted_pairs(step))  6.8 us
  transfers between devices with their start and end apart: 15, of which 9 were waited for; matrix products, arithmetic and copies ran while one was open for 7% of the time, Pallas kernels for 1%

commit v1 on v0

--- a/solution.py
+++ b/solution.py
@@ -8,6 +8,7 @@
 from jax.experimental import pallas as pl
 from jax.experimental.pallas import tpu as pltpu
 from jax.sharding import PartitionSpec as P
+
 
 DZ = 4
 INTERPRET = False
@@ -136,9 +137,21 @@
     return lax.dot_general(left, right, (contract, ((), ())), preferred_element_type=jnp.float32)
 
 
-def forward_y_kernel(wave_ref, matrix_ref, twiddle_ref, out_ref, mid_ref):
+def fetch(sources, targets, sems):
+    copies = [pltpu.make_async_copy(s, t, sems.at[i]) for i, (s, t) in enumerate(zip(sources, targets))]
+    for copy in copies:
+        copy.start()
+    return copies
+
+
+def forward_y_kernel(wave_hbm, matrix_hbm, twiddle_hbm, out_ref, wave_ref, matrix_ref, twiddle_ref, mid_ref, sems):
+    parts = [(field, slice(8 * tile, 8 * tile + 8)) for field in range(2) for tile in range(4)]
+    views = [[ref.at[field, 0, :, rows, :] for field, rows in parts] for ref in (wave_hbm, wave_ref)]
+    waits = fetch([twiddle_hbm] + views[0] + [matrix_hbm], [twiddle_ref] + views[1] + [matrix_ref], sems)
+    waits[0].wait()
     for field in range(2):
         for tile in range(4):
+            waits[1 + 4 * field + tile].wait()
             rows = slice(8 * tile, 8 * tile + 8)
             values = [
                 tuple(wave_ref[field, 0, c, rows, 128 * a : 128 * a + 128] for c in range(2))
@@ -151,6 +164,7 @@
                 at = k1 * 64 + field * 32 + tile * 8
                 mid_ref[at : at + 8, 0:128] = real
                 mid_ref[at : at + 8, 128:256] = imag
+    waits[9].wait()
     matrix = matrix_ref[...]
     for pair in range(4):
         packed = spread(mid_ref[256 * pair : 256 * pair + 256, :])
@@ -174,8 +188,26 @@
 
 
 def middle_kernel(
-    in_ref, shift_ref, mask_ref, forward_ref, inverse_ref, twiddle_ref, out_ref, mid_ref, back_ref, hold_ref
+    refs_ref,
+    in_ref,
+    shift_ref,
+    forward_hbm,
+    inverse_hbm,
+    twiddle_hbm,
+    out_ref,
+    forward_ref,
+    inverse_ref,
+    twiddle_ref,
+    mid_ref,
+    back_ref,
+    hold_ref,
+    sems,
 ):
+    waits = fetch(
+        [twiddle_hbm, forward_hbm, inverse_hbm], [twiddle_ref, forward_ref, inverse_ref], sems
+    )
+    waits[0].wait()
+    early = lax.broadcasted_iota(jnp.int32, (8, 128), 1) % 32 < 16
     for tile in range(2):
         sub = 8 * tile
 
@@ -190,6 +222,8 @@
             mid_ref[at : at + 8, 128:256] = real * ti + imag * tr
 
         column_transform(load, store, -1, hold_ref.at[0])
+    waits[1].wait()
+    waits[2].wait()
     forward, inverse = forward_ref[...], inverse_ref[...]
     for part in range(4):
         rows = slice(256 * part, 256 * part + 256)
@@ -218,7 +252,7 @@
             else:
 
                 def store(s, value, sub=sub):
-                    chosen = mask_ref[s : s + 1, :] > 0.5
+                    chosen = jnp.where(early, refs_ref[0, 2 * s], refs_ref[0, 2 * s + 1]) > 0
                     out_ref[s, sub : sub + 8, :] = jnp.where(chosen, value[0], out_ref[s, sub : sub + 8, :])
                     out_ref[s, 16 + sub : 24 + sub, :] = jnp.where(
                         chosen, value[1], out_ref[s, 16 + sub : 24 + sub, :]
@@ -315,11 +349,13 @@
     return jax.ShapeDtypeStruct(shape, jnp.float32)
 
 
-def call(kernel, out_shape, operands, scratch=(), smem=0, near=(), near_out=False):
+def call(kernel, out_shape, operands, scratch=(), smem=0, far=0, near=(), near_out=False):
     many = isinstance(out_shape, (tuple, list))
     if not INTERPRET:
         operands = tuple(
-            pltpu.with_memory_space_constraint(x, pltpu.VMEM) if i in near else x
+            pltpu.with_memory_space_constraint(x, pltpu.VMEM)
+            if i in near
+            else pltpu.with_memory_space_constraint(x, pltpu.HBM) if i >= len(operands) - far else x
             for i, x in enumerate(operands)
         )
         if near_out:
@@ -329,7 +365,9 @@
     return pl.pallas_call(
         kernel,
         out_shape=out_shape,
-        in_specs=[whole(pltpu.SMEM)] * smem + [whole()] * (len(operands) - smem),
+        in_specs=[whole(pltpu.SMEM)] * smem
+        + [whole()] * (len(operands) - smem - far)
+        + [whole(pl.ANY if INTERPRET else pltpu.HBM)] * far,
         out_specs=[whole()] * len(out_shape) if many else whole(),
         scratch_shapes=list(scratch),
         interpret=INTERPRET,
@@ -343,30 +381,43 @@
         forward_y_kernel,
         f32(64, 32, 128),
         (wavefields, jnp.asarray(const["y_forward"]), jnp.asarray(const["y_twiddle"])),
-        (pltpu.VMEM((1024, 256), jnp.float32),),
+        (
+            pltpu.VMEM((2, 1, 2, 32, 2048), jnp.float32),
+            pltpu.VMEM((256, 768), BF16),
+            pltpu.VMEM((2, 16, 128), jnp.float32),
+            pltpu.VMEM((1024, 256), jnp.float32),
+            pltpu.SemaphoreType.DMA((10,)),
+        ),
+        far=3,
         near_out=True,
     )
 
 
-def middle(blocks, shift, mask):
+def middle(blocks, shift, ref_index):
     const = constants()
     return call(
         middle_kernel,
         f32(64, 32, 128),
         (
+            ref_index,
             blocks,
             shift,
-            mask,
             jnp.asarray(const["x_forward"]),
             jnp.asarray(const["x_inverse"]),
             jnp.asarray(const["x_twiddle"]),
         ),
         (
+            pltpu.VMEM((768, 256), BF16),
+            pltpu.VMEM((768, 256), BF16),
+            pltpu.VMEM((2, 64, 128), jnp.float32),
             pltpu.VMEM((1024, 256), jnp.float32),
             pltpu.VMEM((2, 1024, 256), jnp.float32),
             pltpu.VMEM((2, 2, 64, 8, 128), jnp.float32),
+            pltpu.SemaphoreType.DMA((3,)),
         ),
-        near=(0, 1, 2),
+        smem=1,
+        far=3,
+        near=(1, 2),
         near_out=True,
     )
 
@@ -421,10 +472,6 @@
     return jnp.stack(tables)
 
 
-def mask_table(ref_index):
-    return jnp.tile(jnp.repeat(ref_index.reshape(64, 2), 16, axis=1), (1, 4)).astype(jnp.float32)
-
-
 def phase_tables(speed, ref_rows, omega):
     time_shift = omega * DZ * (1.0 / speed - 1.0 / ref_rows)
     return jnp.stack([jnp.cos(time_shift), jnp.sin(time_shift)])
@@ -450,26 +497,32 @@
 
 
 def gathered(mine):
-    return [mine] + [lax.ppermute(mine, "freq", shifted_pairs(step)) for step in (1, 2, 3)]
-
-
-def per_device(wavefields, frequencies, velocity, slab_owner, ref_velocity, ref_index):
+    pieces = [mine]
+    for step in (1, 2, 3):
+        pieces.append(lax.ppermute(mine, "freq", shifted_pairs(step)))
+    return pieces
+
+
+def exchange(blocks):
+    return lax.all_to_all(blocks, "space", split_axis=0, concat_axis=0, tiled=True)
+
+
+def step_down(wavefields, frequencies, velocity, slab_owner, ref_velocity, ref_index):
     space_index = lax.axis_index("space")
     freq_index = lax.axis_index("freq")
     place = freq_index.reshape(1).astype(jnp.int32)
     omega = frequencies[0]
+    slab = slab_speed(velocity, slab_owner[0], freq_index)
     blocks = forward_y(wavefields)
-    blocks = lax.all_to_all(blocks, "space", split_axis=0, concat_axis=0, tiled=True)
+    blocks = exchange(blocks)
     shift = shift_tables(space_index, omega, ref_velocity[0])
-    speed = assemble(place, slab_speed(velocity, slab_owner[0], freq_index))[0]
+    speed = assemble(place, slab)[0]
     local_refs = lax.dynamic_slice_in_dim(ref_index[0], 2 * space_index, 2)
     ref_rows = jnp.repeat(ref_velocity[0][local_refs], 16)[:, None]
     phase = phase_tables(speed, ref_rows, omega)
     coupling = coupling_table(speed, ref_rows, omega)
-    mask = mask_table(ref_index[0])
-    blocks, shift, mask, phase, coupling = lax.optimization_barrier((blocks, shift, mask, phase, coupling))
-    blocks = middle(blocks, shift, mask)
-    blocks = lax.all_to_all(blocks, "space", split_axis=0, concat_axis=0, tiled=True)
+    blocks = middle(blocks, shift, ref_index)
+    blocks = exchange(blocks)
     wave, edges = inverse_y(blocks, phase)
     count = 64
     above = lax.ppermute(edges[1], "space", [(i, i + 1) for i in range(count - 1)])
@@ -493,5 +546,5 @@
     )
     out_specs = (P(None, "freq", None, "space", None), P(None, "space", None))
     return jax.shard_map(
-        per_device, mesh=mesh, in_specs=in_specs, out_specs=out_specs, check_vma=False
-    )
+        step_down, mesh=mesh, in_specs=in_specs, out_specs=out_specs, check_vma=False
+    )

time: 145 us -> 133 us (0.917); the launches traced: 144 us -> 131 us
  blocking collectives: 37.4 us -> 0 us
  waiting for transfers between devices: 25.2 us -> 50.4 us
  local copies, waits for them, and re-layouts: 9.81 us -> 2.5 us
  starting transfers between devices: 49.9 us -> 55.9 us
  Pallas kernels: 9.57 us -> 12 us
  other arithmetic: 8.59 us -> 6.29 us
    all_to_all x1 -> x0, blocking collectives: 37.4 us -> none  [per_device(): lax.all_to_all(blocks, 'space', split_axis=0, concat_axis=0, tiled=True)]
    ppermute x3, waiting for transfers between devices: 0.01 us -> 18.5 us  [slab_speed(): arrived = lax.ppermute(piece, 'freq', shifted_pairs(step))]
    all_to_all x1 -> x2, waiting for transfers between devices: 0.01 us -> 14.7 us  [exchange(): lax.all_to_all(blocks, 'space', split_axis=0, concat_axis=0, tiled=True)]
    ppermute x11, starting transfers between devices: 31.6 us -> 22.9 us  [the longest x1 10.6 us: step_down(): lax.ppermute(edges[0], 'space', [(i + 1, i) for i in range(count - 1)])]
    all_to_all x1 -> x2, starting transfers between devices: 13 us -> 21.7 us  [exchange(): lax.all_to_all(blocks, 'space', split_axis=0, concat_axis=0, tiled=True)]
    ppermute x11, waiting for transfers between devices: 25.2 us -> 17.2 us  [the longest x3 7.9 us: step_down(): total = total + lax.ppermute(quarters[step], 'freq', shifted_pairs(step))]
    ppermute x3, starting transfers between devices: 5.3 us -> 11.3 us  [slab_speed(): arrived = lax.ppermute(piece, 'freq', shifted_pairs(step))]
    unnamed x26 -> x12, local copies, waits for them, and re-layouts: 6.01 us -> 1 us
  transfers between devices with their start and end apart: 15 -> 16, of which waited for: 9 -> 11; matrix products, arithmetic and copies ran while one was open for 7% -> 6% of each run, Pallas kernels for 1% -> 0%
where the time goes in v1:
time: 133 us; the launch traced here: 131 us
  starting transfers between devices  55.9 us (42%)
  waiting for transfers between devices  50.4 us (38%)
  Pallas kernels  12 us (9%)
  other arithmetic  6.29 us (5%)
  between operations  3.78 us (3%)
  local copies, waits for them, and re-layouts  2.5 us (2%)
    all_to_all x2, starting transfers between devices, exchange(): lax.all_to_all(blocks, 'space', split_axis=0, concat_axis=0, tiled=True)  21.7 us
    ppermute x3, waiting for transfers between devices, slab_speed(): arrived = lax.ppermute(piece, 'freq', shifted_pairs(step))  18.5 us
    all_to_all x2, waiting for transfers between devices, exchange(): lax.all_to_all(blocks, 'space', split_axis=0, concat_axis=0, tiled=True)  14.7 us
    pallas_call x6, Pallas kernels, call(): pl.pallas_call(kernel, out_shape=out_shape, in_specs=[whole(pltpu.SMEM)]...  12 us
    ppermute x3, starting transfers between devices, slab_speed(): arrived = lax.ppermute(piece, 'freq', shifted_pairs(step))  11.3 us
    ppermute x1, starting transfers between devices, step_down(): lax.ppermute(edges[0], 'space', [(i + 1, i) for i in range(count - 1)])  10.6 us
    ppermute x3, waiting for transfers between devices, step_down(): total = total + lax.ppermute(quarters[step], 'freq', shifted_pairs(step))  7.9 us
    ppermute x6, starting transfers between devices, gathered(): pieces.append(lax.ppermute(mine, 'freq', shifted_pairs(step)))  7.79 us
  transfers between devices with their start and end apart: 16, of which 11 were waited for; matrix products, arithmetic and copies ran while one was open for 6% of the time, Pallas kernels for 0%

profile of v1, /device:TPU:2, one launch (start us, length us, event | category | flops | bytes accessed | tf_op | source)
XLA Modules:
  0.0 130.8 jit_solution(5576593336792247883)
XLA Ops:
  0.6 0.0 copy-start
  0.6 0.0 copy-start.5
  0.7 3.2 %shard_map.131 = f32[64,32,128]{2,1,0:T(8,128)} custom-call(f32[2,1,2,32,2048]{4,3,2,1,0:T(8,128)} %wave_hbm.1, bf16[256,768]{1,0:T(8,128)(2,1)} %constant.218.clone.matrix_hbm, f32[2,16,128]{2,1,0:T(8,128)} %constant.219.clone.twiddle_hbm.twiddle_ref), custom_call_target="tpu_custom_call" | custom-call | tf_op jit(solution)/shard_map/pallas_call | solution.py:365
  3.8 14.8 %all-to-all-start = ((f32[64,32,128]{2,1,0:T(8,128)}), f32[64,32,128]{2,1,0:T(8,128)}, u32[]{:S(2)}, u32[]{:S(2)}) async-start(f32[64,32,128]{2,1,0:T(8,128)} %shard_map.131), calls=%async_computation | async-start | bytes 2097152 | tf_op jit(solution)/shard_map/all_to_all | solution.py:507
  20.1 0.0 copy-done.5
  20.1 0.6 fusion.25
  22.3 4.7 %exponential_select_fusion.1 = (f32[1,1024,128]{2,1,0:T(8,128)S(1)}, f32[1,1024,128]{2,1,0:T(8,128)S(1)}, f32[1,1024,128]{2,1,0:T(8,128)S(1)}, f32[1,1024,128]{2,1,0:T(8,128)S(1)}) fusion(f32[]{:T(128)S(6)} %integer_pow.50, s32[1024]{0:T(1024)S(1)} %get-tuple-element.36, s32[1024]{0:T(1024)S(1)} %get-tuple-element.37, ...), kind=kLoop, calls=%fused_computation.25 | loop fusion | flops 6946816 | bytes 2119056 | tf_op jit(solution)/shard_map/jit(_where)/select_n | solution.py:470
  27.0 0.0 copy-start.4
  27.0 0.1 pad_maximum_fusion.shift_ref
  27.2 14.7 %all-to-all-done.in_ref = f32[64,32,128]{2,1,0:T(8,128)} async-done(((f32[64,32,128]{2,1,0:T(8,128)}), f32[64,32,128]{2,1,0:T(8,128)}, u32[]{:S(2)}, u32[]{:S(2)}) %all-to-all-start) | async-done | bytes 1048608 | tf_op jit(solution)/shard_map/all_to_all | solution.py:507
  41.8 0.0 copy-done.4
  41.8 5.5 %shard_map.132 = f32[64,32,128]{2,1,0:T(8,128)S(1)} custom-call(s32[1,128]{1,0:T(1,128)S(1)} %copy-done.4, f32[64,32,128]{2,1,0:T(8,128)} %all-to-all-done.in_ref, f32[4,1024,128]{2,1,0:T(8,128)S(1)} %pad_maximum_fusion.shift_ref, bf16[768,256]{1,0:T(8,128)(2,1)} %constant.220.clone.forward_hbm, bf16[768,256]{1,0:T(8,128)(2,1)} %constant.221.clone.inverse_hbm, ...), custom_call_target="tpu_custom_call" | custom-call | tf_op jit(solution)/shard_map/pallas_call | solution.py:365
  47.3 0.0 copy-start.1
  47.3 1.0 copy-done.1
  48.3 6.8 %all-to-all-start.1 = ((f32[64,32,128]{2,1,0:T(8,128)}), f32[64,32,128]{2,1,0:T(8,128)S(1)}, u32[]{:S(2)}, u32[]{:S(2)}) async-start(f32[64,32,128]{2,1,0:T(8,128)} %copy-done.1), calls=%async_computation.1 | async-start | bytes 2097152 | tf_op jit(solution)/shard_map/all_to_all | solution.py:507
  55.1 0.0 copy-done
  55.1 0.0 copy-start.2
  55.1 0.0 copy-start.3
  55.2 2.0 %collective-permute-start = (f32[8,2048]{1,0:T(8,128)S(1)}, f32[8,2048]{1,0:T(8,128)S(1)}, u32[]{:S(2)}, u32[]{:S(2)}) collective-permute-start(f32[8,2048]{1,0:T(8,128)S(1)} %get-tuple-element.20), channel_id=1, source_target_pairs={{0,192},{64,0},{128,64},{192,128},{1,193},{65,1},{129,65},{193,129... | collective-permute-start | bytes 196616 | tf_op jit(solution)/shard_map/ppermute | solution.py:494
  57.2 8.3 %collective-permute-start.1 = (f32[8,2048]{1,0:T(8,128)S(1)}, f32[8,2048]{1,0:T(8,128)S(1)}, u32[]{:S(2)}, u32[]{:S(2)}) collective-permute-start(f32[8,2048]{1,0:T(8,128)S(1)} %get-tuple-element.19), channel_id=1, source_target_pairs={{0,128},{64,192},{128,0},{192,64},{1,129},{65,193},{129,1},{193,65... | collective-permute-start | bytes 196616 | tf_op jit(solution)/shard_map/ppermute | solution.py:494
  65.5 1.0 collective-permute-start.2
  66.5 0.1 fusion.24
  66.6 0.6 gather_fusion
  67.2 0.1 broadcast_in_dim.17
  67.3 0.1 broadcast_in_dim_reshape.3
  67.4 16.4 %collective-permute-done = f32[8,2048]{1,0:T(8,128)S(1)} collective-permute-done((f32[8,2048]{1,0:T(8,128)S(1)}, f32[8,2048]{1,0:T(8,128)S(1)}, u32[]{:S(2)}, u32[]{:S(2)}) %collective-permute-start) | collective-permute-done | bytes 65568 | tf_op jit(solution)/shard_map/ppermute | solution.py:494
  83.8 2.1 %collective-permute-done.1 = f32[8,2048]{1,0:T(8,128)S(1)} collective-permute-done((f32[8,2048]{1,0:T(8,128)S(1)}, f32[8,2048]{1,0:T(8,128)S(1)}, u32[]{:S(2)}, u32[]{:S(2)}) %collective-permute-start.1) | collective-permute-done | bytes 65568 | tf_op jit(solution)/shard_map/ppermute | solution.py:494
  85.9 0.0 collective-permute-done.2
  85.9 0.1 collective-permute-start.3
  86.0 1.1 collective-permute-start.4
  87.1 2.7 %collective-permute-start.5 = (f32[8,2048]{1,0:T(8,128)S(1)}, f32[8,2048]{1,0:T(8,128)S(1)}, u32[]{:S(2)}, u32[]{:S(2)}) collective-permute-start(f32[8,2048]{1,0:T(8,128)S(1)} %fusion.14.own_ref), channel_id=1, source_target_pairs={{0,192},{64,0},{128,64},{192,128},{1,193},{65,1},{129,65},{193,129... | collective-permute-start | bytes 196616 | tf_op jit(solution)/shard_map/ppermute | solution.py:502
  89.8 3.0 %collective-permute-done.3.rest_0_ = f32[8,2048]{1,0:T(8,128)S(1)} collective-permute-done((f32[8,2048]{1,0:T(8,128)S(1)}, f32[8,2048]{1,0:T(8,128)S(1)}, u32[]{:S(2)}, u32[]{:S(2)}) %collective-permute-start.3) | collective-permute-done | bytes 65568 | tf_op jit(solution)/shard_map/ppermute | solution.py:502
  92.8 1.7 %collective-permute-done.4.rest_1_ = f32[8,2048]{1,0:T(8,128)S(1)} collective-permute-done((f32[8,2048]{1,0:T(8,128)S(1)}, f32[8,2048]{1,0:T(8,128)S(1)}, u32[]{:S(2)}, u32[]{:S(2)}) %collective-permute-start.4) | collective-permute-done | bytes 65568 | tf_op jit(solution)/shard_map/ppermute | solution.py:502
  94.5 0.0 collective-permute-done.5.rest_2_
  94.6 1.1 fusion.16
  95.8 0.0 all-to-all-done.1.in_ref
  95.8 0.0 copy-done.2
  95.8 0.0 copy-done.3
  95.8 1.0 shard_map.134
  96.8 1.9 %collective-permute-start.6 = (f32[4,2048]{1,0:T(4,128)S(1)}, f32[4,2048]{1,0:T(4,128)S(1)}, u32[]{:S(2)}, u32[]{:S(2)}) collective-permute-start(f32[4,2048]{1,0:T(4,128)S(1)} %get-tuple-element.22), channel_id=1, source_target_pairs={{0,1},{1,2},{2,3},{3,4},{4,5},{5,6},{6,7},{7,8},{8,9},{9,10},{10,1... | collective-permute-start | bytes 98312 | tf_op jit(solution)/shard_map/ppermute | solution.py:528
  98.7 10.6 %collective-permute-start.7 = (f32[4,2048]{1,0:T(4,128)S(1)}, f32[4,2048]{1,0:T(4,128)S(1)}, u32[]{:S(2)}, u32[]{:S(2)}) collective-permute-start(f32[4,2048]{1,0:T(4,128)S(1)} %get-tuple-element.21), channel_id=1, source_target_pairs={{1,0},{2,1},{3,2},{4,3},{5,4},{6,5},{7,6},{8,7},{9,8},{10,9},{11,1... | collective-permute-start | bytes 98312 | tf_op jit(solution)/shard_map/ppermute | solution.py:529
  109.3 0.1 fusion.12.coupling_ref
  109.4 0.0 collective-permute-done.6.above_ref
  109.4 1.6 %collective-permute-done.7.below_ref = f32[4,2048]{1,0:T(4,128)S(1)} collective-permute-done((f32[4,2048]{1,0:T(4,128)S(1)}, f32[4,2048]{1,0:T(4,128)S(1)}, u32[]{:S(2)}, u32[]{:S(2)}) %collective-permute-start.7) | collective-permute-done | bytes 32800 | tf_op jit(solution)/shard_map/ppermute | solution.py:529
  111.0 1.6 %shard_map.135 = (f32[2,1,2,32,2048]{4,3,2,1,0:T(8,128)}, f32[8,2048]{1,0:T(8,128)S(1)}, f32[8,2048]{1,0:T(8,128)S(1)}, f32[8,2048]{1,0:T(8,128)S(1)}, f32[8,2048]{1,0:T(8,128)S(1)}) custom-call(s32[1]{0:T(128)} %bitcast.place_ref, f32[2,2,32,2048]{3,2,1,0:T(8,128)S(1)} %get-tuple-element.9.wave_ref, f32[4,2048]{1,0:T(4,128)S(1)} %collective-permute-done.6.above_ref, ...), custom_call_target="tpu_custom_call" | custom-call | tf_op jit(solution)/shard_map/pallas_call | solution.py:365
  112.7 1.6 %collective-permute-start.10 = (f32[8,2048]{1,0:T(8,128)S(1)}, f32[8,2048]{1,0:T(8,128)S(1)}, u32[]{:S(2)}, u32[]{:S(2)}) collective-permute-start(f32[8,2048]{1,0:T(8,128)S(1)} %get-tuple-element.15), channel_id=1, source_target_pairs={{0,192},{64,0},{128,64},{192,128},{1,193},{65,1},{129,65},{193,129... | collective-permute-start | bytes 196616 | tf_op jit(solution)/shard_map/ppermute | solution.py:533
  114.3 0.4 collective-permute-start.8
  114.7 0.6 collective-permute-start.9
  115.3 1.6 %collective-permute-done.10 = f32[8,2048]{1,0:T(8,128)S(1)} collective-permute-done((f32[8,2048]{1,0:T(8,128)S(1)}, f32[8,2048]{1,0:T(8,128)S(1)}, u32[]{:S(2)}, u32[]{:S(2)}) %collective-permute-start.10) | collective-permute-done | bytes 65568 | tf_op jit(solution)/shard_map/ppermute | solution.py:533
  116.9 4.2 %collective-permute-done.8 = f32[8,2048]{1,0:T(8,128)S(1)} collective-permute-done((f32[8,2048]{1,0:T(8,128)S(1)}, f32[8,2048]{1,0:T(8,128)S(1)}, u32[]{:S(2)}, u32[]{:S(2)}) %collective-permute-start.8) | collective-permute-done | bytes 65568 | tf_op jit(solution)/shard_map/ppermute | solution.py:533
  121.2 2.1 %collective-permute-done.9 = f32[8,2048]{1,0:T(8,128)S(1)} collective-permute-done((f32[8,2048]{1,0:T(8,128)S(1)}, f32[8,2048]{1,0:T(8,128)S(1)}, u32[]{:S(2)}, u32[]{:S(2)}) %collective-permute-start.9) | collective-permute-done | bytes 65568 | tf_op jit(solution)/shard_map/ppermute | solution.py:533
  123.2 0.1 collective-permute-start.11
  123.3 2.5 %collective-permute-start.12 = (f32[8,2048]{1,0:T(8,128)S(1)}, f32[8,2048]{1,0:T(8,128)S(1)}, u32[]{:S(2)}, u32[]{:S(2)}) collective-permute-start(f32[8,2048]{1,0:T(8,128)S(1)} %add_add_fusion.own_ref), channel_id=1, source_target_pairs={{0,128},{64,192},{128,0},{192,64},{1,129},{65,193},{129,1},{193,65... | collective-permute-start | bytes 196616 | tf_op jit(solution)/shard_map/ppermute | solution.py:502
  125.8 1.3 %collective-permute-start.13 = (f32[8,2048]{1,0:T(8,128)S(1)}, f32[8,2048]{1,0:T(8,128)S(1)}, u32[]{:S(2)}, u32[]{:S(2)}) collective-permute-start(f32[8,2048]{1,0:T(8,128)S(1)} %add_add_fusion.own_ref), channel_id=1, source_target_pairs={{0,192},{64,0},{128,64},{192,128},{1,193},{65,1},{129,65},{193,129... | collective-permute-start | bytes 196616 | tf_op jit(solution)/shard_map/ppermute | solution.py:502
  127.1 2.2 %collective-permute-done.11.rest_0_ = f32[8,2048]{1,0:T(8,128)S(1)} collective-permute-done((f32[8,2048]{1,0:T(8,128)S(1)}, f32[8,2048]{1,0:T(8,128)S(1)}, u32[]{:S(2)}, u32[]{:S(2)}) %collective-permute-start.11) | collective-permute-done | bytes 65568 | tf_op jit(solution)/shard_map/ppermute | solution.py:502
  129.4 0.0 collective-permute-done.12.rest_1_
  129.4 0.7 collective-permute-done.13.rest_2_
  130.1 0.7 shard_map.136
  (17 shorter events, 0.2 us)
Async XLA Ops:
  0.6 54.5 %copy-start = (f32[4,32,2048]{2,1,0:T(8,128)S(1)}, f32[4,32,2048]{2,1,0:T(8,128)}, u32[]{:S(2)}) copy-start(f32[4,32,2048]{2,1,0:T(8,128)} %param.14) | copy-start | bytes 3145732
  0.6 19.4 %copy-start.5 = (f32[1,2]{1,0:T(1,128)S(1)}, f32[1,2]{1,0:T(1,128)}, u32[]{:S(2)}) copy-start(f32[1,2]{1,0:T(1,128)} %param.16) | copy-start | bytes 28
  3.8 38.0 %all-to-all-start = ((f32[64,32,128]{2,1,0:T(8,128)}), f32[64,32,128]{2,1,0:T(8,128)}, u32[]{:S(2)}, u32[]{:S(2)}) async-start(f32[64,32,128]{2,1,0:T(8,128)} %shard_map.131), calls=%async_computation | async-start | bytes 2097152 | tf_op jit(solution)/shard_map/all_to_all | solution.py:507
  27.0 14.8 %copy-start.4 = (s32[1,128]{1,0:T(1,128)S(1)}, s32[1,128]{1,0:T(1,128)}, u32[]{:S(2)}) copy-start(s32[1,128]{1,0:T(1,128)} %refs_ref.1) | copy-start | bytes 1540
  47.3 1.0 copy-start.1
  48.3 47.5 %all-to-all-start.1 = ((f32[64,32,128]{2,1,0:T(8,128)}), f32[64,32,128]{2,1,0:T(8,128)S(1)}, u32[]{:S(2)}, u32[]{:S(2)}) async-start(f32[64,32,128]{2,1,0:T(8,128)} %copy-done.1), calls=%async_computation.1 | async-start | bytes 2097152 | tf_op jit(solution)/shard_map/all_to_all | solution.py:507
  55.1 40.6 %copy-start.2 = (bf16[768,256]{1,0:T(8,128)(2,1)S(1)}, bf16[768,256]{1,0:T(8,128)(2,1)}, u32[]{:S(2)}) copy-start(bf16[768,256]{1,0:T(8,128)(2,1)} %constant.223.clone.matrix_ref) | copy-start | bytes 1179652
  55.1 40.6 %copy-start.3 = (f32[2,16,128]{2,1,0:T(8,128)S(1)}, f32[2,16,128]{2,1,0:T(8,128)}, u32[]{:S(2)}) copy-start(f32[2,16,128]{2,1,0:T(8,128)} %constant.219.clone.twiddle_hbm.twiddle_ref) | copy-start | bytes 49156
  55.2 28.6 %collective-permute-start = (f32[8,2048]{1,0:T(8,128)S(1)}, f32[8,2048]{1,0:T(8,128)S(1)}, u32[]{:S(2)}, u32[]{:S(2)}) collective-permute-start(f32[8,2048]{1,0:T(8,128)S(1)} %get-tuple-element.20), channel_id=1, source_target_pairs={{0,192},{64,0},{128,64},{192,128},{1,193},{65,1},{129,65},{193,129... | collective-permute-start | bytes 196616 | tf_op jit(solution)/shard_map/ppermute | solution.py:494
  57.2 28.7 %collective-permute-start.1 = (f32[8,2048]{1,0:T(8,128)S(1)}, f32[8,2048]{1,0:T(8,128)S(1)}, u32[]{:S(2)}, u32[]{:S(2)}) collective-permute-start(f32[8,2048]{1,0:T(8,128)S(1)} %get-tuple-element.19), channel_id=1, source_target_pairs={{0,128},{64,192},{128,0},{192,64},{1,129},{65,193},{129,1},{193,65... | collective-permute-start | bytes 196616 | tf_op jit(solution)/shard_map/ppermute | solution.py:494
  65.5 20.4 %collective-permute-start.2 = (f32[8,2048]{1,0:T(8,128)S(1)}, f32[8,2048]{1,0:T(8,128)S(1)}, u32[]{:S(2)}, u32[]{:S(2)}) collective-permute-start(f32[8,2048]{1,0:T(8,128)S(1)} %get-tuple-element.18), channel_id=1, source_target_pairs={{0,64},{64,128},{128,192},{192,0},{1,65},{65,129},{129,193},{193,1... | collective-permute-start | bytes 196616 | tf_op jit(solution)/shard_map/ppermute | solution.py:494
  85.9 6.9 %collective-permute-start.3 = (f32[8,2048]{1,0:T(8,128)S(1)}, f32[8,2048]{1,0:T(8,128)S(1)}, u32[]{:S(2)}, u32[]{:S(2)}) collective-permute-start(f32[8,2048]{1,0:T(8,128)S(1)} %fusion.14.own_ref), channel_id=1, source_target_pairs={{0,64},{64,128},{128,192},{192,0},{1,65},{65,129},{129,193},{193,1... | collective-permute-start | bytes 196616 | tf_op jit(solution)/shard_map/ppermute | solution.py:502
  86.0 8.5 %collective-permute-start.4 = (f32[8,2048]{1,0:T(8,128)S(1)}, f32[8,2048]{1,0:T(8,128)S(1)}, u32[]{:S(2)}, u32[]{:S(2)}) collective-permute-start(f32[8,2048]{1,0:T(8,128)S(1)} %fusion.14.own_ref), channel_id=1, source_target_pairs={{0,128},{64,192},{128,0},{192,64},{1,129},{65,193},{129,1},{193,65... | collective-permute-start | bytes 196616 | tf_op jit(solution)/shard_map/ppermute | solution.py:502
  87.1 7.5 %collective-permute-start.5 = (f32[8,2048]{1,0:T(8,128)S(1)}, f32[8,2048]{1,0:T(8,128)S(1)}, u32[]{:S(2)}, u32[]{:S(2)}) collective-permute-start(f32[8,2048]{1,0:T(8,128)S(1)} %fusion.14.own_ref), channel_id=1, source_target_pairs={{0,192},{64,0},{128,64},{192,128},{1,193},{65,1},{129,65},{193,129... | collective-permute-start | bytes 196616 | tf_op jit(solution)/shard_map/ppermute | solution.py:502
  96.8 12.6 %collective-permute-start.6 = (f32[4,2048]{1,0:T(4,128)S(1)}, f32[4,2048]{1,0:T(4,128)S(1)}, u32[]{:S(2)}, u32[]{:S(2)}) collective-permute-start(f32[4,2048]{1,0:T(4,128)S(1)} %get-tuple-element.22), channel_id=1, source_target_pairs={{0,1},{1,2},{2,3},{3,4},{4,5},{5,6},{6,7},{7,8},{8,9},{9,10},{10,1... | collective-permute-start | bytes 98312 | tf_op jit(solution)/shard_map/ppermute | solution.py:528
  98.7 12.3 %collective-permute-start.7 = (f32[4,2048]{1,0:T(4,128)S(1)}, f32[4,2048]{1,0:T(4,128)S(1)}, u32[]{:S(2)}, u32[]{:S(2)}) collective-permute-start(f32[4,2048]{1,0:T(4,128)S(1)} %get-tuple-element.21), channel_id=1, source_target_pairs={{1,0},{2,1},{3,2},{4,3},{5,4},{6,5},{7,6},{8,7},{9,8},{10,9},{11,1... | collective-permute-start | bytes 98312 | tf_op jit(solution)/shard_map/ppermute | solution.py:529
  112.7 4.3 %collective-permute-start.10 = (f32[8,2048]{1,0:T(8,128)S(1)}, f32[8,2048]{1,0:T(8,128)S(1)}, u32[]{:S(2)}, u32[]{:S(2)}) collective-permute-start(f32[8,2048]{1,0:T(8,128)S(1)} %get-tuple-element.15), channel_id=1, source_target_pairs={{0,192},{64,0},{128,64},{192,128},{1,193},{65,1},{129,65},{193,129... | collective-permute-start | bytes 196616 | tf_op jit(solution)/shard_map/ppermute | solution.py:533
  114.3 6.9 %collective-permute-start.8 = (f32[8,2048]{1,0:T(8,128)S(1)}, f32[8,2048]{1,0:T(8,128)S(1)}, u32[]{:S(2)}, u32[]{:S(2)}) collective-permute-start(f32[8,2048]{1,0:T(8,128)S(1)} %get-tuple-element.13), channel_id=1, source_target_pairs={{0,64},{64,128},{128,192},{192,0},{1,65},{65,129},{129,193},{193,1... | collective-permute-start | bytes 196616 | tf_op jit(solution)/shard_map/ppermute | solution.py:533
  114.7 8.5 %collective-permute-start.9 = (f32[8,2048]{1,0:T(8,128)S(1)}, f32[8,2048]{1,0:T(8,128)S(1)}, u32[]{:S(2)}, u32[]{:S(2)}) collective-permute-start(f32[8,2048]{1,0:T(8,128)S(1)} %get-tuple-element.14), channel_id=1, source_target_pairs={{0,128},{64,192},{128,0},{192,64},{1,129},{65,193},{129,1},{193,65... | collective-permute-start | bytes 196616 | tf_op jit(solution)/shard_map/ppermute | solution.py:533
  123.2 6.1 %collective-permute-start.11 = (f32[8,2048]{1,0:T(8,128)S(1)}, f32[8,2048]{1,0:T(8,128)S(1)}, u32[]{:S(2)}, u32[]{:S(2)}) collective-permute-start(f32[8,2048]{1,0:T(8,128)S(1)} %add_add_fusion.own_ref), channel_id=1, source_target_pairs={{0,64},{64,128},{128,192},{192,0},{1,65},{65,129},{129,193},{193,1... | collective-permute-start | bytes 196616 | tf_op jit(solution)/shard_map/ppermute | solution.py:502
  123.3 6.1 %collective-permute-start.12 = (f32[8,2048]{1,0:T(8,128)S(1)}, f32[8,2048]{1,0:T(8,128)S(1)}, u32[]{:S(2)}, u32[]{:S(2)}) collective-permute-start(f32[8,2048]{1,0:T(8,128)S(1)} %add_add_fusion.own_ref), channel_id=1, source_target_pairs={{0,128},{64,192},{128,0},{192,64},{1,129},{65,193},{129,1},{193,65... | collective-permute-start | bytes 196616 | tf_op jit(solution)/shard_map/ppermute | solution.py:502
  125.8 4.3 %collective-permute-start.13 = (f32[8,2048]{1,0:T(8,128)S(1)}, f32[8,2048]{1,0:T(8,128)S(1)}, u32[]{:S(2)}, u32[]{:S(2)}) collective-permute-start(f32[8,2048]{1,0:T(8,128)S(1)} %add_add_fusion.own_ref), channel_id=1, source_target_pairs={{0,192},{64,0},{128,64},{192,128},{1,193},{65,1},{129,65},{193,129... | collective-permute-start | bytes 196616 | tf_op jit(solution)/shard_map/ppermute | solution.py:502

commit v2 on v1

--- a/solution.py
+++ b/solution.py
@@ -189,11 +189,13 @@
 
 def middle_kernel(
     refs_ref,
-    in_ref,
     shift_ref,
+    in_hbm,
     forward_hbm,
     inverse_hbm,
     twiddle_hbm,
+    out_hbm,
+    in_ref,
     out_ref,
     forward_ref,
     inverse_ref,
@@ -204,7 +206,9 @@
     sems,
 ):
     waits = fetch(
-        [twiddle_hbm, forward_hbm, inverse_hbm], [twiddle_ref, forward_ref, inverse_ref], sems
+        [twiddle_hbm] + [in_hbm.at[:, n] for n in range(8)] + [forward_hbm, inverse_hbm],
+        [twiddle_ref] + [in_ref.at[:, n] for n in range(8)] + [forward_ref, inverse_ref],
+        sems,
     )
     waits[0].wait()
     early = lax.broadcasted_iota(jnp.int32, (8, 128), 1) % 32 < 16
@@ -212,7 +216,9 @@
         sub = 8 * tile
 
         def load(s, sub=sub):
-            return in_ref[s, sub : sub + 8, :], in_ref[s, 16 + sub : 24 + sub, :]
+            if sub == 0 and s < 8:
+                waits[1 + s].wait()
+            return in_ref[s // 8, s % 8, sub : sub + 8, :], in_ref[s // 8, s % 8, 16 + sub : 24 + sub, :]
 
         def store(m1, value, sub=sub):
             real, imag = value
@@ -222,8 +228,8 @@
             mid_ref[at : at + 8, 128:256] = real * ti + imag * tr
 
         column_transform(load, store, -1, hold_ref.at[0])
-    waits[1].wait()
-    waits[2].wait()
+    waits[9].wait()
+    waits[10].wait()
     forward, inverse = forward_ref[...], inverse_ref[...]
     for part in range(4):
         rows = slice(256 * part, 256 * part + 256)
@@ -233,6 +239,7 @@
             cosine, sine = shift_ref[2 * ref, rows, :], shift_ref[2 * ref + 1, rows, :]
             turned = jnp.concatenate([real * cosine - imag * sine, real * sine + imag * cosine], axis=1)
             back_ref[ref, rows, :] = matmul(spread(turned), inverse, ((1,), (0,)))
+    leaving = []
     for tile in range(2):
         sub = 8 * tile
         for ref in range(2):
@@ -246,22 +253,30 @@
             if ref == 0:
 
                 def store(s, value, sub=sub):
-                    out_ref[s, sub : sub + 8, :] = value[0]
-                    out_ref[s, 16 + sub : 24 + sub, :] = value[1]
+                    out_ref[s // 8, s % 8, sub : sub + 8, :] = value[0]
+                    out_ref[s // 8, s % 8, 16 + sub : 24 + sub, :] = value[1]
 
             else:
 
                 def store(s, value, sub=sub):
                     chosen = jnp.where(early, refs_ref[0, 2 * s], refs_ref[0, 2 * s + 1]) > 0
-                    out_ref[s, sub : sub + 8, :] = jnp.where(chosen, value[0], out_ref[s, sub : sub + 8, :])
-                    out_ref[s, 16 + sub : 24 + sub, :] = jnp.where(
-                        chosen, value[1], out_ref[s, 16 + sub : 24 + sub, :]
-                    )
+                    for c in range(2):
+                        at = (s // 8, s % 8, slice(16 * c + sub, 16 * c + sub + 8))
+                        out_ref[at] = jnp.where(chosen, value[c], out_ref[at])
+                    if sub == 8 and s >= 56:
+                        copy = pltpu.make_async_copy(
+                            out_ref.at[:, s % 8], out_hbm.at[:, s % 8], sems.at[11 + s % 8]
+                        )
+                        copy.start()
+                        leaving.append(copy)
 
             column_transform(load, store, 1, hold_ref.at[ref])
-
-
-def inverse_y_kernel(in_ref, phase_ref, matrix_ref, twiddle_ref, out_ref, edge_ref, mid_ref):
+    for copy in leaving:
+        copy.wait()
+
+
+def inverse_y_kernel(place_ref, in_ref, phase_ref, coupling_ref, matrix_ref, twiddle_ref, out_ref, *rest):
+    first_ref, last_ref, image_refs, mid_ref, image_hold = rest[0], rest[1], rest[2:6], rest[6], rest[7]
     matrix = matrix_ref[...]
     for p in range(8):
         block = in_ref[8 * p : 8 * p + 8].reshape(256, 128)
@@ -288,13 +303,39 @@
                     out_ref[field, c, rows, lanes] = value
                     row = 2 * field + c
                     if tile == 0:
-                        edge_ref[0, row : row + 1, lanes] = value[0:1]
+                        first_ref[row : row + 1, lanes] = value[0:1]
                     if tile == 3:
-                        edge_ref[1, row : row + 1, lanes] = value[7:8]
-
-
-def laplace_kernel(place_ref, wave_ref, above_ref, below_ref, coupling_ref, out_ref, *rest):
-    image_refs, image_hold = rest[:4], rest[4]
+                        last_ref[row : row + 1, lanes] = value[7:8]
+    row = lax.broadcasted_iota(jnp.int32, (8, 2048), 0)
+    for tile, source, receiver in corrected(out_ref, None, None, coupling_ref):
+        image = source[0] * receiver[0] + source[1] * receiver[1]
+        if tile == 0:
+            image = jnp.where(row == 0, 0.0, image)
+        if tile == 3:
+            image = jnp.where(row == 7, 0.0, image)
+        image_hold[8 * tile : 8 * tile + 8, :] = image
+    place = place_ref[0]
+    for k in range(4):
+        at = pl.multiple_of(((place + k) % 4) * 8, 8)
+        image_refs[k][...] = image_hold[pl.ds(at, 8), :]
+
+
+def laplace_kernel(wave_ref, above_ref, below_ref, coupling_ref, out_ref, edge_ref):
+    for tile, source, receiver in corrected(wave_ref, above_ref, below_ref, coupling_ref):
+        rows = slice(8 * tile, 8 * tile + 8)
+        for field, pair in enumerate((source, receiver)):
+            out_ref[field, 0, 0, rows, :] = pair[0]
+            out_ref[field, 0, 1, rows, :] = pair[1]
+        image = source[0] * receiver[0] + source[1] * receiver[1]
+        for part in range(4):
+            lanes = slice(512 * part, 512 * part + 512)
+            if tile == 0:
+                edge_ref[part : part + 1, :] = image[0:1, lanes]
+            if tile == 3:
+                edge_ref[4 + part : 5 + part, :] = image[7:8, lanes]
+
+
+def corrected(wave_ref, above_ref, below_ref, coupling_ref):
     row = lax.broadcasted_iota(jnp.int32, (8, 2048), 0)
     lane = lax.broadcasted_iota(jnp.int32, (8, 2048), 1)
     for tile in range(4):
@@ -306,14 +347,14 @@
             for c in range(2):
                 value = wave_ref[field, c, rows, :]
                 index = 2 * field + c
-                if tile == 0:
-                    before = above_ref[index : index + 1, :]
+                if tile > 0:
+                    before = wave_ref[field, c, 8 * tile - 1 : 8 * tile, :]
                 else:
-                    before = wave_ref[field, c, 8 * tile - 1 : 8 * tile, :]
-                if tile == 3:
-                    after = below_ref[index : index + 1, :]
+                    before = 0.0 if above_ref is None else above_ref[index : index + 1, :]
+                if tile < 3:
+                    after = wave_ref[field, c, 8 * tile + 8 : 8 * tile + 9, :]
                 else:
-                    after = wave_ref[field, c, 8 * tile + 8 : 8 * tile + 9, :]
+                    after = 0.0 if below_ref is None else below_ref[index : index + 1, :]
                 up = jnp.where(row == 0, before, pltpu.roll(value, 1, 0))
                 down = jnp.where(row == 7, after, pltpu.roll(value, 7, 0))
                 left = jnp.where(lane == 0, 0.0, pltpu.roll(value, 1, 1))
@@ -323,22 +364,23 @@
             scaled = coupling * sign
             real = wave_ref[field, 0, rows, :] - scaled * laplace[1]
             imag = wave_ref[field, 1, rows, :] + scaled * laplace[0]
-            out_ref[field, 0, 0, rows, :] = real
-            out_ref[field, 0, 1, rows, :] = imag
             results.append((real, imag))
-        image_hold[rows, :] = results[0][0] * results[1][0] + results[0][1] * results[1][1]
+        yield tile, results[0], results[1]
+
+
+def assemble_kernel(place_ref, own_ref, *rest):
+    refs, out_ref = (own_ref,) + rest[:3], rest[3]
     place = place_ref[0]
-    for k in range(4):
-        at = pl.multiple_of(((place + k) % 4) * 8, 8)
-        image_refs[k][...] = image_hold[pl.ds(at, 8), :]
-
-
-def assemble_kernel(place_ref, own_ref, *rest):
-    others, out_ref = rest[:3], rest[3]
-    place = place_ref[0]
-    for k, ref in enumerate((own_ref,) + tuple(others)):
+    for k, ref in enumerate(refs):
         at = pl.multiple_of(((place + 4 - k) % 4) * 8, 8)
-        out_ref[0, pl.ds(at, 8), :] = ref[...]
+        out_ref[0, pl.ds(at, 8), :] = ref[:, 0:2048]
+    if own_ref.shape[1] > 2048:
+        edges = [ref[:, 2048:2560] for ref in refs]
+        total = edges[0] + edges[1] + edges[2] + edges[3]
+        for part in range(4):
+            lanes = slice(512 * part, 512 * part + 512)
+            out_ref[0, 0:1, lanes] = total[part : part + 1]
+            out_ref[0, 31:32, lanes] = total[4 + part : 5 + part]
 
 
 def whole(memory=pltpu.VMEM):
@@ -349,7 +391,8 @@
     return jax.ShapeDtypeStruct(shape, jnp.float32)
 
 
-def call(kernel, out_shape, operands, scratch=(), smem=0, far=0, near=(), near_out=False):
+def call(kernel, out_shape, operands, scratch=(), smem=0, far=0, near=(), near_out=False, far_out=False):
+    hbm = whole(pl.ANY if INTERPRET else pltpu.HBM)
     many = isinstance(out_shape, (tuple, list))
     if not INTERPRET:
         operands = tuple(
@@ -362,13 +405,15 @@
             shapes = out_shape if many else (out_shape,)
             shapes = tuple(pltpu.VMEM(x.shape, x.dtype) for x in shapes)
             out_shape = shapes if many else shapes[0]
+        if far_out:
+            out_shape = pltpu.HBM(out_shape.shape, out_shape.dtype)
     return pl.pallas_call(
         kernel,
         out_shape=out_shape,
         in_specs=[whole(pltpu.SMEM)] * smem
         + [whole()] * (len(operands) - smem - far)
-        + [whole(pl.ANY if INTERPRET else pltpu.HBM)] * far,
-        out_specs=[whole()] * len(out_shape) if many else whole(),
+        + [hbm] * far,
+        out_specs=[whole()] * len(out_shape) if many else hbm if far_out else whole(),
         scratch_shapes=list(scratch),
         interpret=INTERPRET,
         compiler_params=pltpu.CompilerParams(vmem_limit_bytes=VMEM_BYTES),
@@ -395,52 +440,55 @@
 
 def middle(blocks, shift, ref_index):
     const = constants()
-    return call(
+    blocks = call(
         middle_kernel,
-        f32(64, 32, 128),
+        f32(8, 8, 32, 128),
         (
             ref_index,
-            blocks,
             shift,
+            blocks.reshape(8, 8, 32, 128),
             jnp.asarray(const["x_forward"]),
             jnp.asarray(const["x_inverse"]),
             jnp.asarray(const["x_twiddle"]),
         ),
         (
+            pltpu.VMEM((8, 8, 32, 128), jnp.float32),
+            pltpu.VMEM((8, 8, 32, 128), jnp.float32),
             pltpu.VMEM((768, 256), BF16),
             pltpu.VMEM((768, 256), BF16),
             pltpu.VMEM((2, 64, 128), jnp.float32),
             pltpu.VMEM((1024, 256), jnp.float32),
             pltpu.VMEM((2, 1024, 256), jnp.float32),
             pltpu.VMEM((2, 2, 64, 8, 128), jnp.float32),
-            pltpu.SemaphoreType.DMA((3,)),
+            pltpu.SemaphoreType.DMA((19,)),
         ),
         smem=1,
-        far=3,
-        near=(1, 2),
-        near_out=True,
-    )
-
-
-def inverse_y(blocks, phase):
+        far=4,
+        near=(1,),
+        far_out=True,
+    )
+    return blocks.reshape(64, 32, 128)
+
+
+def inverse_y(place, blocks, phase, coupling):
     const = constants()
     return call(
         inverse_y_kernel,
-        (f32(2, 2, 32, 2048), f32(2, 4, 2048)),
-        (blocks, phase, jnp.asarray(const["y_inverse"]), jnp.asarray(const["y_twiddle"])),
-        (pltpu.VMEM((1024, 256), jnp.float32),),
-        near=(0, 1),
+        (f32(2, 2, 32, 2048),) + (f32(4, 2048),) * 2 + (f32(8, 2048),) * 4,
+        (place, blocks, phase, coupling, jnp.asarray(const["y_inverse"]), jnp.asarray(const["y_twiddle"])),
+        (pltpu.VMEM((1024, 256), jnp.float32), pltpu.VMEM((32, 2048), jnp.float32)),
+        smem=1,
+        near=(1, 2, 3),
         near_out=True,
     )
 
 
-def laplace(place, wave, above, below, coupling):
+def laplace(wave, above, below, coupling):
     return call(
         laplace_kernel,
-        (f32(2, 1, 2, 32, 2048),) + (f32(8, 2048),) * 4,
-        (place, wave, above, below, coupling),
-        (pltpu.VMEM((32, 2048), jnp.float32),),
-        smem=1,
+        (f32(2, 1, 2, 32, 2048), f32(8, 512)),
+        (wave, above, below, coupling),
+        near=(0, 1, 2, 3),
     )
 
 
@@ -523,15 +571,16 @@
     coupling = coupling_table(speed, ref_rows, omega)
     blocks = middle(blocks, shift, ref_index)
     blocks = exchange(blocks)
-    wave, edges = inverse_y(blocks, phase)
+    wave, first, last, *quarters = inverse_y(place, blocks, phase, coupling)
     count = 64
-    above = lax.ppermute(edges[1], "space", [(i, i + 1) for i in range(count - 1)])
-    below = lax.ppermute(edges[0], "space", [(i + 1, i) for i in range(count - 1)])
-    fields, *quarters = laplace(place, wave, above, below, coupling)
+    above = lax.ppermute(last, "space", [(i, i + 1) for i in range(count - 1)])
+    below = lax.ppermute(first, "space", [(i + 1, i) for i in range(count - 1)])
     total = quarters[0]
     for step in (1, 2, 3):
-        total = total + lax.ppermute(quarters[step], "freq", shifted_pairs(step))
-    image = assemble(place, gathered(total))
+        arrived = lax.ppermute(quarters[step], "freq", shifted_pairs(step))
+        total = total + arrived
+    fields, edges = laplace(wave, above, below, coupling)
+    image = assemble(place, gathered(jnp.concatenate([total, edges], axis=1)))
     return fields, image
 
 
@@ -545,6 +594,4 @@
         P(),
     )
     out_specs = (P(None, "freq", None, "space", None), P(None, "space", None))
-    return jax.shard_map(
-        step_down, mesh=mesh, in_specs=in_specs, out_specs=out_specs, check_vma=False
-    )
+    return jax.shard_map(step_down, mesh=mesh, in_specs=in_specs, out_specs=out_specs, check_vma=False)

time: 133 us -> 124 us (0.932)
  waiting for transfers between devices: 50.4 us -> 32.2 us
  starting transfers between devices: 55.9 us -> 64 us
  Pallas kernels: 12 us -> 13.4 us
    ppermute x3, waiting for transfers between devices: 18.5 us -> 0.01 us  [slab_speed(): arrived = lax.ppermute(piece, 'freq', shifted_pairs(step))]
    ppermute x6, starting transfers between devices: 7.79 us -> 20.3 us  [gathered(): pieces.append(lax.ppermute(mine, 'freq', shifted_pairs(step)))]
    ppermute x6, waiting for transfers between devices: 7.65 us -> 19.9 us  [gathered(): pieces.append(lax.ppermute(mine, 'freq', shifted_pairs(step)))]
    ppermute x3, starting transfers between devices: 11.3 us -> 3.49 us  [slab_speed(): arrived = lax.ppermute(piece, 'freq', shifted_pairs(step))]
    ppermute x5, waiting for transfers between devices: 9.54 us -> 1.75 us  [the longest x1 1.74 us: step_down(): below = lax.ppermute(first, 'space', [(i + 1, i) for i in range(count - 1)])]
    ppermute x5, starting transfers between devices: 15.1 us -> 19.2 us  [the longest x1 10.6 us: step_down(): below = lax.ppermute(first, 'space', [(i + 1, i) for i in range(count - 1)])]
    all_to_all x2, waiting for transfers between devices: 14.7 us -> 10.6 us  [exchange(): lax.all_to_all(blocks, 'space', split_axis=0, concat_axis=0, tiled=True)]
    pallas_call x6, Pallas kernels: 12 us -> 13.4 us  [call(): pl.pallas_call(kernel, out_shape=out_shape, in_specs=[whole(pltpu.SMEM)]...]
  transfers between devices with their start and end apart: 16 -> 16, of which waited for: 11 -> 8; matrix products, arithmetic and copies ran while one was open for 6% -> 8% of each run, Pallas kernels for 0% -> 6%
where the time goes in v2:
time: 124 us; the launch traced here: 123 us
  starting transfers between devices  64 us (52%)
  waiting for transfers between devices  32.2 us (26%)
  Pallas kernels  13.4 us (11%)
  other arithmetic  7.17 us (6%)
  between operations  3.62 us (3%)
  local copies, waits for them, and re-layouts  2.18 us (2%)
    all_to_all x2, starting transfers between devices, exchange(): lax.all_to_all(blocks, 'space', split_axis=0, concat_axis=0, tiled=True)  21 us
    ppermute x6, starting transfers between devices, gathered(): pieces.append(lax.ppermute(mine, 'freq', shifted_pairs(step)))  20.3 us
    ppermute x6, waiting for transfers between devices, gathered(): pieces.append(lax.ppermute(mine, 'freq', shifted_pairs(step)))  19.9 us
    pallas_call x6, Pallas kernels, call(): pl.pallas_call(kernel, out_shape=out_shape, in_specs=[whole(pltpu.SMEM)]...  13.4 us
    all_to_all x2, waiting for transfers between devices, exchange(): lax.all_to_all(blocks, 'space', split_axis=0, concat_axis=0, tiled=True)  10.6 us
    ppermute x1, starting transfers between devices, step_down(): below = lax.ppermute(first, 'space', [(i + 1, i) for i in range(count - 1)])  10.6 us
    ppermute x3, starting transfers between devices, step_down(): arrived = lax.ppermute(quarters[step], 'freq', shifted_pairs(step))  6.76 us
    select_n x1, other arithmetic, shift_tables(): tables.append(jnp.where(travels, jnp.cos(root), jnp.exp(-root)))  4.72 us
  transfers between devices with their start and end apart: 16, of which 8 were waited for; matrix products, arithmetic and copies ran while one was open for 8% of the time, Pallas kernels for 6%

profile of v2, /device:TPU:2, one launch (start us, length us, event | category | flops | bytes accessed | tf_op | source)
XLA Modules:
  0.0 122.6 jit_solution(1458270176618652044)
XLA Ops:
  0.6 0.0 copy-start
  0.6 3.2 %shard_map.131 = f32[64,32,128]{2,1,0:T(8,128)} custom-call(f32[2,1,2,32,2048]{4,3,2,1,0:T(8,128)} %wave_hbm.1, bf16[256,768]{1,0:T(8,128)(2,1)} %constant.218.clone.matrix_hbm, f32[2,16,128]{2,1,0:T(8,128)} %constant.219.clone.twiddle_hbm.twiddle_ref), custom_call_target="tpu_custom_call" | custom-call | tf_op jit(solution)/shard_map/pallas_call | solution.py:410
  3.8 0.0 copy-start.4
  3.8 14.9 %all-to-all-start = ((f32[64,32,128]{2,1,0:T(8,128)}), f32[64,32,128]{2,1,0:T(8,128)}, u32[]{:S(2)}, u32[]{:S(2)}) async-start(f32[64,32,128]{2,1,0:T(8,128)} %shard_map.131), calls=%async_computation | async-start | bytes 2097152 | tf_op jit(solution)/shard_map/all_to_all | solution.py:555
  19.4 0.0 copy-done
  19.5 0.0 copy-start.5
  19.5 0.7 dynamic-slice_bitcast_fusion.1
  20.2 1.9 %collective-permute-start = (f32[8,2048]{1,0:T(8,128)}, f32[8,2048]{1,0:T(8,128)S(1)}, u32[]{:S(2)}, u32[]{:S(2)}) collective-permute-start(f32[8,2048]{1,0:T(8,128)} %get-tuple-element.24), channel_id=1, source_target_pairs={{0,192},{64,0},{128,64},{192,128},{1,193},{65,1},{129,65},{193,129... | collective-permute-start | bytes 196616 | tf_op jit(solution)/shard_map/ppermute | solution.py:542
  22.2 0.5 collective-permute-start.1
  22.7 1.0 collective-permute-start.2
  24.4 0.0 copy-done.4
  24.4 0.6 fusion.25
  26.4 4.7 %exponential_select_fusion.1 = (f32[1,1024,128]{2,1,0:T(8,128)S(1)}, f32[1,1024,128]{2,1,0:T(8,128)S(1)}, f32[1,1024,128]{2,1,0:T(8,128)S(1)}, f32[1,1024,128]{2,1,0:T(8,128)S(1)}) fusion(f32[]{:T(128)S(6)} %integer_pow.50, s32[1024]{0:T(1024)S(1)} %get-tuple-element.38, s32[1024]{0:T(1024)S(1)} %get-tuple-element.39, ...), kind=kLoop, calls=%fused_computation.25 | loop fusion | flops 6946816 | bytes 2119056 | tf_op jit(solution)/shard_map/jit(_where)/select_n | solution.py:518
  31.1 0.0 copy-done.5
  31.1 0.0 copy-start.3
  31.1 0.1 pad_maximum_fusion.shift_ref
  31.3 10.6 %all-to-all-done = f32[64,32,128]{2,1,0:T(8,128)} async-done(((f32[64,32,128]{2,1,0:T(8,128)}), f32[64,32,128]{2,1,0:T(8,128)}, u32[]{:S(2)}, u32[]{:S(2)}) %all-to-all-start) | async-done | bytes 1048608 | tf_op jit(solution)/shard_map/all_to_all | solution.py:555
  41.8 0.0 copy-done.3
  41.9 6.2 %shard_map.132 = f32[8,8,32,128]{3,2,1,0:T(8,128)} custom-call(s32[1,128]{1,0:T(1,128)S(1)} %copy-done.3, f32[4,1024,128]{2,1,0:T(8,128)S(1)} %pad_maximum_fusion.shift_ref, f32[8,8,32,128]{3,2,1,0:T(8,128)} %bitcast.4.in_hbm, bf16[768,256]{1,0:T(8,128)(2,1)} %constant.220.clone.forward_hbm, bf16[768,256]{1,0:T(8,128)(2,1)} %constant.221.clone.inverse_hbm, ...), custom_call_target="tpu_custom_call" | custom-call | tf_op jit(solution)/shard_map/pallas_call | solution.py:410
  48.0 6.1 %all-to-all-start.1 = ((f32[64,32,128]{2,1,0:T(8,128)}), f32[64,32,128]{2,1,0:T(8,128)S(1)}, u32[]{:S(2)}, u32[]{:S(2)}) async-start(f32[64,32,128]{2,1,0:T(8,128)} %bitcast.45), calls=%async_computation.1 | async-start | bytes 2097152 | tf_op jit(solution)/shard_map/all_to_all | solution.py:555
  54.2 0.0 copy-start.1
  54.2 0.0 copy-start.2
  54.2 0.1 fusion.24
  54.3 0.6 gather_fusion
  54.9 0.1 broadcast_in_dim.17
  55.0 0.1 broadcast_in_dim_reshape.3
  55.1 0.0 collective-permute-done
  55.1 0.0 collective-permute-done.1
  55.1 0.0 collective-permute-done.2
  55.1 0.9 fusion.14.own_ref
  55.9 10.6 %collective-permute-start.3 = (f32[8,2048]{1,0:T(8,128)S(1)}, f32[8,2048]{1,0:T(8,128)S(1)}, u32[]{:S(2)}, u32[]{:S(2)}) collective-permute-start(f32[8,2048]{1,0:T(8,128)S(1)} %fusion.14.own_ref), channel_id=1, source_target_pairs={{0,64},{64,128},{128,192},{192,0},{1,65},{65,129},{129,193},{193,1... | collective-permute-start | bytes 196616 | tf_op jit(solution)/shard_map/ppermute | solution.py:550
  66.6 2.4 %collective-permute-start.4 = (f32[8,2048]{1,0:T(8,128)S(1)}, f32[8,2048]{1,0:T(8,128)S(1)}, u32[]{:S(2)}, u32[]{:S(2)}) collective-permute-start(f32[8,2048]{1,0:T(8,128)S(1)} %fusion.14.own_ref), channel_id=1, source_target_pairs={{0,128},{64,192},{128,0},{192,64},{1,129},{65,193},{129,1},{193,65... | collective-permute-start | bytes 196616 | tf_op jit(solution)/shard_map/ppermute | solution.py:550
  68.9 2.8 %collective-permute-start.5 = (f32[8,2048]{1,0:T(8,128)S(1)}, f32[8,2048]{1,0:T(8,128)S(1)}, u32[]{:S(2)}, u32[]{:S(2)}) collective-permute-start(f32[8,2048]{1,0:T(8,128)S(1)} %fusion.14.own_ref), channel_id=1, source_target_pairs={{0,192},{64,0},{128,64},{192,128},{1,193},{65,1},{129,65},{193,129... | collective-permute-start | bytes 196616 | tf_op jit(solution)/shard_map/ppermute | solution.py:550
  71.8 2.2 %collective-permute-done.3.rest_0_ = f32[8,2048]{1,0:T(8,128)S(1)} collective-permute-done((f32[8,2048]{1,0:T(8,128)S(1)}, f32[8,2048]{1,0:T(8,128)S(1)}, u32[]{:S(2)}, u32[]{:S(2)}) %collective-permute-start.3) | collective-permute-done | bytes 65568 | tf_op jit(solution)/shard_map/ppermute | solution.py:550
  74.0 2.3 %collective-permute-done.4.rest_1_ = f32[8,2048]{1,0:T(8,128)S(1)} collective-permute-done((f32[8,2048]{1,0:T(8,128)S(1)}, f32[8,2048]{1,0:T(8,128)S(1)}, u32[]{:S(2)}, u32[]{:S(2)}) %collective-permute-start.4) | collective-permute-done | bytes 65568 | tf_op jit(solution)/shard_map/ppermute | solution.py:550
  76.2 11.0 %collective-permute-done.5.rest_2_ = f32[8,2048]{1,0:T(8,128)S(1)} collective-permute-done((f32[8,2048]{1,0:T(8,128)S(1)}, f32[8,2048]{1,0:T(8,128)S(1)}, u32[]{:S(2)}, u32[]{:S(2)}) %collective-permute-start.5) | collective-permute-done | bytes 65568 | tf_op jit(solution)/shard_map/ppermute | solution.py:550
  87.2 1.1 fusion.16
  88.4 0.1 pad_maximum_fusion.1.phase_ref
  88.4 0.1 fusion.12.coupling_ref
  88.5 0.0 all-to-all-done.1.in_ref
  88.6 0.0 copy-done.1
  88.6 0.0 copy-done.2
  88.6 1.6 %shard_map.134 = (f32[2,2,32,2048]{3,2,1,0:T(8,128)S(1)}, f32[4,2048]{1,0:T(4,128)S(1)}, f32[4,2048]{1,0:T(4,128)S(1)}, f32[8,2048]{1,0:T(8,128)S(1)}, f32[8,204...) custom-call(s32[1]{0:T(128)} %bitcast.place_ref, f32[64,32,128]{2,1,0:T(8,128)S(1)} %all-to-all-done.1.in_ref, ...), custom_call_target="tpu_custom_call" | custom-call | tf_op jit(solution)/shard_map/pallas_call | solution.py:410
  90.2 2.2 %collective-permute-start.10 = (f32[8,2048]{1,0:T(8,128)S(1)}, f32[8,2048]{1,0:T(8,128)S(1)}, u32[]{:S(2)}, u32[]{:S(2)}) collective-permute-start(f32[8,2048]{1,0:T(8,128)S(1)} %get-tuple-element.18), channel_id=1, source_target_pairs={{0,192},{64,0},{128,64},{192,128},{1,193},{65,1},{129,65},{193,129... | collective-permute-start | bytes 196616 | tf_op jit(solution)/shard_map/ppermute | solution.py:580
  92.3 4.6 %collective-permute-start.9 = (f32[8,2048]{1,0:T(8,128)S(1)}, f32[8,2048]{1,0:T(8,128)S(1)}, u32[]{:S(2)}, u32[]{:S(2)}) collective-permute-start(f32[8,2048]{1,0:T(8,128)S(1)} %get-tuple-element.17), channel_id=1, source_target_pairs={{0,128},{64,192},{128,0},{192,64},{1,129},{65,193},{129,1},{193,65... | collective-permute-start | bytes 196616 | tf_op jit(solution)/shard_map/ppermute | solution.py:580
  96.9 0.0 collective-permute-start.8
  96.9 1.9 %collective-permute-start.6 = (f32[4,2048]{1,0:T(4,128)S(1)}, f32[4,2048]{1,0:T(4,128)S(1)}, u32[]{:S(2)}, u32[]{:S(2)}) collective-permute-start(f32[4,2048]{1,0:T(4,128)S(1)} %get-tuple-element.12), channel_id=1, source_target_pairs={{0,1},{1,2},{2,3},{3,4},{4,5},{5,6},{6,7},{7,8},{8,9},{9,10},{10,1... | collective-permute-start | bytes 98312 | tf_op jit(solution)/shard_map/ppermute | solution.py:576
  98.9 10.6 %collective-permute-start.7 = (f32[4,2048]{1,0:T(4,128)S(1)}, f32[4,2048]{1,0:T(4,128)S(1)}, u32[]{:S(2)}, u32[]{:S(2)}) collective-permute-start(f32[4,2048]{1,0:T(4,128)S(1)} %get-tuple-element.13), channel_id=1, source_target_pairs={{1,0},{2,1},{3,2},{4,3},{5,4},{6,5},{7,6},{8,7},{9,8},{10,9},{11,1... | collective-permute-start | bytes 98312 | tf_op jit(solution)/shard_map/ppermute | solution.py:577
  109.4 0.0 collective-permute-done.6.above_ref
  109.4 1.7 %collective-permute-done.7.below_ref = f32[4,2048]{1,0:T(4,128)S(1)} collective-permute-done((f32[4,2048]{1,0:T(4,128)S(1)}, f32[4,2048]{1,0:T(4,128)S(1)}, u32[]{:S(2)}, u32[]{:S(2)}) %collective-permute-start.7) | collective-permute-done | bytes 32800 | tf_op jit(solution)/shard_map/ppermute | solution.py:577
  111.2 1.7 %shard_map.135 = (f32[2,1,2,32,2048]{4,3,2,1,0:T(8,128)}, f32[8,512]{1,0:T(8,128)S(1)}) custom-call(f32[2,2,32,2048]{3,2,1,0:T(8,128)S(1)} %get-tuple-element.11.wave_ref, f32[4,2048]{1,0:T(4,128)S(1)} %collective-permute-done.6.above_ref, f32[4,2048]{1,0:T(4,128)S(1)} %collective-permute-done.7.below_ref, f32[32,2048]{1,0:T(8,128)S(1)} %fusion.12.coupling_ref), custom_call_target="tpu_custom_call" | custom-call | tf_op jit(solution)/shard_map/pallas_call | solution.py:410
  112.8 0.0 collective-permute-done.10
  112.8 0.0 collective-permute-done.9
  112.8 0.0 collective-permute-done.8
  112.9 0.5 collective-permute-start.11
  113.4 3.8 %collective-permute-start.12 = (f32[8,2560]{1,0:T(8,128)S(1)}, f32[8,2560]{1,0:T(8,128)S(1)}, u32[]{:S(2)}, u32[]{:S(2)}) collective-permute-start(f32[8,2560]{1,0:T(8,128)S(1)} %pad_maximum_fusion.2.own_ref), channel_id=1, source_target_pairs={{0,128},{64,192},{128,0},{192,64},{1,129},{65,193},{129,1},{193,65... | collective-permute-start | bytes 245768 | tf_op jit(solution)/shard_map/ppermute | solution.py:550
  117.2 0.2 collective-permute-start.13
  117.4 1.9 %collective-permute-done.11.rest_0_ = f32[8,2560]{1,0:T(8,128)S(1)} collective-permute-done((f32[8,2560]{1,0:T(8,128)S(1)}, f32[8,2560]{1,0:T(8,128)S(1)}, u32[]{:S(2)}, u32[]{:S(2)}) %collective-permute-start.11) | collective-permute-done | bytes 81952 | tf_op jit(solution)/shard_map/ppermute | solution.py:550
  119.2 1.7 %collective-permute-done.12.rest_1_ = f32[8,2560]{1,0:T(8,128)S(1)} collective-permute-done((f32[8,2560]{1,0:T(8,128)S(1)}, f32[8,2560]{1,0:T(8,128)S(1)}, u32[]{:S(2)}, u32[]{:S(2)}) %collective-permute-start.12) | collective-permute-done | bytes 81952 | tf_op jit(solution)/shard_map/ppermute | solution.py:550
  121.0 0.9 collective-permute-done.13.rest_2_
  121.8 0.7 shard_map.136
  (14 shorter events, 0.1 us)
Async XLA Ops:
  0.6 18.8 %copy-start = (f32[4,32,2048]{2,1,0:T(8,128)S(1)}, f32[4,32,2048]{2,1,0:T(8,128)}, u32[]{:S(2)}) copy-start(f32[4,32,2048]{2,1,0:T(8,128)} %param.14) | copy-start | bytes 3145732
  3.8 20.5 %copy-start.4 = (f32[1,2]{1,0:T(1,128)S(1)}, f32[1,2]{1,0:T(1,128)}, u32[]{:S(2)}) copy-start(f32[1,2]{1,0:T(1,128)} %param.16) | copy-start | bytes 28
  3.8 38.0 %all-to-all-start = ((f32[64,32,128]{2,1,0:T(8,128)}), f32[64,32,128]{2,1,0:T(8,128)}, u32[]{:S(2)}, u32[]{:S(2)}) async-start(f32[64,32,128]{2,1,0:T(8,128)} %shard_map.131), calls=%async_computation | async-start | bytes 2097152 | tf_op jit(solution)/shard_map/all_to_all | solution.py:555
  19.5 11.6 %copy-start.5 = (f32[4,8,2048]{2,1,0:T(8,128)}, f32[4,8,2048]{2,1,0:T(8,128)S(1)}, u32[]{:S(2)}) copy-start(f32[4,8,2048]{2,1,0:T(8,128)S(1)} %dynamic-slice_bitcast_fusion) | copy-start | bytes 786436
  20.2 34.8 %collective-permute-start = (f32[8,2048]{1,0:T(8,128)}, f32[8,2048]{1,0:T(8,128)S(1)}, u32[]{:S(2)}, u32[]{:S(2)}) collective-permute-start(f32[8,2048]{1,0:T(8,128)} %get-tuple-element.24), channel_id=1, source_target_pairs={{0,192},{64,0},{128,64},{192,128},{1,193},{65,1},{129,65},{193,129... | collective-permute-start | bytes 196616 | tf_op jit(solution)/shard_map/ppermute | solution.py:542
  22.2 32.9 %collective-permute-start.1 = (f32[8,2048]{1,0:T(8,128)}, f32[8,2048]{1,0:T(8,128)S(1)}, u32[]{:S(2)}, u32[]{:S(2)}) collective-permute-start(f32[8,2048]{1,0:T(8,128)} %get-tuple-element.23), channel_id=1, source_target_pairs={{0,128},{64,192},{128,0},{192,64},{1,129},{65,193},{129,1},{193,65... | collective-permute-start | bytes 196616 | tf_op jit(solution)/shard_map/ppermute | solution.py:542
  22.7 32.4 %collective-permute-start.2 = (f32[8,2048]{1,0:T(8,128)}, f32[8,2048]{1,0:T(8,128)S(1)}, u32[]{:S(2)}, u32[]{:S(2)}) collective-permute-start(f32[8,2048]{1,0:T(8,128)} %get-tuple-element.22), channel_id=1, source_target_pairs={{0,64},{64,128},{128,192},{192,0},{1,65},{65,129},{129,193},{193,1... | collective-permute-start | bytes 196616 | tf_op jit(solution)/shard_map/ppermute | solution.py:542
  31.1 10.7 %copy-start.3 = (s32[1,128]{1,0:T(1,128)S(1)}, s32[1,128]{1,0:T(1,128)}, u32[]{:S(2)}) copy-start(s32[1,128]{1,0:T(1,128)} %refs_ref.1) | copy-start | bytes 1540
  48.0 40.5 %all-to-all-start.1 = ((f32[64,32,128]{2,1,0:T(8,128)}), f32[64,32,128]{2,1,0:T(8,128)S(1)}, u32[]{:S(2)}, u32[]{:S(2)}) async-start(f32[64,32,128]{2,1,0:T(8,128)} %bitcast.45), calls=%async_computation.1 | async-start | bytes 2097152 | tf_op jit(solution)/shard_map/all_to_all | solution.py:555
  54.2 34.4 %copy-start.1 = (bf16[768,256]{1,0:T(8,128)(2,1)S(1)}, bf16[768,256]{1,0:T(8,128)(2,1)}, u32[]{:S(2)}) copy-start(bf16[768,256]{1,0:T(8,128)(2,1)} %constant.223.clone.matrix_ref) | copy-start | bytes 1179652
  54.2 34.4 %copy-start.2 = (f32[2,16,128]{2,1,0:T(8,128)S(1)}, f32[2,16,128]{2,1,0:T(8,128)}, u32[]{:S(2)}) copy-start(f32[2,16,128]{2,1,0:T(8,128)} %constant.219.clone.twiddle_hbm.twiddle_ref) | copy-start | bytes 49156
  55.9 18.0 %collective-permute-start.3 = (f32[8,2048]{1,0:T(8,128)S(1)}, f32[8,2048]{1,0:T(8,128)S(1)}, u32[]{:S(2)}, u32[]{:S(2)}) collective-permute-start(f32[8,2048]{1,0:T(8,128)S(1)} %fusion.14.own_ref), channel_id=1, source_target_pairs={{0,64},{64,128},{128,192},{192,0},{1,65},{65,129},{129,193},{193,1... | collective-permute-start | bytes 196616 | tf_op jit(solution)/shard_map/ppermute | solution.py:550
  66.6 9.7 %collective-permute-start.4 = (f32[8,2048]{1,0:T(8,128)S(1)}, f32[8,2048]{1,0:T(8,128)S(1)}, u32[]{:S(2)}, u32[]{:S(2)}) collective-permute-start(f32[8,2048]{1,0:T(8,128)S(1)} %fusion.14.own_ref), channel_id=1, source_target_pairs={{0,128},{64,192},{128,0},{192,64},{1,129},{65,193},{129,1},{193,65... | collective-permute-start | bytes 196616 | tf_op jit(solution)/shard_map/ppermute | solution.py:550
  68.9 18.3 %collective-permute-start.5 = (f32[8,2048]{1,0:T(8,128)S(1)}, f32[8,2048]{1,0:T(8,128)S(1)}, u32[]{:S(2)}, u32[]{:S(2)}) collective-permute-start(f32[8,2048]{1,0:T(8,128)S(1)} %fusion.14.own_ref), channel_id=1, source_target_pairs={{0,192},{64,0},{128,64},{192,128},{1,193},{65,1},{129,65},{193,129... | collective-permute-start | bytes 196616 | tf_op jit(solution)/shard_map/ppermute | solution.py:550
  90.2 22.7 %collective-permute-start.10 = (f32[8,2048]{1,0:T(8,128)S(1)}, f32[8,2048]{1,0:T(8,128)S(1)}, u32[]{:S(2)}, u32[]{:S(2)}) collective-permute-start(f32[8,2048]{1,0:T(8,128)S(1)} %get-tuple-element.18), channel_id=1, source_target_pairs={{0,192},{64,0},{128,64},{192,128},{1,193},{65,1},{129,65},{193,129... | collective-permute-start | bytes 196616 | tf_op jit(solution)/shard_map/ppermute | solution.py:580
  92.3 20.5 %collective-permute-start.9 = (f32[8,2048]{1,0:T(8,128)S(1)}, f32[8,2048]{1,0:T(8,128)S(1)}, u32[]{:S(2)}, u32[]{:S(2)}) collective-permute-start(f32[8,2048]{1,0:T(8,128)S(1)} %get-tuple-element.17), channel_id=1, source_target_pairs={{0,128},{64,192},{128,0},{192,64},{1,129},{65,193},{129,1},{193,65... | collective-permute-start | bytes 196616 | tf_op jit(solution)/shard_map/ppermute | solution.py:580
  96.9 15.9 %collective-permute-start.8 = (f32[8,2048]{1,0:T(8,128)S(1)}, f32[8,2048]{1,0:T(8,128)S(1)}, u32[]{:S(2)}, u32[]{:S(2)}) collective-permute-start(f32[8,2048]{1,0:T(8,128)S(1)} %get-tuple-element.16), channel_id=1, source_target_pairs={{0,64},{64,128},{128,192},{192,0},{1,65},{65,129},{129,193},{193,1... | collective-permute-start | bytes 196616 | tf_op jit(solution)/shard_map/ppermute | solution.py:580
  96.9 12.5 %collective-permute-start.6 = (f32[4,2048]{1,0:T(4,128)S(1)}, f32[4,2048]{1,0:T(4,128)S(1)}, u32[]{:S(2)}, u32[]{:S(2)}) collective-permute-start(f32[4,2048]{1,0:T(4,128)S(1)} %get-tuple-element.12), channel_id=1, source_target_pairs={{0,1},{1,2},{2,3},{3,4},{4,5},{5,6},{6,7},{7,8},{8,9},{9,10},{10,1... | collective-permute-start | bytes 98312 | tf_op jit(solution)/shard_map/ppermute | solution.py:576
  98.9 12.3 %collective-permute-start.7 = (f32[4,2048]{1,0:T(4,128)S(1)}, f32[4,2048]{1,0:T(4,128)S(1)}, u32[]{:S(2)}, u32[]{:S(2)}) collective-permute-start(f32[4,2048]{1,0:T(4,128)S(1)} %get-tuple-element.13), channel_id=1, source_target_pairs={{1,0},{2,1},{3,2},{4,3},{5,4},{6,5},{7,6},{8,7},{9,8},{10,9},{11,1... | collective-permute-start | bytes 98312 | tf_op jit(solution)/shard_map/ppermute | solution.py:577
  112.9 6.4 %collective-permute-start.11 = (f32[8,2560]{1,0:T(8,128)S(1)}, f32[8,2560]{1,0:T(8,128)S(1)}, u32[]{:S(2)}, u32[]{:S(2)}) collective-permute-start(f32[8,2560]{1,0:T(8,128)S(1)} %pad_maximum_fusion.2.own_ref), channel_id=1, source_target_pairs={{0,64},{64,128},{128,192},{192,0},{1,65},{65,129},{129,193},{193,1... | collective-permute-start | bytes 245768 | tf_op jit(solution)/shard_map/ppermute | solution.py:550
  113.4 7.6 %collective-permute-start.12 = (f32[8,2560]{1,0:T(8,128)S(1)}, f32[8,2560]{1,0:T(8,128)S(1)}, u32[]{:S(2)}, u32[]{:S(2)}) collective-permute-start(f32[8,2560]{1,0:T(8,128)S(1)} %pad_maximum_fusion.2.own_ref), channel_id=1, source_target_pairs={{0,128},{64,192},{128,0},{192,64},{1,129},{65,193},{129,1},{193,65... | collective-permute-start | bytes 245768 | tf_op jit(solution)/shard_map/ppermute | solution.py:550
  117.2 4.7 %collective-permute-start.13 = (f32[8,2560]{1,0:T(8,128)S(1)}, f32[8,2560]{1,0:T(8,128)S(1)}, u32[]{:S(2)}, u32[]{:S(2)}) collective-permute-start(f32[8,2560]{1,0:T(8,128)S(1)} %pad_maximum_fusion.2.own_ref), channel_id=1, source_target_pairs={{0,192},{64,0},{128,64},{192,128},{1,193},{65,1},{129,65},{193,129... | collective-permute-start | bytes 245768 | tf_op jit(solution)/shard_map/ppermute | solution.py:550

commit v3 on v2

--- a/solution.py
+++ b/solution.py
@@ -320,8 +320,11 @@
         image_refs[k][...] = image_hold[pl.ds(at, 8), :]
 
 
-def laplace_kernel(wave_ref, above_ref, below_ref, coupling_ref, out_ref, edge_ref):
-    for tile, source, receiver in corrected(wave_ref, above_ref, below_ref, coupling_ref):
+def laplace_kernel(index_ref, wave_ref, above_ref, below_ref, coupling_ref, out_ref, edge_ref):
+    index = jnp.full((1, 2048), index_ref[0], jnp.int32)
+    above = [jnp.where(index == 0, 0.0, above_ref[row : row + 1, :]) for row in range(4)]
+    below = [jnp.where(index == 63, 0.0, below_ref[row : row + 1, :]) for row in range(4)]
+    for tile, source, receiver in corrected(wave_ref, above, below, coupling_ref):
         rows = slice(8 * tile, 8 * tile + 8)
         for field, pair in enumerate((source, receiver)):
             out_ref[field, 0, 0, rows, :] = pair[0]
@@ -335,7 +338,7 @@
                 edge_ref[4 + part : 5 + part, :] = image[7:8, lanes]
 
 
-def corrected(wave_ref, above_ref, below_ref, coupling_ref):
+def corrected(wave_ref, above, below, coupling_ref):
     row = lax.broadcasted_iota(jnp.int32, (8, 2048), 0)
     lane = lax.broadcasted_iota(jnp.int32, (8, 2048), 1)
     for tile in range(4):
@@ -350,11 +353,11 @@
                 if tile > 0:
                     before = wave_ref[field, c, 8 * tile - 1 : 8 * tile, :]
                 else:
-                    before = 0.0 if above_ref is None else above_ref[index : index + 1, :]
+                    before = 0.0 if above is None else above[index]
                 if tile < 3:
                     after = wave_ref[field, c, 8 * tile + 8 : 8 * tile + 9, :]
                 else:
-                    after = 0.0 if below_ref is None else below_ref[index : index + 1, :]
+                    after = 0.0 if below is None else below[index]
                 up = jnp.where(row == 0, before, pltpu.roll(value, 1, 0))
                 down = jnp.where(row == 7, after, pltpu.roll(value, 7, 0))
                 left = jnp.where(lane == 0, 0.0, pltpu.roll(value, 1, 1))
@@ -483,12 +486,13 @@
     )
 
 
-def laplace(wave, above, below, coupling):
+def laplace(index, wave, above, below, coupling):
     return call(
         laplace_kernel,
         (f32(2, 1, 2, 32, 2048), f32(8, 512)),
-        (wave, above, below, coupling),
-        near=(0, 1, 2, 3),
+        (index, wave, above, below, coupling),
+        smem=1,
+        near=(1, 2, 3, 4),
     )
 
 
@@ -572,14 +576,14 @@
     blocks = middle(blocks, shift, ref_index)
     blocks = exchange(blocks)
     wave, first, last, *quarters = inverse_y(place, blocks, phase, coupling)
-    count = 64
-    above = lax.ppermute(last, "space", [(i, i + 1) for i in range(count - 1)])
-    below = lax.ppermute(first, "space", [(i + 1, i) for i in range(count - 1)])
+    above = lax.ppermute(last, "space", shifted_pairs(1, 64))
+    below = lax.ppermute(first, "space", shifted_pairs(63, 64))
     total = quarters[0]
     for step in (1, 2, 3):
         arrived = lax.ppermute(quarters[step], "freq", shifted_pairs(step))
         total = total + arrived
-    fields, edges = laplace(wave, above, below, coupling)
+    index = space_index.reshape(1).astype(jnp.int32)
+    fields, edges = laplace(index, wave, above, below, coupling)
     image = assemble(place, gathered(jnp.concatenate([total, edges], axis=1)))
     return fields, image
 

time: 124 us -> 120 us (0.968)
  starting transfers between devices: 64 us -> 60 us
    ppermute x2, starting transfers between devices: 12.5 us -> 8.66 us  [the longest x1 8.66 us: step_down(): below = lax.ppermute(first, 'space', shifted_pairs(63, 64))]
  transfers between devices with their start and end apart: 16 -> 16, of which waited for: 8 -> 8; matrix products, arithmetic and copies ran while one was open for 8% -> 8% of each run, Pallas kernels for 6% -> 7%
where the time goes in v3:
time: 120 us; the launch traced here: 119 us
  starting transfers between devices  60 us (50%)
  waiting for transfers between devices  32.7 us (27%)
  Pallas kernels  13.4 us (11%)
  other arithmetic  7.17 us (6%)
  between operations  3.54 us (3%)
  local copies, waits for them, and re-layouts  2.18 us (2%)
    all_to_all x2, starting transfers between devices, exchange(): lax.all_to_all(blocks, 'space', split_axis=0, concat_axis=0, tiled=True)  21 us
    ppermute x6, starting transfers between devices, gathered(): pieces.append(lax.ppermute(mine, 'freq', shifted_pairs(step)))  20.2 us
    ppermute x6, waiting for transfers between devices, gathered(): pieces.append(lax.ppermute(mine, 'freq', shifted_pairs(step)))  20.1 us
    pallas_call x6, Pallas kernels, call(): pl.pallas_call(kernel, out_shape=out_shape, in_specs=[whole(pltpu.SMEM)]...  13.4 us
    all_to_all x2, waiting for transfers between devices, exchange(): lax.all_to_all(blocks, 'space', split_axis=0, concat_axis=0, tiled=True)  10.6 us
    ppermute x1, starting transfers between devices, step_down(): below = lax.ppermute(first, 'space', shifted_pairs(63, 64))  8.66 us
    ppermute x3, starting transfers between devices, step_down(): arrived = lax.ppermute(quarters[step], 'freq', shifted_pairs(step))  6.76 us
    select_n x1, other arithmetic, shift_tables(): tables.append(jnp.where(travels, jnp.cos(root), jnp.exp(-root)))  4.72 us
  transfers between devices with their start and end apart: 16, of which 8 were waited for; matrix products, arithmetic and copies ran while one was open for 8% of the time, Pallas kernels for 7%

profile of v3, /device:TPU:2, one launch (start us, length us, event | category | flops | bytes accessed | tf_op | source)
XLA Modules:
  0.0 119.0 jit_solution(15304175388590522888)
XLA Ops:
  0.6 0.0 copy-start
  0.6 3.2 %shard_map.131 = f32[64,32,128]{2,1,0:T(8,128)} custom-call(f32[2,1,2,32,2048]{4,3,2,1,0:T(8,128)} %wave_hbm.1, bf16[256,768]{1,0:T(8,128)(2,1)} %constant.218.clone.matrix_hbm, f32[2,16,128]{2,1,0:T(8,128)} %constant.219.clone.twiddle_hbm.twiddle_ref), custom_call_target="tpu_custom_call" | custom-call | tf_op jit(solution)/shard_map/pallas_call | solution.py:413
  3.8 0.0 copy-start.4
  3.8 14.9 %all-to-all-start = ((f32[64,32,128]{2,1,0:T(8,128)}), f32[64,32,128]{2,1,0:T(8,128)}, u32[]{:S(2)}, u32[]{:S(2)}) async-start(f32[64,32,128]{2,1,0:T(8,128)} %shard_map.131), calls=%async_computation | async-start | bytes 2097152 | tf_op jit(solution)/shard_map/all_to_all | solution.py:559
  19.4 0.0 copy-done
  19.5 0.0 copy-start.5
  19.5 0.7 dynamic-slice_bitcast_fusion.1
  20.2 1.9 %collective-permute-start = (f32[8,2048]{1,0:T(8,128)}, f32[8,2048]{1,0:T(8,128)S(1)}, u32[]{:S(2)}, u32[]{:S(2)}) collective-permute-start(f32[8,2048]{1,0:T(8,128)} %get-tuple-element.24), channel_id=1, source_target_pairs={{0,192},{64,0},{128,64},{192,128},{1,193},{65,1},{129,65},{193,129... | collective-permute-start | bytes 196616 | tf_op jit(solution)/shard_map/ppermute | solution.py:546
  22.2 0.5 collective-permute-start.1
  22.7 1.0 collective-permute-start.2
  24.4 0.0 copy-done.4
  24.4 0.6 fusion.25
  26.3 4.7 %exponential_select_fusion.1 = (f32[1,1024,128]{2,1,0:T(8,128)S(1)}, f32[1,1024,128]{2,1,0:T(8,128)S(1)}, f32[1,1024,128]{2,1,0:T(8,128)S(1)}, f32[1,1024,128]{2,1,0:T(8,128)S(1)}) fusion(f32[]{:T(128)S(6)} %integer_pow.50, s32[1024]{0:T(1024)S(1)} %get-tuple-element.38, s32[1024]{0:T(1024)S(1)} %get-tuple-element.39, ...), kind=kLoop, calls=%fused_computation.25 | loop fusion | flops 6946816 | bytes 2119056 | tf_op jit(solution)/shard_map/jit(_where)/select_n | solution.py:522
  31.0 0.0 copy-done.5
  31.1 0.0 copy-start.3
  31.1 0.1 pad_maximum_fusion.shift_ref
  31.2 10.6 %all-to-all-done = f32[64,32,128]{2,1,0:T(8,128)} async-done(((f32[64,32,128]{2,1,0:T(8,128)}), f32[64,32,128]{2,1,0:T(8,128)}, u32[]{:S(2)}, u32[]{:S(2)}) %all-to-all-start) | async-done | bytes 1048608 | tf_op jit(solution)/shard_map/all_to_all | solution.py:559
  41.8 0.0 copy-done.3
  41.9 6.2 %shard_map.132 = f32[8,8,32,128]{3,2,1,0:T(8,128)} custom-call(s32[1,128]{1,0:T(1,128)S(1)} %copy-done.3, f32[4,1024,128]{2,1,0:T(8,128)S(1)} %pad_maximum_fusion.shift_ref, f32[8,8,32,128]{3,2,1,0:T(8,128)} %bitcast.5.in_hbm, bf16[768,256]{1,0:T(8,128)(2,1)} %constant.220.clone.forward_hbm, bf16[768,256]{1,0:T(8,128)(2,1)} %constant.221.clone.inverse_hbm, ...), custom_call_target="tpu_custom_call" | custom-call | tf_op jit(solution)/shard_map/pallas_call | solution.py:413
  48.0 6.1 %all-to-all-start.1 = ((f32[64,32,128]{2,1,0:T(8,128)}), f32[64,32,128]{2,1,0:T(8,128)S(1)}, u32[]{:S(2)}, u32[]{:S(2)}) async-start(f32[64,32,128]{2,1,0:T(8,128)} %bitcast.46), calls=%async_computation.1 | async-start | bytes 2097152 | tf_op jit(solution)/shard_map/all_to_all | solution.py:559
  54.2 0.0 copy-start.1
  54.2 0.0 copy-start.2
  54.2 0.1 fusion.24
  54.3 0.6 gather_fusion
  54.9 0.1 broadcast_in_dim.17
  55.0 0.1 broadcast_in_dim_reshape.3
  55.1 0.0 collective-permute-done
  55.1 0.0 collective-permute-done.1
  55.1 0.0 collective-permute-done.2
  55.1 0.9 fusion.14.own_ref
  55.9 10.6 %collective-permute-start.3 = (f32[8,2048]{1,0:T(8,128)S(1)}, f32[8,2048]{1,0:T(8,128)S(1)}, u32[]{:S(2)}, u32[]{:S(2)}) collective-permute-start(f32[8,2048]{1,0:T(8,128)S(1)} %fusion.14.own_ref), channel_id=1, source_target_pairs={{0,64},{64,128},{128,192},{192,0},{1,65},{65,129},{129,193},{193,1... | collective-permute-start | bytes 196616 | tf_op jit(solution)/shard_map/ppermute | solution.py:554
  66.6 2.4 %collective-permute-start.4 = (f32[8,2048]{1,0:T(8,128)S(1)}, f32[8,2048]{1,0:T(8,128)S(1)}, u32[]{:S(2)}, u32[]{:S(2)}) collective-permute-start(f32[8,2048]{1,0:T(8,128)S(1)} %fusion.14.own_ref), channel_id=1, source_target_pairs={{0,128},{64,192},{128,0},{192,64},{1,129},{65,193},{129,1},{193,65... | collective-permute-start | bytes 196616 | tf_op jit(solution)/shard_map/ppermute | solution.py:554
  68.9 2.8 %collective-permute-start.5 = (f32[8,2048]{1,0:T(8,128)S(1)}, f32[8,2048]{1,0:T(8,128)S(1)}, u32[]{:S(2)}, u32[]{:S(2)}) collective-permute-start(f32[8,2048]{1,0:T(8,128)S(1)} %fusion.14.own_ref), channel_id=1, source_target_pairs={{0,192},{64,0},{128,64},{192,128},{1,193},{65,1},{129,65},{193,129... | collective-permute-start | bytes 196616 | tf_op jit(solution)/shard_map/ppermute | solution.py:554
  71.8 2.2 %collective-permute-done.3.rest_0_ = f32[8,2048]{1,0:T(8,128)S(1)} collective-permute-done((f32[8,2048]{1,0:T(8,128)S(1)}, f32[8,2048]{1,0:T(8,128)S(1)}, u32[]{:S(2)}, u32[]{:S(2)}) %collective-permute-start.3) | collective-permute-done | bytes 65568 | tf_op jit(solution)/shard_map/ppermute | solution.py:554
  74.0 2.3 %collective-permute-done.4.rest_1_ = f32[8,2048]{1,0:T(8,128)S(1)} collective-permute-done((f32[8,2048]{1,0:T(8,128)S(1)}, f32[8,2048]{1,0:T(8,128)S(1)}, u32[]{:S(2)}, u32[]{:S(2)}) %collective-permute-start.4) | collective-permute-done | bytes 65568 | tf_op jit(solution)/shard_map/ppermute | solution.py:554
  76.2 11.0 %collective-permute-done.5.rest_2_ = f32[8,2048]{1,0:T(8,128)S(1)} collective-permute-done((f32[8,2048]{1,0:T(8,128)S(1)}, f32[8,2048]{1,0:T(8,128)S(1)}, u32[]{:S(2)}, u32[]{:S(2)}) %collective-permute-start.5) | collective-permute-done | bytes 65568 | tf_op jit(solution)/shard_map/ppermute | solution.py:554
  87.2 1.1 fusion.16
  88.4 0.1 pad_maximum_fusion.1.phase_ref
  88.4 0.1 fusion.12.coupling_ref
  88.5 0.0 all-to-all-done.1.in_ref
  88.6 0.0 copy-done.1
  88.6 0.0 copy-done.2
  88.6 1.6 %shard_map.134 = (f32[2,2,32,2048]{3,2,1,0:T(8,128)S(1)}, f32[4,2048]{1,0:T(4,128)S(1)}, f32[4,2048]{1,0:T(4,128)S(1)}, f32[8,2048]{1,0:T(8,128)S(1)}, f32[8,204...) custom-call(s32[1]{0:T(128)} %bitcast.1.place_ref, f32[64,32,128]{2,1,0:T(8,128)S(1)} %all-to-all-done.1.in_ref, ...), custom_call_target="tpu_custom_call" | custom-call | tf_op jit(solution)/shard_map/pallas_call | solution.py:413
  90.2 2.2 %collective-permute-start.10 = (f32[8,2048]{1,0:T(8,128)S(1)}, f32[8,2048]{1,0:T(8,128)S(1)}, u32[]{:S(2)}, u32[]{:S(2)}) collective-permute-start(f32[8,2048]{1,0:T(8,128)S(1)} %get-tuple-element.18), channel_id=1, source_target_pairs={{0,192},{64,0},{128,64},{192,128},{1,193},{65,1},{129,65},{193,129... | collective-permute-start | bytes 196616 | tf_op jit(solution)/shard_map/ppermute | solution.py:583
  92.3 4.6 %collective-permute-start.9 = (f32[8,2048]{1,0:T(8,128)S(1)}, f32[8,2048]{1,0:T(8,128)S(1)}, u32[]{:S(2)}, u32[]{:S(2)}) collective-permute-start(f32[8,2048]{1,0:T(8,128)S(1)} %get-tuple-element.17), channel_id=1, source_target_pairs={{0,128},{64,192},{128,0},{192,64},{1,129},{65,193},{129,1},{193,65... | collective-permute-start | bytes 196616 | tf_op jit(solution)/shard_map/ppermute | solution.py:583
  96.9 0.0 collective-permute-start.8
  96.9 0.0 collective-permute-start.6
  96.9 8.7 %collective-permute-start.7 = (f32[4,2048]{1,0:T(4,128)S(1)}, f32[4,2048]{1,0:T(4,128)S(1)}, u32[]{:S(2)}, u32[]{:S(2)}) collective-permute-start(f32[4,2048]{1,0:T(4,128)S(1)} %get-tuple-element.13), channel_id=1, source_target_pairs={{0,63},{1,0},{2,1},{3,2},{4,3},{5,4},{6,5},{7,6},{8,7},{9,8},{10,9... | collective-permute-start | bytes 98312 | tf_op jit(solution)/shard_map/ppermute | solution.py:580
  105.6 1.9 %collective-permute-done.6.above_ref = f32[4,2048]{1,0:T(4,128)S(1)} collective-permute-done((f32[4,2048]{1,0:T(4,128)S(1)}, f32[4,2048]{1,0:T(4,128)S(1)}, u32[]{:S(2)}, u32[]{:S(2)}) %collective-permute-start.6) | collective-permute-done | bytes 32800 | tf_op jit(solution)/shard_map/ppermute | solution.py:579
  107.6 0.0 collective-permute-done.7.below_ref
  107.6 1.7 %shard_map.135 = (f32[2,1,2,32,2048]{4,3,2,1,0:T(8,128)}, f32[8,512]{1,0:T(8,128)S(1)}) custom-call(s32[1]{0:T(128)} %bitcast.index_ref, f32[2,2,32,2048]{3,2,1,0:T(8,128)S(1)} %get-tuple-element.11.wave_ref, f32[4,2048]{1,0:T(4,128)S(1)} %collective-permute-done.6.above_ref, f32[4,2048]{1,0:T(4,128)S(1)} %collective-permute-done.7.below_ref, ...), custom_call_target="tpu_custom_call" | custom-call | tf_op jit(solution)/shard_map/pallas_call | solution.py:413
  109.2 0.0 collective-permute-done.10
  109.2 0.0 collective-permute-done.9
  109.2 0.0 collective-permute-done.8
  109.3 0.3 collective-permute-start.11
  109.6 3.8 %collective-permute-start.12 = (f32[8,2560]{1,0:T(8,128)S(1)}, f32[8,2560]{1,0:T(8,128)S(1)}, u32[]{:S(2)}, u32[]{:S(2)}) collective-permute-start(f32[8,2560]{1,0:T(8,128)S(1)} %pad_maximum_fusion.2.own_ref), channel_id=1, source_target_pairs={{0,128},{64,192},{128,0},{192,64},{1,129},{65,193},{129,1},{193,65... | collective-permute-start | bytes 245768 | tf_op jit(solution)/shard_map/ppermute | solution.py:554
  113.4 0.2 collective-permute-start.13
  113.6 2.0 %collective-permute-done.11.rest_0_ = f32[8,2560]{1,0:T(8,128)S(1)} collective-permute-done((f32[8,2560]{1,0:T(8,128)S(1)}, f32[8,2560]{1,0:T(8,128)S(1)}, u32[]{:S(2)}, u32[]{:S(2)}) %collective-permute-start.11) | collective-permute-done | bytes 81952 | tf_op jit(solution)/shard_map/ppermute | solution.py:554
  115.7 1.7 %collective-permute-done.12.rest_1_ = f32[8,2560]{1,0:T(8,128)S(1)} collective-permute-done((f32[8,2560]{1,0:T(8,128)S(1)}, f32[8,2560]{1,0:T(8,128)S(1)}, u32[]{:S(2)}, u32[]{:S(2)}) %collective-permute-start.12) | collective-permute-done | bytes 81952 | tf_op jit(solution)/shard_map/ppermute | solution.py:554
  117.4 0.8 collective-permute-done.13.rest_2_
  118.2 0.7 shard_map.136
  (14 shorter events, 0.1 us)
Async XLA Ops:
  0.6 18.8 %copy-start = (f32[4,32,2048]{2,1,0:T(8,128)S(1)}, f32[4,32,2048]{2,1,0:T(8,128)}, u32[]{:S(2)}) copy-start(f32[4,32,2048]{2,1,0:T(8,128)} %param.14) | copy-start | bytes 3145732
  3.8 20.5 %copy-start.4 = (f32[1,2]{1,0:T(1,128)S(1)}, f32[1,2]{1,0:T(1,128)}, u32[]{:S(2)}) copy-start(f32[1,2]{1,0:T(1,128)} %param.16) | copy-start | bytes 28
  3.8 38.0 %all-to-all-start = ((f32[64,32,128]{2,1,0:T(8,128)}), f32[64,32,128]{2,1,0:T(8,128)}, u32[]{:S(2)}, u32[]{:S(2)}) async-start(f32[64,32,128]{2,1,0:T(8,128)} %shard_map.131), calls=%async_computation | async-start | bytes 2097152 | tf_op jit(solution)/shard_map/all_to_all | solution.py:559
  19.5 11.6 %copy-start.5 = (f32[4,8,2048]{2,1,0:T(8,128)}, f32[4,8,2048]{2,1,0:T(8,128)S(1)}, u32[]{:S(2)}) copy-start(f32[4,8,2048]{2,1,0:T(8,128)S(1)} %dynamic-slice_bitcast_fusion) | copy-start | bytes 786436
  20.2 34.8 %collective-permute-start = (f32[8,2048]{1,0:T(8,128)}, f32[8,2048]{1,0:T(8,128)S(1)}, u32[]{:S(2)}, u32[]{:S(2)}) collective-permute-start(f32[8,2048]{1,0:T(8,128)} %get-tuple-element.24), channel_id=1, source_target_pairs={{0,192},{64,0},{128,64},{192,128},{1,193},{65,1},{129,65},{193,129... | collective-permute-start | bytes 196616 | tf_op jit(solution)/shard_map/ppermute | solution.py:546
  22.2 32.9 %collective-permute-start.1 = (f32[8,2048]{1,0:T(8,128)}, f32[8,2048]{1,0:T(8,128)S(1)}, u32[]{:S(2)}, u32[]{:S(2)}) collective-permute-start(f32[8,2048]{1,0:T(8,128)} %get-tuple-element.23), channel_id=1, source_target_pairs={{0,128},{64,192},{128,0},{192,64},{1,129},{65,193},{129,1},{193,65... | collective-permute-start | bytes 196616 | tf_op jit(solution)/shard_map/ppermute | solution.py:546
  22.7 32.4 %collective-permute-start.2 = (f32[8,2048]{1,0:T(8,128)}, f32[8,2048]{1,0:T(8,128)S(1)}, u32[]{:S(2)}, u32[]{:S(2)}) collective-permute-start(f32[8,2048]{1,0:T(8,128)} %get-tuple-element.22), channel_id=1, source_target_pairs={{0,64},{64,128},{128,192},{192,0},{1,65},{65,129},{129,193},{193,1... | collective-permute-start | bytes 196616 | tf_op jit(solution)/shard_map/ppermute | solution.py:546
  31.1 10.8 %copy-start.3 = (s32[1,128]{1,0:T(1,128)S(1)}, s32[1,128]{1,0:T(1,128)}, u32[]{:S(2)}) copy-start(s32[1,128]{1,0:T(1,128)} %refs_ref.1) | copy-start | bytes 1540
  48.0 40.5 %all-to-all-start.1 = ((f32[64,32,128]{2,1,0:T(8,128)}), f32[64,32,128]{2,1,0:T(8,128)S(1)}, u32[]{:S(2)}, u32[]{:S(2)}) async-start(f32[64,32,128]{2,1,0:T(8,128)} %bitcast.46), calls=%async_computation.1 | async-start | bytes 2097152 | tf_op jit(solution)/shard_map/all_to_all | solution.py:559
  54.2 34.4 %copy-start.1 = (bf16[768,256]{1,0:T(8,128)(2,1)S(1)}, bf16[768,256]{1,0:T(8,128)(2,1)}, u32[]{:S(2)}) copy-start(bf16[768,256]{1,0:T(8,128)(2,1)} %constant.223.clone.matrix_ref) | copy-start | bytes 1179652
  54.2 34.4 %copy-start.2 = (f32[2,16,128]{2,1,0:T(8,128)S(1)}, f32[2,16,128]{2,1,0:T(8,128)}, u32[]{:S(2)}) copy-start(f32[2,16,128]{2,1,0:T(8,128)} %constant.219.clone.twiddle_hbm.twiddle_ref) | copy-start | bytes 49156
  55.9 18.0 %collective-permute-start.3 = (f32[8,2048]{1,0:T(8,128)S(1)}, f32[8,2048]{1,0:T(8,128)S(1)}, u32[]{:S(2)}, u32[]{:S(2)}) collective-permute-start(f32[8,2048]{1,0:T(8,128)S(1)} %fusion.14.own_ref), channel_id=1, source_target_pairs={{0,64},{64,128},{128,192},{192,0},{1,65},{65,129},{129,193},{193,1... | collective-permute-start | bytes 196616 | tf_op jit(solution)/shard_map/ppermute | solution.py:554
  66.6 9.7 %collective-permute-start.4 = (f32[8,2048]{1,0:T(8,128)S(1)}, f32[8,2048]{1,0:T(8,128)S(1)}, u32[]{:S(2)}, u32[]{:S(2)}) collective-permute-start(f32[8,2048]{1,0:T(8,128)S(1)} %fusion.14.own_ref), channel_id=1, source_target_pairs={{0,128},{64,192},{128,0},{192,64},{1,129},{65,193},{129,1},{193,65... | collective-permute-start | bytes 196616 | tf_op jit(solution)/shard_map/ppermute | solution.py:554
  68.9 18.3 %collective-permute-start.5 = (f32[8,2048]{1,0:T(8,128)S(1)}, f32[8,2048]{1,0:T(8,128)S(1)}, u32[]{:S(2)}, u32[]{:S(2)}) collective-permute-start(f32[8,2048]{1,0:T(8,128)S(1)} %fusion.14.own_ref), channel_id=1, source_target_pairs={{0,192},{64,0},{128,64},{192,128},{1,193},{65,1},{129,65},{193,129... | collective-permute-start | bytes 196616 | tf_op jit(solution)/shard_map/ppermute | solution.py:554
  90.2 19.0 %collective-permute-start.10 = (f32[8,2048]{1,0:T(8,128)S(1)}, f32[8,2048]{1,0:T(8,128)S(1)}, u32[]{:S(2)}, u32[]{:S(2)}) collective-permute-start(f32[8,2048]{1,0:T(8,128)S(1)} %get-tuple-element.18), channel_id=1, source_target_pairs={{0,192},{64,0},{128,64},{192,128},{1,193},{65,1},{129,65},{193,129... | collective-permute-start | bytes 196616 | tf_op jit(solution)/shard_map/ppermute | solution.py:583
  92.3 16.9 %collective-permute-start.9 = (f32[8,2048]{1,0:T(8,128)S(1)}, f32[8,2048]{1,0:T(8,128)S(1)}, u32[]{:S(2)}, u32[]{:S(2)}) collective-permute-start(f32[8,2048]{1,0:T(8,128)S(1)} %get-tuple-element.17), channel_id=1, source_target_pairs={{0,128},{64,192},{128,0},{192,64},{1,129},{65,193},{129,1},{193,65... | collective-permute-start | bytes 196616 | tf_op jit(solution)/shard_map/ppermute | solution.py:583
  96.9 12.3 %collective-permute-start.8 = (f32[8,2048]{1,0:T(8,128)S(1)}, f32[8,2048]{1,0:T(8,128)S(1)}, u32[]{:S(2)}, u32[]{:S(2)}) collective-permute-start(f32[8,2048]{1,0:T(8,128)S(1)} %get-tuple-element.16), channel_id=1, source_target_pairs={{0,64},{64,128},{128,192},{192,0},{1,65},{65,129},{129,193},{193,1... | collective-permute-start | bytes 196616 | tf_op jit(solution)/shard_map/ppermute | solution.py:583
  96.9 10.6 %collective-permute-start.6 = (f32[4,2048]{1,0:T(4,128)S(1)}, f32[4,2048]{1,0:T(4,128)S(1)}, u32[]{:S(2)}, u32[]{:S(2)}) collective-permute-start(f32[4,2048]{1,0:T(4,128)S(1)} %get-tuple-element.12), channel_id=1, source_target_pairs={{0,1},{1,2},{2,3},{3,4},{4,5},{5,6},{6,7},{7,8},{8,9},{9,10},{10,1... | collective-permute-start | bytes 98312 | tf_op jit(solution)/shard_map/ppermute | solution.py:579
  96.9 10.6 %collective-permute-start.7 = (f32[4,2048]{1,0:T(4,128)S(1)}, f32[4,2048]{1,0:T(4,128)S(1)}, u32[]{:S(2)}, u32[]{:S(2)}) collective-permute-start(f32[4,2048]{1,0:T(4,128)S(1)} %get-tuple-element.13), channel_id=1, source_target_pairs={{0,63},{1,0},{2,1},{3,2},{4,3},{5,4},{6,5},{7,6},{8,7},{9,8},{10,9... | collective-permute-start | bytes 98312 | tf_op jit(solution)/shard_map/ppermute | solution.py:580
  109.3 6.4 %collective-permute-start.11 = (f32[8,2560]{1,0:T(8,128)S(1)}, f32[8,2560]{1,0:T(8,128)S(1)}, u32[]{:S(2)}, u32[]{:S(2)}) collective-permute-start(f32[8,2560]{1,0:T(8,128)S(1)} %pad_maximum_fusion.2.own_ref), channel_id=1, source_target_pairs={{0,64},{64,128},{128,192},{192,0},{1,65},{65,129},{129,193},{193,1... | collective-permute-start | bytes 245768 | tf_op jit(solution)/shard_map/ppermute | solution.py:554
  109.6 7.8 %collective-permute-start.12 = (f32[8,2560]{1,0:T(8,128)S(1)}, f32[8,2560]{1,0:T(8,128)S(1)}, u32[]{:S(2)}, u32[]{:S(2)}) collective-permute-start(f32[8,2560]{1,0:T(8,128)S(1)} %pad_maximum_fusion.2.own_ref), channel_id=1, source_target_pairs={{0,128},{64,192},{128,0},{192,64},{1,129},{65,193},{129,1},{193,65... | collective-permute-start | bytes 245768 | tf_op jit(solution)/shard_map/ppermute | solution.py:554
  113.4 4.8 %collective-permute-start.13 = (f32[8,2560]{1,0:T(8,128)S(1)}, f32[8,2560]{1,0:T(8,128)S(1)}, u32[]{:S(2)}, u32[]{:S(2)}) collective-permute-start(f32[8,2560]{1,0:T(8,128)S(1)} %pad_maximum_fusion.2.own_ref), channel_id=1, source_target_pairs={{0,192},{64,0},{128,64},{192,128},{1,193},{65,1},{129,65},{193,129... | collective-permute-start | bytes 245768 | tf_op jit(solution)/shard_map/ppermute | solution.py:554

commit v4 on v3

--- a/solution.py
+++ b/solution.py
@@ -36,30 +36,20 @@
         [np.concatenate([cosine, sine], 1), np.concatenate([-sine, cosine], 1)], 0
     )
     forward = forward.reshape(2, 8, 16, 256).transpose(1, 0, 2, 3).reshape(256, 256)
-    inverse = forward.copy() / NY
-    fh, fl = split_bf16(forward)
-    y_forward = np.concatenate([fh, fl, fh], 1)
-    ih, il = split_bf16(inverse)
-    y_inverse = np.concatenate([ih, il, ih], 0)
+    y_matrix = np.stack(split_bf16(forward))
     r = np.arange(NX_R)
     angle = 2.0 * np.pi * (np.outer(r, r) % NX_R) / NX_R
     cosine = np.kron(np.eye(4), np.cos(angle))
     sine = np.kron(np.eye(4), np.sin(angle))
     x_forward = np.block([[cosine, -sine], [sine, cosine]])
-    x_inverse = np.block([[cosine, sine], [-sine, cosine]]) / NX
-    xh, xl = split_bf16(x_forward)
-    x_forward = np.concatenate([xh, xl, xh], 0)
-    xh, xl = split_bf16(x_inverse)
-    x_inverse = np.concatenate([xh, xl, xh], 0)
+    x_matrix = np.stack(split_bf16(x_forward))
     angle = 2.0 * np.pi * np.outer(np.arange(NY_A), b) / NY
     y_twiddle = np.stack([np.cos(angle), -np.sin(angle)]).astype(np.float32)
     angle = 2.0 * np.pi * np.outer(np.arange(NX_S), np.tile(r, 4)) / NX
     x_twiddle = np.stack([np.cos(angle), -np.sin(angle)]).astype(np.float32)
     return dict(
-        y_forward=y_forward,
-        y_inverse=y_inverse,
-        x_forward=x_forward,
-        x_inverse=x_inverse,
+        y_matrix=y_matrix,
+        x_matrix=x_matrix,
         y_twiddle=y_twiddle,
         x_twiddle=x_twiddle,
     )
@@ -133,6 +123,10 @@
     return jnp.concatenate([high, high, low], axis=1)
 
 
+def tripled(matrix_ref, axis):
+    return jnp.concatenate([matrix_ref[0], matrix_ref[1], matrix_ref[0]], axis=axis)
+
+
 def matmul(left, right, contract):
     return lax.dot_general(left, right, (contract, ((), ())), preferred_element_type=jnp.float32)
 
@@ -165,7 +159,7 @@
                 mid_ref[at : at + 8, 0:128] = real
                 mid_ref[at : at + 8, 128:256] = imag
     waits[9].wait()
-    matrix = matrix_ref[...]
+    matrix = tripled(matrix_ref, 1)
     for pair in range(4):
         packed = spread(mid_ref[256 * pair : 256 * pair + 256, :])
         product = matmul(matrix, packed, ((1,), (1,)))
@@ -174,110 +168,110 @@
             out_ref[at : at + 8] = product[:, 128 * half : 128 * half + 128].reshape(8, 32, 128)
 
 
-def column_transform(load, store, sign, hold_ref):
-    for n0 in range(8):
-        piece = transform([load(8 * n1 + n0) for n1 in range(8)], sign)
-        for ka in range(8):
-            real, imag = times(piece[ka], n0 * ka, 64, sign)
-            hold_ref[0, ka * 8 + n0] = real
-            hold_ref[1, ka * 8 + n0] = imag
-    for ka in range(8):
-        values = [(hold_ref[0, ka * 8 + n0], hold_ref[1, ka * 8 + n0]) for n0 in range(8)]
-        for kb, value in enumerate(transform(values, sign)):
-            store(ka + 8 * kb, value)
-
-
 def middle_kernel(
     refs_ref,
     shift_ref,
     in_hbm,
-    forward_hbm,
-    inverse_hbm,
+    matrix_hbm,
     twiddle_hbm,
     out_hbm,
     in_ref,
     out_ref,
-    forward_ref,
-    inverse_ref,
+    matrix_ref,
     twiddle_ref,
     mid_ref,
     back_ref,
     hold_ref,
+    last_ref,
     sems,
 ):
     waits = fetch(
-        [twiddle_hbm] + [in_hbm.at[:, n] for n in range(8)] + [forward_hbm, inverse_hbm],
-        [twiddle_ref] + [in_ref.at[:, n] for n in range(8)] + [forward_ref, inverse_ref],
+        [twiddle_hbm] + [in_hbm.at[:, n] for n in range(8)] + [matrix_hbm],
+        [twiddle_ref] + [in_ref.at[:, n] for n in range(8)] + [matrix_ref],
         sems,
     )
     waits[0].wait()
     early = lax.broadcasted_iota(jnp.int32, (8, 128), 1) % 32 < 16
-    for tile in range(2):
-        sub = 8 * tile
-
-        def load(s, sub=sub):
-            if sub == 0 and s < 8:
-                waits[1 + s].wait()
-            return in_ref[s // 8, s % 8, sub : sub + 8, :], in_ref[s // 8, s % 8, 16 + sub : 24 + sub, :]
-
-        def store(m1, value, sub=sub):
-            real, imag = value
-            tr, ti = twiddle_ref[0, m1 : m1 + 1, :], twiddle_ref[1, m1 : m1 + 1, :]
-            at = m1 * 16 + sub
-            mid_ref[at : at + 8, 0:128] = real * tr - imag * ti
-            mid_ref[at : at + 8, 128:256] = real * ti + imag * tr
-
-        column_transform(load, store, -1, hold_ref.at[0])
-    waits[9].wait()
-    waits[10].wait()
-    forward, inverse = forward_ref[...], inverse_ref[...]
-    for part in range(4):
-        rows = slice(256 * part, 256 * part + 256)
-        spectrum = matmul(spread(mid_ref[rows, :]), forward, ((1,), (0,)))
+    for n0 in range(8):
+        waits[1 + n0].wait()
+        for tile in range(2):
+            pieces = [
+                tuple(in_ref[n1, n0, 16 * c + 8 * tile : 16 * c + 8 * tile + 8, :] for c in range(2))
+                for n1 in range(8)
+            ]
+            for ka, value in enumerate(transform(pieces, -1)):
+                hold_ref[0, tile, 0, 8 * ka + n0], hold_ref[0, tile, 1, 8 * ka + n0] = times(value, n0 * ka, 64, -1)
+
+    def waves(ka):
+        for tile in range(2):
+            pieces = [tuple(hold_ref[0, tile, c, 8 * ka + n0] for c in range(2)) for n0 in range(8)]
+            for kb, (real, imag) in enumerate(transform(pieces, -1)):
+                m1 = ka + 8 * kb
+                tr, ti = twiddle_ref[0, m1 : m1 + 1, :], twiddle_ref[1, m1 : m1 + 1, :]
+                at = 128 * ka + 16 * kb + 8 * tile
+                mid_ref[at : at + 8, 0:128] = real * tr - imag * ti
+                mid_ref[at : at + 8, 128:256] = real * ti + imag * tr
+
+    def turn(pair):
+        rows = slice(256 * pair, 256 * pair + 256)
+        spectrum = matmul(spread(mid_ref[rows, :]), matrix, ((1,), (0,)))
         real, imag = spectrum[:, :128], spectrum[:, 128:]
         for ref in range(2):
             cosine, sine = shift_ref[2 * ref, rows, :], shift_ref[2 * ref + 1, rows, :]
-            turned = jnp.concatenate([real * cosine - imag * sine, real * sine + imag * cosine], axis=1)
-            back_ref[ref, rows, :] = matmul(spread(turned), inverse, ((1,), (0,)))
+            turned = jnp.concatenate([real * sine + imag * cosine, real * cosine - imag * sine], axis=1)
+            back_ref[ref, rows, :] = matmul(spread(turned), matrix, ((1,), (0,)))
+
+    def back(ka):
+        for ref in range(2):
+            for tile in range(2):
+                pieces = []
+                for kb in range(8):
+                    m1 = ka + 8 * kb
+                    at = 128 * ka + 16 * kb + 8 * tile
+                    imag, real = back_ref[ref, at : at + 8, 0:128], back_ref[ref, at : at + 8, 128:256]
+                    tr, ti = twiddle_ref[0, m1 : m1 + 1, :], twiddle_ref[1, m1 : m1 + 1, :]
+                    pieces.append((real * tr + imag * ti, imag * tr - real * ti))
+                for sa, value in enumerate(transform(pieces, 1)):
+                    real, imag = times(value, ka * sa, 64, 1)
+                    last_ref[ref, tile, 0, 8 * sa + ka], last_ref[ref, tile, 1, 8 * sa + ka] = real, imag
+
+    waits[9].wait()
+    matrix = tripled(matrix_ref, 0)
+    waves(0)
+    waves(1)
+    for pair in range(4):
+        turn(pair)
+        for ka in (2 * pair + 2, 2 * pair + 3):
+            if ka < 8:
+                waves(ka)
+        for ka in (2 * pair - 2, 2 * pair - 1):
+            if ka >= 0:
+                back(ka)
+    back(6)
+    back(7)
     leaving = []
-    for tile in range(2):
-        sub = 8 * tile
-        for ref in range(2):
-
-            def load(m1, ref=ref, sub=sub):
-                at = m1 * 16 + sub
-                real, imag = back_ref[ref, at : at + 8, 0:128], back_ref[ref, at : at + 8, 128:256]
-                tr, ti = twiddle_ref[0, m1 : m1 + 1, :], twiddle_ref[1, m1 : m1 + 1, :]
-                return real * tr + imag * ti, imag * tr - real * ti
-
-            if ref == 0:
-
-                def store(s, value, sub=sub):
-                    out_ref[s // 8, s % 8, sub : sub + 8, :] = value[0]
-                    out_ref[s // 8, s % 8, 16 + sub : 24 + sub, :] = value[1]
-
-            else:
-
-                def store(s, value, sub=sub):
-                    chosen = jnp.where(early, refs_ref[0, 2 * s], refs_ref[0, 2 * s + 1]) > 0
-                    for c in range(2):
-                        at = (s // 8, s % 8, slice(16 * c + sub, 16 * c + sub + 8))
-                        out_ref[at] = jnp.where(chosen, value[c], out_ref[at])
-                    if sub == 8 and s >= 56:
-                        copy = pltpu.make_async_copy(
-                            out_ref.at[:, s % 8], out_hbm.at[:, s % 8], sems.at[11 + s % 8]
-                        )
-                        copy.start()
-                        leaving.append(copy)
-
-            column_transform(load, store, 1, hold_ref.at[ref])
+    for sa in range(8):
+        for tile in range(2):
+            both = [
+                transform([tuple(last_ref[ref, tile, c, 8 * sa + n0] for c in range(2)) for n0 in range(8)], 1)
+                for ref in range(2)
+            ]
+            for sb in range(8):
+                s = sa + 8 * sb
+                chosen = jnp.where(early, refs_ref[0, 2 * s], refs_ref[0, 2 * s + 1]) > 0
+                for c in range(2):
+                    at = slice(16 * c + 8 * tile, 16 * c + 8 * tile + 8)
+                    out_ref[sb, sa, at, :] = jnp.where(chosen, both[1][sb][c], both[0][sb][c])
+        copy = pltpu.make_async_copy(out_ref.at[:, sa], out_hbm.at[:, sa], sems.at[10 + sa])
+        copy.start()
+        leaving.append(copy)
     for copy in leaving:
         copy.wait()
 
 
-def inverse_y_kernel(place_ref, in_ref, phase_ref, coupling_ref, matrix_ref, twiddle_ref, out_ref, *rest):
-    first_ref, last_ref, image_refs, mid_ref, image_hold = rest[0], rest[1], rest[2:6], rest[6], rest[7]
-    matrix = matrix_ref[...]
+def inverse_y_kernel(place_ref, in_ref, phase_ref, coupling_ref, matrix_ref, twiddle_ref, part_ref, *rest):
+    first_ref, last_ref, image_refs, mid_ref, image_hold, out_ref = rest[0], rest[1], rest[2:6], *rest[6:]
+    matrix = tripled(matrix_ref, 0)
     for p in range(8):
         block = in_ref[8 * p : 8 * p + 8].reshape(256, 128)
         mid_ref[128 * p : 128 * p + 128, :] = matmul(spread(block.T), matrix, ((1,), (0,)))
@@ -307,7 +301,10 @@
                     if tile == 3:
                         last_ref[row : row + 1, lanes] = value[7:8]
     row = lax.broadcasted_iota(jnp.int32, (8, 2048), 0)
-    for tile, source, receiver in corrected(out_ref, None, None, coupling_ref):
+    for tile, source, receiver in corrected(out_ref, coupling_ref):
+        for field, pair in enumerate((source, receiver)):
+            for c in range(2):
+                part_ref[field, 0, c, 8 * tile : 8 * tile + 8, :] = pair[c]
         image = source[0] * receiver[0] + source[1] * receiver[1]
         if tile == 0:
             image = jnp.where(row == 0, 0.0, image)
@@ -320,25 +317,43 @@
         image_refs[k][...] = image_hold[pl.ds(at, 8), :]
 
 
-def laplace_kernel(index_ref, wave_ref, above_ref, below_ref, coupling_ref, out_ref, edge_ref):
+def edges_kernel(index_ref, above_ref, below_ref, part_ref, coupling_ref, out_hbm, edge_ref, whole_ref, sems):
+    inner = pltpu.make_async_copy(part_ref.at[:, :, :, 8:24, :], out_hbm.at[:, :, :, 8:24, :], sems.at[0])
+    inner.start()
     index = jnp.full((1, 2048), index_ref[0], jnp.int32)
-    above = [jnp.where(index == 0, 0.0, above_ref[row : row + 1, :]) for row in range(4)]
-    below = [jnp.where(index == 63, 0.0, below_ref[row : row + 1, :]) for row in range(4)]
-    for tile, source, receiver in corrected(wave_ref, above, below, coupling_ref):
-        rows = slice(8 * tile, 8 * tile + 8)
-        for field, pair in enumerate((source, receiver)):
-            out_ref[field, 0, 0, rows, :] = pair[0]
-            out_ref[field, 0, 1, rows, :] = pair[1]
-        image = source[0] * receiver[0] + source[1] * receiver[1]
+    whole_ref[:, :, :, 0] = part_ref[:, :, :, 0:8, :]
+    whole_ref[:, :, :, 1] = part_ref[:, :, :, 24:32, :]
+    for side, (halo_ref, row, end) in enumerate(((above_ref, 0, 0), (below_ref, 7, 63))):
+        coupling = coupling_ref[31 * side : 31 * side + 1, :]
+        results = []
+        for field in range(2):
+            real, imag = (
+                jnp.where(index == end, 0.0, halo_ref[2 * field + c : 2 * field + c + 1, :]) for c in range(2)
+            )
+            scaled = coupling if field else -coupling
+            real, imag = (
+                whole_ref[field, 0, 0, side, row : row + 1, :] - scaled * imag,
+                whole_ref[field, 0, 1, side, row : row + 1, :] + scaled * real,
+            )
+            whole_ref[field, 0, 0, side, row : row + 1, :] = real
+            whole_ref[field, 0, 1, side, row : row + 1, :] = imag
+            results.append((real, imag))
+        image = results[0][0] * results[1][0] + results[0][1] * results[1][1]
         for part in range(4):
-            lanes = slice(512 * part, 512 * part + 512)
-            if tile == 0:
-                edge_ref[part : part + 1, :] = image[0:1, lanes]
-            if tile == 3:
-                edge_ref[4 + part : 5 + part, :] = image[7:8, lanes]
-
-
-def corrected(wave_ref, above, below, coupling_ref):
+            edge_ref[4 * side + part : 4 * side + part + 1, :] = image[:, 512 * part : 512 * part + 512]
+    outer = [
+        pltpu.make_async_copy(
+            whole_ref.at[:, :, :, side], out_hbm.at[:, :, :, 24 * side : 24 * side + 8, :], sems.at[1 + side]
+        )
+        for side in range(2)
+    ]
+    for copy in outer:
+        copy.start()
+    for copy in [inner] + outer:
+        copy.wait()
+
+
+def corrected(wave_ref, coupling_ref):
     row = lax.broadcasted_iota(jnp.int32, (8, 2048), 0)
     lane = lax.broadcasted_iota(jnp.int32, (8, 2048), 1)
     for tile in range(4):
@@ -349,22 +364,14 @@
             laplace = []
             for c in range(2):
                 value = wave_ref[field, c, rows, :]
-                index = 2 * field + c
-                if tile > 0:
-                    before = wave_ref[field, c, 8 * tile - 1 : 8 * tile, :]
-                else:
-                    before = 0.0 if above is None else above[index]
-                if tile < 3:
-                    after = wave_ref[field, c, 8 * tile + 8 : 8 * tile + 9, :]
-                else:
-                    after = 0.0 if below is None else below[index]
+                before = wave_ref[field, c, 8 * tile - 1 : 8 * tile, :] if tile > 0 else 0.0
+                after = wave_ref[field, c, 8 * tile + 8 : 8 * tile + 9, :] if tile < 3 else 0.0
                 up = jnp.where(row == 0, before, pltpu.roll(value, 1, 0))
                 down = jnp.where(row == 7, after, pltpu.roll(value, 7, 0))
                 left = jnp.where(lane == 0, 0.0, pltpu.roll(value, 1, 1))
                 right = jnp.where(lane == 2047, 0.0, pltpu.roll(value, 2047, 1))
                 laplace.append(up + down + left + right - 4.0 * value)
-            sign = -1.0 if field == 0 else 1.0
-            scaled = coupling * sign
+            scaled = coupling if field else -coupling
             real = wave_ref[field, 0, rows, :] - scaled * laplace[1]
             imag = wave_ref[field, 1, rows, :] + scaled * laplace[0]
             results.append((real, imag))
@@ -394,7 +401,7 @@
     return jax.ShapeDtypeStruct(shape, jnp.float32)
 
 
-def call(kernel, out_shape, operands, scratch=(), smem=0, far=0, near=(), near_out=False, far_out=False):
+def call(kernel, out_shape, operands, scratch=(), smem=0, far=0, near=(), near_out=False, far_out=False, first_out_far=False):
     hbm = whole(pl.ANY if INTERPRET else pltpu.HBM)
     many = isinstance(out_shape, (tuple, list))
     if not INTERPRET:
@@ -408,6 +415,8 @@
             shapes = out_shape if many else (out_shape,)
             shapes = tuple(pltpu.VMEM(x.shape, x.dtype) for x in shapes)
             out_shape = shapes if many else shapes[0]
+        if first_out_far:
+            out_shape = (pltpu.HBM(out_shape[0].shape, out_shape[0].dtype),) + tuple(out_shape[1:])
         if far_out:
             out_shape = pltpu.HBM(out_shape.shape, out_shape.dtype)
     return pl.pallas_call(
@@ -416,7 +425,11 @@
         in_specs=[whole(pltpu.SMEM)] * smem
         + [whole()] * (len(operands) - smem - far)
         + [hbm] * far,
-        out_specs=[whole()] * len(out_shape) if many else hbm if far_out else whole(),
+        out_specs=(
+            [hbm if first_out_far and i == 0 else whole() for i in range(len(out_shape))]
+            if many
+            else hbm if far_out else whole()
+        ),
         scratch_shapes=list(scratch),
         interpret=INTERPRET,
         compiler_params=pltpu.CompilerParams(vmem_limit_bytes=VMEM_BYTES),
@@ -428,10 +441,10 @@
     return call(
         forward_y_kernel,
         f32(64, 32, 128),
-        (wavefields, jnp.asarray(const["y_forward"]), jnp.asarray(const["y_twiddle"])),
+        (wavefields, jnp.asarray(const["y_matrix"]), jnp.asarray(const["y_twiddle"])),
         (
             pltpu.VMEM((2, 1, 2, 32, 2048), jnp.float32),
-            pltpu.VMEM((256, 768), BF16),
+            pltpu.VMEM((2, 256, 256), BF16),
             pltpu.VMEM((2, 16, 128), jnp.float32),
             pltpu.VMEM((1024, 256), jnp.float32),
             pltpu.SemaphoreType.DMA((10,)),
@@ -450,23 +463,22 @@
             ref_index,
             shift,
             blocks.reshape(8, 8, 32, 128),
-            jnp.asarray(const["x_forward"]),
-            jnp.asarray(const["x_inverse"]),
+            jnp.asarray(const["x_matrix"]),
             jnp.asarray(const["x_twiddle"]),
         ),
         (
             pltpu.VMEM((8, 8, 32, 128), jnp.float32),
             pltpu.VMEM((8, 8, 32, 128), jnp.float32),
-            pltpu.VMEM((768, 256), BF16),
-            pltpu.VMEM((768, 256), BF16),
+            pltpu.VMEM((2, 256, 256), BF16),
             pltpu.VMEM((2, 64, 128), jnp.float32),
             pltpu.VMEM((1024, 256), jnp.float32),
             pltpu.VMEM((2, 1024, 256), jnp.float32),
-            pltpu.VMEM((2, 2, 64, 8, 128), jnp.float32),
-            pltpu.SemaphoreType.DMA((19,)),
+            pltpu.VMEM((1, 2, 2, 64, 8, 128), jnp.float32),
+            pltpu.VMEM((2, 2, 2, 64, 8, 128), jnp.float32),
+            pltpu.SemaphoreType.DMA((18,)),
         ),
         smem=1,
-        far=4,
+        far=3,
         near=(1,),
         far_out=True,
     )
@@ -477,22 +489,28 @@
     const = constants()
     return call(
         inverse_y_kernel,
-        (f32(2, 2, 32, 2048),) + (f32(4, 2048),) * 2 + (f32(8, 2048),) * 4,
-        (place, blocks, phase, coupling, jnp.asarray(const["y_inverse"]), jnp.asarray(const["y_twiddle"])),
-        (pltpu.VMEM((1024, 256), jnp.float32), pltpu.VMEM((32, 2048), jnp.float32)),
+        (f32(2, 1, 2, 32, 2048),) + (f32(4, 2048),) * 2 + (f32(8, 2048),) * 4,
+        (place, blocks, phase, coupling, jnp.asarray(const["y_matrix"]), jnp.asarray(const["y_twiddle"])),
+        (
+            pltpu.VMEM((1024, 256), jnp.float32),
+            pltpu.VMEM((32, 2048), jnp.float32),
+            pltpu.VMEM((2, 2, 32, 2048), jnp.float32),
+        ),
         smem=1,
         near=(1, 2, 3),
         near_out=True,
     )
 
 
-def laplace(index, wave, above, below, coupling):
+def add_edges(index, above, below, part, coupling):
     return call(
-        laplace_kernel,
+        edges_kernel,
         (f32(2, 1, 2, 32, 2048), f32(8, 512)),
-        (index, wave, above, below, coupling),
+        (index, above, below, part, coupling),
+        (pltpu.VMEM((2, 1, 2, 2, 8, 2048), jnp.float32), pltpu.SemaphoreType.DMA((3,))),
         smem=1,
         near=(1, 2, 3, 4),
+        first_out_far=True,
     )
 
 
@@ -508,7 +526,7 @@
 def shift_tables(space_index, omega, ref_velocity):
     row = lax.broadcasted_iota(jnp.int32, (1024, 128), 0)
     lane = lax.broadcasted_iota(jnp.int32, (1024, 128), 1)
-    kx = wave_values(row // 16 + 64 * (lane % 32), NX)
+    kx = wave_values(row // 128 + 8 * (row // 16 % 8) + 64 * (lane % 32), NX)
     k1 = 2 * (space_index // 8) + lane // 64
     k2 = 16 * (space_index % 8) + row % 16
     ky = wave_values(k1 + 16 * k2, NY)
@@ -521,12 +539,12 @@
         travels = vertical >= 0.0
         tables.append(jnp.where(travels, jnp.cos(root), jnp.exp(-root)))
         tables.append(jnp.where(travels, sign * jnp.sin(root), 0.0))
-    return jnp.stack(tables)
+    return jnp.stack(tables) * (1.0 / NX)
 
 
 def phase_tables(speed, ref_rows, omega):
     time_shift = omega * DZ * (1.0 / speed - 1.0 / ref_rows)
-    return jnp.stack([jnp.cos(time_shift), jnp.sin(time_shift)])
+    return jnp.stack([jnp.cos(time_shift), jnp.sin(time_shift)]) * (1.0 / NY)
 
 
 def coupling_table(speed, ref_rows, omega):
@@ -575,7 +593,7 @@
     coupling = coupling_table(speed, ref_rows, omega)
     blocks = middle(blocks, shift, ref_index)
     blocks = exchange(blocks)
-    wave, first, last, *quarters = inverse_y(place, blocks, phase, coupling)
+    part, first, last, *quarters = inverse_y(place, blocks, phase, coupling)
     above = lax.ppermute(last, "space", shifted_pairs(1, 64))
     below = lax.ppermute(first, "space", shifted_pairs(63, 64))
     total = quarters[0]
@@ -583,7 +601,7 @@
         arrived = lax.ppermute(quarters[step], "freq", shifted_pairs(step))
         total = total + arrived
     index = space_index.reshape(1).astype(jnp.int32)
-    fields, edges = laplace(index, wave, above, below, coupling)
+    fields, edges = add_edges(index, above, below, part, coupling)
     image = assemble(place, gathered(jnp.concatenate([total, edges], axis=1)))
     return fields, image
 

time: 120 us -> 121 us (level)
  other arithmetic: 7.17 us -> 14.2 us
  waiting for transfers between devices: 32.7 us -> 26 us
  starting transfers between devices: 60 us -> 61.3 us
    all_to_all x2, waiting for transfers between devices: 10.6 us -> 2.73 us  [exchange(): lax.all_to_all(blocks, 'space', split_axis=0, concat_axis=0, tiled=True)]
    select_n x0 -> x2, other arithmetic: none -> 6.3 us  [shift_tables(): tables.append(jnp.where(travels, sign * jnp.sin(root), 0.0))]
    all_to_all x2, starting transfers between devices: 21 us -> 25.4 us  [exchange(): lax.all_to_all(blocks, 'space', split_axis=0, concat_axis=0, tiled=True)]
    ppermute x6, starting transfers between devices: 20.2 us -> 17 us  [gathered(): pieces.append(lax.ppermute(mine, 'freq', shifted_pairs(step)))]
    select_n x1, other arithmetic: 4.72 us -> 6.21 us  [shift_tables(): tables.append(jnp.where(travels, jnp.cos(root), jnp.exp(-root)))]
    ppermute x6, waiting for transfers between devices: 20.1 us -> 21.3 us  [gathered(): pieces.append(lax.ppermute(mine, 'freq', shifted_pairs(step)))]
  transfers between devices with their start and end apart: 16 -> 16, of which waited for: 8 -> 8; matrix products, arithmetic and copies ran while one was open for 8% -> 14% of each run, Pallas kernels for 7% -> 6%
where the time goes in v4:
time: 121 us; the launch traced here: 119 us
  starting transfers between devices  61.3 us (51%)
  waiting for transfers between devices  26 us (21%)
  other arithmetic  14.2 us (12%)
  Pallas kernels  12.2 us (10%)
  between operations  3.64 us (3%)
  local copies, waits for them, and re-layouts  2.15 us (2%)
    all_to_all x2, starting transfers between devices, exchange(): lax.all_to_all(blocks, 'space', split_axis=0, concat_axis=0, tiled=True)  25.4 us
    ppermute x6, waiting for transfers between devices, gathered(): pieces.append(lax.ppermute(mine, 'freq', shifted_pairs(step)))  21.3 us
    ppermute x6, starting transfers between devices, gathered(): pieces.append(lax.ppermute(mine, 'freq', shifted_pairs(step)))  17 us
    pallas_call x6, Pallas kernels, call(): pl.pallas_call(kernel, out_shape=out_shape, in_specs=[whole(pltpu.SMEM)]...  12.2 us
    ppermute x1, starting transfers between devices, step_down(): below = lax.ppermute(first, 'space', shifted_pairs(63, 64))  8.66 us
    ppermute x3, starting transfers between devices, step_down(): arrived = lax.ppermute(quarters[step], 'freq', shifted_pairs(step))  6.81 us
    select_n x2, other arithmetic, shift_tables(): tables.append(jnp.where(travels, sign * jnp.sin(root), 0.0))  6.3 us
    select_n x1, other arithmetic, shift_tables(): tables.append(jnp.where(travels, jnp.cos(root), jnp.exp(-root)))  6.21 us
  transfers between devices with their start and end apart: 16, of which 8 were waited for; matrix products, arithmetic and copies ran while one was open for 14% of the time, Pallas kernels for 6%

profile of v4, /device:TPU:2, one launch (start us, length us, event | category | flops | bytes accessed | tf_op | source)
XLA Modules:
  0.0 119.5 jit_solution(17666944927948979732)
XLA Ops:
  0.6 0.0 copy-start
  0.6 3.1 %shard_map.113 = f32[64,32,128]{2,1,0:T(8,128)} custom-call(f32[2,1,2,32,2048]{4,3,2,1,0:T(8,128)} %wave_hbm.1, bf16[2,256,256]{2,1,0:T(8,128)(2,1)} %constant.234.clone.matrix_hbm.matrix_ref, f32[2,16,128]{2,1,0:T(8,128)} %constant.235.clone.twiddle_hbm.twiddle_ref), custom_call_target="tpu_custom_call" | custom-call | tf_op jit(solution)/shard_map/pallas_call | solution.py:422
  3.8 0.0 copy-start.4
  3.8 14.8 %all-to-all-start = ((f32[64,32,128]{2,1,0:T(8,128)}), f32[64,32,128]{2,1,0:T(8,128)}, u32[]{:S(2)}, u32[]{:S(2)}) async-start(f32[64,32,128]{2,1,0:T(8,128)} %shard_map.113), calls=%async_computation | async-start | bytes 2097152 | tf_op jit(solution)/shard_map/all_to_all | solution.py:577
  19.4 0.0 copy-done
  19.4 0.7 dynamic-slice_bitcast_fusion.1
  20.1 1.9 %collective-permute-start = (f32[8,2048]{1,0:T(8,128)}, f32[8,2048]{1,0:T(8,128)S(1)}, u32[]{:S(2)}, u32[]{:S(2)}) collective-permute-start(f32[8,2048]{1,0:T(8,128)} %get-tuple-element.24), channel_id=1, source_target_pairs={{0,192},{64,0},{128,64},{192,128},{1,193},{65,1},{129,65},{193,129... | collective-permute-start | bytes 196616 | tf_op jit(solution)/shard_map/ppermute | solution.py:564
  22.0 0.6 collective-permute-start.1
  22.6 1.0 collective-permute-start.2
  24.3 0.0 copy-done.4
  24.3 0.6 fusion.31
  26.4 6.2 %exponential_select_fusion.1 = (f32[1,1024,128]{2,1,0:T(8,128)S(1)}, f32[1,1024,128]{2,1,0:T(8,128)S(1)}) fusion(f32[]{:T(128)S(6)} %integer_pow.50, s32[1024]{0:T(1024)S(1)} %get-tuple-element.34, s32[1024]{0:T(1024)S(1)} %get-tuple-element.36, pred[1024]{0:T(1024)(128)(4,1)S(1)} %get-tuple-element.37, s32[]{:T(128)S(6)} %mul.214, ...), kind=kLoop, calls=%fused_computation.34 | loop fusion | flops 6422528 | bytes 1078544 | tf_op jit(solution)/shard_map/jit(_where)/select_n | solution.py:540
  32.6 3.0 %fusion.1 = f32[1,1024,128]{2,1,0:T(8,128)S(1)} fusion(f32[]{:T(128)S(6)} %integer_pow.53, s32[128]{0:T(128)S(1)} %get-tuple-element.42, s32[128]{0:T(128)S(1)} %get-tuple-element.44, pred[128]{0:T(512)(128)(4,1)S(1)} %compare_and_fusion.2, s32[1024]{0:T(1024)S(1)} %get-tuple-element.34, s32[1024]{0:T(1024)S(1)} %get-tuple-element.36, ...), kind=kLoop, calls=%fused_computation.17 | loop fusion | flops 7471104 | bytes 555404 | tf_op jit(solution)/shard_map/jit(_where)/select_n | solution.py:541
  35.6 3.3 %fusion = f32[1,1024,128]{2,1,0:T(8,128)S(1)} fusion(f32[]{:T(128)S(6)} %integer_pow.50, s32[128]{0:T(128)S(1)} %get-tuple-element.42, s32[128]{0:T(128)S(1)} %get-tuple-element.44, pred[128]{0:T(512)(128)(4,1)S(1)} %compare_and_fusion.2, s32[1024]{0:T(1024)S(1)} %get-tuple-element.34, s32[1024]{0:T(1024)S(1)} %get-tuple-element.36, ...), kind=kLoop, calls=%fused_computation.16 | loop fusion | flops 7471104 | bytes 555404 | tf_op jit(solution)/shard_map/jit(_where)/select_n | solution.py:541
  38.9 0.0 copy-start.3
  38.9 0.1 maximum_multiply_fusion.shift_ref
  39.0 2.7 %all-to-all-done = f32[64,32,128]{2,1,0:T(8,128)} async-done(((f32[64,32,128]{2,1,0:T(8,128)}), f32[64,32,128]{2,1,0:T(8,128)}, u32[]{:S(2)}, u32[]{:S(2)}) %all-to-all-start) | async-done | bytes 1048608 | tf_op jit(solution)/shard_map/all_to_all | solution.py:577
  41.8 0.0 copy-done.3
  41.8 5.8 %shard_map.114 = f32[8,8,32,128]{3,2,1,0:T(8,128)} custom-call(s32[1,128]{1,0:T(1,128)S(1)} %copy-done.3, f32[4,1024,128]{2,1,0:T(8,128)S(1)} %maximum_multiply_fusion.shift_ref, f32[8,8,32,128]{3,2,1,0:T(8,128)} %bitcast.5.in_hbm, bf16[2,256,256]{2,1,0:T(8,128)(2,1)} %constant.236.clone.matrix_hbm, f32[2,64,128]{2,1,0:T(8,128)} %constant.237.clone.twiddle_hbm), custom_call_target="tpu_custom_call" | custom-call | tf_op jit(solution)/shard_map/pallas_call | solution.py:422
  47.6 10.5 %all-to-all-start.1 = ((f32[64,32,128]{2,1,0:T(8,128)}), f32[64,32,128]{2,1,0:T(8,128)S(1)}, u32[]{:S(2)}, u32[]{:S(2)}) async-start(f32[64,32,128]{2,1,0:T(8,128)} %bitcast.46), calls=%async_computation.1 | async-start | bytes 2097152 | tf_op jit(solution)/shard_map/all_to_all | solution.py:577
  58.1 0.0 copy-start.1
  58.1 0.0 copy-start.2
  58.1 0.1 fusion.30
  58.2 0.6 gather_fusion
  58.9 0.1 broadcast_in_dim.17
  58.9 0.1 broadcast_in_dim_reshape.3
  59.0 0.0 collective-permute-done
  59.0 0.0 collective-permute-done.1
  59.0 0.0 collective-permute-done.2
  59.1 7.1 %collective-permute-start.3 = (f32[8,2048]{1,0:T(8,128)S(1)}, f32[8,2048]{1,0:T(8,128)S(1)}, u32[]{:S(2)}, u32[]{:S(2)}) collective-permute-start(f32[8,2048]{1,0:T(8,128)S(1)} %fusion.18.own_ref), channel_id=1, source_target_pairs={{0,64},{64,128},{128,192},{192,0},{1,65},{65,129},{129,193},{193,1... | collective-permute-start | bytes 196616 | tf_op jit(solution)/shard_map/ppermute | solution.py:572
  66.2 2.3 %collective-permute-start.4 = (f32[8,2048]{1,0:T(8,128)S(1)}, f32[8,2048]{1,0:T(8,128)S(1)}, u32[]{:S(2)}, u32[]{:S(2)}) collective-permute-start(f32[8,2048]{1,0:T(8,128)S(1)} %fusion.18.own_ref), channel_id=1, source_target_pairs={{0,128},{64,192},{128,0},{192,64},{1,129},{65,193},{129,1},{193,65... | collective-permute-start | bytes 196616 | tf_op jit(solution)/shard_map/ppermute | solution.py:572
  68.5 2.8 %collective-permute-start.5 = (f32[8,2048]{1,0:T(8,128)S(1)}, f32[8,2048]{1,0:T(8,128)S(1)}, u32[]{:S(2)}, u32[]{:S(2)}) collective-permute-start(f32[8,2048]{1,0:T(8,128)S(1)} %fusion.18.own_ref), channel_id=1, source_target_pairs={{0,192},{64,0},{128,64},{192,128},{1,193},{65,1},{129,65},{193,129... | collective-permute-start | bytes 196616 | tf_op jit(solution)/shard_map/ppermute | solution.py:572
  71.4 3.8 %collective-permute-done.3.rest_0_ = f32[8,2048]{1,0:T(8,128)S(1)} collective-permute-done((f32[8,2048]{1,0:T(8,128)S(1)}, f32[8,2048]{1,0:T(8,128)S(1)}, u32[]{:S(2)}, u32[]{:S(2)}) %collective-permute-start.3) | collective-permute-done | bytes 65568 | tf_op jit(solution)/shard_map/ppermute | solution.py:572
  75.2 2.3 %collective-permute-done.4.rest_1_ = f32[8,2048]{1,0:T(8,128)S(1)} collective-permute-done((f32[8,2048]{1,0:T(8,128)S(1)}, f32[8,2048]{1,0:T(8,128)S(1)}, u32[]{:S(2)}, u32[]{:S(2)}) %collective-permute-start.4) | collective-permute-done | bytes 65568 | tf_op jit(solution)/shard_map/ppermute | solution.py:572
  77.4 11.0 %collective-permute-done.5.rest_2_ = f32[8,2048]{1,0:T(8,128)S(1)} collective-permute-done((f32[8,2048]{1,0:T(8,128)S(1)}, f32[8,2048]{1,0:T(8,128)S(1)}, u32[]{:S(2)}, u32[]{:S(2)}) %collective-permute-start.5) | collective-permute-done | bytes 65568 | tf_op jit(solution)/shard_map/ppermute | solution.py:572
  88.4 1.1 fusion.20
  89.6 0.1 maximum_multiply_fusion.1.phase_ref
  89.6 0.1 fusion.16.coupling_ref
  89.7 0.0 all-to-all-done.1.in_ref
  89.7 0.0 copy-done.1
  89.7 0.0 copy-done.2
  89.8 1.5 %shard_map.116 = (f32[2,1,2,32,2048]{4,3,2,1,0:T(8,128)S(1)}, f32[4,2048]{1,0:T(4,128)S(1)}, f32[4,2048]{1,0:T(4,128)S(1)}, f32[8,2048]{1,0:T(8,128)S(1)}, f32[8...) custom-call(s32[1]{0:T(128)} %bitcast.1.place_ref, f32[64,32,128]{2,1,0:T(8,128)S(1)} %all-to-all-done.1.in_ref, ...), custom_call_target="tpu_custom_call" | custom-call | tf_op jit(solution)/shard_map/pallas_call | solution.py:422
  91.3 2.6 %collective-permute-start.10 = (f32[8,2048]{1,0:T(8,128)S(1)}, f32[8,2048]{1,0:T(8,128)S(1)}, u32[]{:S(2)}, u32[]{:S(2)}) collective-permute-start(f32[8,2048]{1,0:T(8,128)S(1)} %get-tuple-element.18), channel_id=1, source_target_pairs={{0,192},{64,0},{128,64},{192,128},{1,193},{65,1},{129,65},{193,129... | collective-permute-start | bytes 196616 | tf_op jit(solution)/shard_map/ppermute | solution.py:601
  93.9 4.2 %collective-permute-start.9 = (f32[8,2048]{1,0:T(8,128)S(1)}, f32[8,2048]{1,0:T(8,128)S(1)}, u32[]{:S(2)}, u32[]{:S(2)}) collective-permute-start(f32[8,2048]{1,0:T(8,128)S(1)} %get-tuple-element.17), channel_id=1, source_target_pairs={{0,128},{64,192},{128,0},{192,64},{1,129},{65,193},{129,1},{193,65... | collective-permute-start | bytes 196616 | tf_op jit(solution)/shard_map/ppermute | solution.py:601
  98.1 0.0 collective-permute-start.8
  98.1 0.0 collective-permute-start.6
  98.1 8.7 %collective-permute-start.7 = (f32[4,2048]{1,0:T(4,128)S(1)}, f32[4,2048]{1,0:T(4,128)S(1)}, u32[]{:S(2)}, u32[]{:S(2)}) collective-permute-start(f32[4,2048]{1,0:T(4,128)S(1)} %get-tuple-element.12), channel_id=1, source_target_pairs={{0,63},{1,0},{2,1},{3,2},{4,3},{5,4},{6,5},{7,6},{8,7},{9,8},{10,9... | collective-permute-start | bytes 98312 | tf_op jit(solution)/shard_map/ppermute | solution.py:598
  106.8 1.9 %collective-permute-done.6.above_ref = f32[4,2048]{1,0:T(4,128)S(1)} collective-permute-done((f32[4,2048]{1,0:T(4,128)S(1)}, f32[4,2048]{1,0:T(4,128)S(1)}, u32[]{:S(2)}, u32[]{:S(2)}) %collective-permute-start.6) | collective-permute-done | bytes 32800 | tf_op jit(solution)/shard_map/ppermute | solution.py:597
  108.7 0.0 collective-permute-done.7.below_ref
  108.7 1.0 shard_map.117
  109.7 0.0 collective-permute-done.10
  109.7 0.0 collective-permute-done.9
  109.7 0.0 collective-permute-done.8
  109.8 0.6 collective-permute-start.11
  110.4 3.6 %collective-permute-start.12 = (f32[8,2560]{1,0:T(8,128)S(1)}, f32[8,2560]{1,0:T(8,128)S(1)}, u32[]{:S(2)}, u32[]{:S(2)}) collective-permute-start(f32[8,2560]{1,0:T(8,128)S(1)} %pad_maximum_fusion.own_ref), channel_id=1, source_target_pairs={{0,128},{64,192},{128,0},{192,64},{1,129},{65,193},{129,1},{193,65... | collective-permute-start | bytes 245768 | tf_op jit(solution)/shard_map/ppermute | solution.py:572
  113.9 0.6 collective-permute-start.13
  114.5 1.7 %collective-permute-done.11.rest_0_ = f32[8,2560]{1,0:T(8,128)S(1)} collective-permute-done((f32[8,2560]{1,0:T(8,128)S(1)}, f32[8,2560]{1,0:T(8,128)S(1)}, u32[]{:S(2)}, u32[]{:S(2)}) %collective-permute-start.11) | collective-permute-done | bytes 81952 | tf_op jit(solution)/shard_map/ppermute | solution.py:572
  116.2 1.7 %collective-permute-done.12.rest_1_ = f32[8,2560]{1,0:T(8,128)S(1)} collective-permute-done((f32[8,2560]{1,0:T(8,128)S(1)}, f32[8,2560]{1,0:T(8,128)S(1)}, u32[]{:S(2)}, u32[]{:S(2)}) %collective-permute-start.12) | collective-permute-done | bytes 81952 | tf_op jit(solution)/shard_map/ppermute | solution.py:572
  117.9 0.8 collective-permute-done.13.rest_2_
  118.8 0.7 shard_map.118
  (17 shorter events, 0.2 us)
Async XLA Ops:
  0.6 18.7 %copy-start = (f32[4,32,2048]{2,1,0:T(8,128)S(1)}, f32[4,32,2048]{2,1,0:T(8,128)}, u32[]{:S(2)}) copy-start(f32[4,32,2048]{2,1,0:T(8,128)} %param.12) | copy-start | bytes 3145732
  3.8 20.5 %copy-start.4 = (f32[1,2]{1,0:T(1,128)S(1)}, f32[1,2]{1,0:T(1,128)}, u32[]{:S(2)}) copy-start(f32[1,2]{1,0:T(1,128)} %param.14) | copy-start | bytes 28
  3.8 38.0 %all-to-all-start = ((f32[64,32,128]{2,1,0:T(8,128)}), f32[64,32,128]{2,1,0:T(8,128)}, u32[]{:S(2)}, u32[]{:S(2)}) async-start(f32[64,32,128]{2,1,0:T(8,128)} %shard_map.113), calls=%async_computation | async-start | bytes 2097152 | tf_op jit(solution)/shard_map/all_to_all | solution.py:577
  20.1 38.9 %collective-permute-start = (f32[8,2048]{1,0:T(8,128)}, f32[8,2048]{1,0:T(8,128)S(1)}, u32[]{:S(2)}, u32[]{:S(2)}) collective-permute-start(f32[8,2048]{1,0:T(8,128)} %get-tuple-element.24), channel_id=1, source_target_pairs={{0,192},{64,0},{128,64},{192,128},{1,193},{65,1},{129,65},{193,129... | collective-permute-start | bytes 196616 | tf_op jit(solution)/shard_map/ppermute | solution.py:564
  22.0 37.0 %collective-permute-start.1 = (f32[8,2048]{1,0:T(8,128)}, f32[8,2048]{1,0:T(8,128)}, u32[]{:S(2)}, u32[]{:S(2)}) collective-permute-start(f32[8,2048]{1,0:T(8,128)} %get-tuple-element.23), channel_id=1, source_target_pairs={{0,128},{64,192},{128,0},{192,64},{1,129},{65,193},{129,1},{193,65... | collective-permute-start | bytes 196616 | tf_op jit(solution)/shard_map/ppermute | solution.py:564
  22.6 36.4 %collective-permute-start.2 = (f32[8,2048]{1,0:T(8,128)}, f32[8,2048]{1,0:T(8,128)}, u32[]{:S(2)}, u32[]{:S(2)}) collective-permute-start(f32[8,2048]{1,0:T(8,128)} %get-tuple-element.22), channel_id=1, source_target_pairs={{0,64},{64,128},{128,192},{192,0},{1,65},{65,129},{129,193},{193,1... | collective-permute-start | bytes 196616 | tf_op jit(solution)/shard_map/ppermute | solution.py:564
  38.9 2.9 %copy-start.3 = (s32[1,128]{1,0:T(1,128)S(1)}, s32[1,128]{1,0:T(1,128)}, u32[]{:S(2)}) copy-start(s32[1,128]{1,0:T(1,128)} %refs_ref.1) | copy-start | bytes 1540
  47.6 42.2 %all-to-all-start.1 = ((f32[64,32,128]{2,1,0:T(8,128)}), f32[64,32,128]{2,1,0:T(8,128)S(1)}, u32[]{:S(2)}, u32[]{:S(2)}) async-start(f32[64,32,128]{2,1,0:T(8,128)} %bitcast.46), calls=%async_computation.1 | async-start | bytes 2097152 | tf_op jit(solution)/shard_map/all_to_all | solution.py:577
  58.1 31.6 %copy-start.1 = (bf16[2,256,256]{2,1,0:T(8,128)(2,1)S(1)}, bf16[2,256,256]{2,1,0:T(8,128)(2,1)}, u32[]{:S(2)}) copy-start(bf16[2,256,256]{2,1,0:T(8,128)(2,1)} %constant.234.clone.matrix_hbm.matrix_ref) | copy-start | bytes 786436
  58.1 31.6 %copy-start.2 = (f32[2,16,128]{2,1,0:T(8,128)S(1)}, f32[2,16,128]{2,1,0:T(8,128)}, u32[]{:S(2)}) copy-start(f32[2,16,128]{2,1,0:T(8,128)} %constant.235.clone.twiddle_hbm.twiddle_ref) | copy-start | bytes 49156
  59.1 16.1 %collective-permute-start.3 = (f32[8,2048]{1,0:T(8,128)S(1)}, f32[8,2048]{1,0:T(8,128)S(1)}, u32[]{:S(2)}, u32[]{:S(2)}) collective-permute-start(f32[8,2048]{1,0:T(8,128)S(1)} %fusion.18.own_ref), channel_id=1, source_target_pairs={{0,64},{64,128},{128,192},{192,0},{1,65},{65,129},{129,193},{193,1... | collective-permute-start | bytes 196616 | tf_op jit(solution)/shard_map/ppermute | solution.py:572
  66.2 11.2 %collective-permute-start.4 = (f32[8,2048]{1,0:T(8,128)S(1)}, f32[8,2048]{1,0:T(8,128)S(1)}, u32[]{:S(2)}, u32[]{:S(2)}) collective-permute-start(f32[8,2048]{1,0:T(8,128)S(1)} %fusion.18.own_ref), channel_id=1, source_target_pairs={{0,128},{64,192},{128,0},{192,64},{1,129},{65,193},{129,1},{193,65... | collective-permute-start | bytes 196616 | tf_op jit(solution)/shard_map/ppermute | solution.py:572
  68.5 19.9 %collective-permute-start.5 = (f32[8,2048]{1,0:T(8,128)S(1)}, f32[8,2048]{1,0:T(8,128)S(1)}, u32[]{:S(2)}, u32[]{:S(2)}) collective-permute-start(f32[8,2048]{1,0:T(8,128)S(1)} %fusion.18.own_ref), channel_id=1, source_target_pairs={{0,192},{64,0},{128,64},{192,128},{1,193},{65,1},{129,65},{193,129... | collective-permute-start | bytes 196616 | tf_op jit(solution)/shard_map/ppermute | solution.py:572
  91.3 18.4 %collective-permute-start.10 = (f32[8,2048]{1,0:T(8,128)S(1)}, f32[8,2048]{1,0:T(8,128)S(1)}, u32[]{:S(2)}, u32[]{:S(2)}) collective-permute-start(f32[8,2048]{1,0:T(8,128)S(1)} %get-tuple-element.18), channel_id=1, source_target_pairs={{0,192},{64,0},{128,64},{192,128},{1,193},{65,1},{129,65},{193,129... | collective-permute-start | bytes 196616 | tf_op jit(solution)/shard_map/ppermute | solution.py:601
  93.9 15.9 %collective-permute-start.9 = (f32[8,2048]{1,0:T(8,128)S(1)}, f32[8,2048]{1,0:T(8,128)S(1)}, u32[]{:S(2)}, u32[]{:S(2)}) collective-permute-start(f32[8,2048]{1,0:T(8,128)S(1)} %get-tuple-element.17), channel_id=1, source_target_pairs={{0,128},{64,192},{128,0},{192,64},{1,129},{65,193},{129,1},{193,65... | collective-permute-start | bytes 196616 | tf_op jit(solution)/shard_map/ppermute | solution.py:601
  98.1 11.6 %collective-permute-start.8 = (f32[8,2048]{1,0:T(8,128)S(1)}, f32[8,2048]{1,0:T(8,128)S(1)}, u32[]{:S(2)}, u32[]{:S(2)}) collective-permute-start(f32[8,2048]{1,0:T(8,128)S(1)} %get-tuple-element.16), channel_id=1, source_target_pairs={{0,64},{64,128},{128,192},{192,0},{1,65},{65,129},{129,193},{193,1... | collective-permute-start | bytes 196616 | tf_op jit(solution)/shard_map/ppermute | solution.py:601
  98.1 10.6 %collective-permute-start.6 = (f32[4,2048]{1,0:T(4,128)S(1)}, f32[4,2048]{1,0:T(4,128)S(1)}, u32[]{:S(2)}, u32[]{:S(2)}) collective-permute-start(f32[4,2048]{1,0:T(4,128)S(1)} %get-tuple-element.11), channel_id=1, source_target_pairs={{0,1},{1,2},{2,3},{3,4},{4,5},{5,6},{6,7},{7,8},{8,9},{9,10},{10,1... | collective-permute-start | bytes 98312 | tf_op jit(solution)/shard_map/ppermute | solution.py:597
  98.1 10.6 %collective-permute-start.7 = (f32[4,2048]{1,0:T(4,128)S(1)}, f32[4,2048]{1,0:T(4,128)S(1)}, u32[]{:S(2)}, u32[]{:S(2)}) collective-permute-start(f32[4,2048]{1,0:T(4,128)S(1)} %get-tuple-element.12), channel_id=1, source_target_pairs={{0,63},{1,0},{2,1},{3,2},{4,3},{5,4},{6,5},{7,6},{8,7},{9,8},{10,9... | collective-permute-start | bytes 98312 | tf_op jit(solution)/shard_map/ppermute | solution.py:598
  109.8 6.4 %collective-permute-start.11 = (f32[8,2560]{1,0:T(8,128)S(1)}, f32[8,2560]{1,0:T(8,128)S(1)}, u32[]{:S(2)}, u32[]{:S(2)}) collective-permute-start(f32[8,2560]{1,0:T(8,128)S(1)} %pad_maximum_fusion.own_ref), channel_id=1, source_target_pairs={{0,64},{64,128},{128,192},{192,0},{1,65},{65,129},{129,193},{193,1... | collective-permute-start | bytes 245768 | tf_op jit(solution)/shard_map/ppermute | solution.py:572
  110.4 7.6 %collective-permute-start.12 = (f32[8,2560]{1,0:T(8,128)S(1)}, f32[8,2560]{1,0:T(8,128)S(1)}, u32[]{:S(2)}, u32[]{:S(2)}) collective-permute-start(f32[8,2560]{1,0:T(8,128)S(1)} %pad_maximum_fusion.own_ref), channel_id=1, source_target_pairs={{0,128},{64,192},{128,0},{192,64},{1,129},{65,193},{129,1},{193,65... | collective-permute-start | bytes 245768 | tf_op jit(solution)/shard_map/ppermute | solution.py:572
  113.9 4.8 %collective-permute-start.13 = (f32[8,2560]{1,0:T(8,128)S(1)}, f32[8,2560]{1,0:T(8,128)S(1)}, u32[]{:S(2)}, u32[]{:S(2)}) collective-permute-start(f32[8,2560]{1,0:T(8,128)S(1)} %pad_maximum_fusion.own_ref), channel_id=1, source_target_pairs={{0,192},{64,0},{128,64},{192,128},{1,193},{65,1},{129,65},{193,129... | collective-permute-start | bytes 245768 | tf_op jit(solution)/shard_map/ppermute | solution.py:572
